TPU v7x, 256 devices: a whole 4x4x8 slice. The times are simulated.
256 devices in a mesh: section: 4 (over x), dp: 64 (over y, z, core).
Axes of the slice: x: 4, y: 4, z: 8, core: 2. Of those that a mesh axis runs over, the one named last changes fastest.
Arguments:
- clean_latent: bfloat16 [8192, 1536], P('dp'), may hold values from -60 to 60
- noise_latent: bfloat16 [8192, 1536], P('dp'), may hold values from -6 to 6
- teacher_velocity: bfloat16 [8192, 1536], P('dp'), may hold values from -6 to 6
- step_index: int32 [8192], P('dp'), may hold values from 0 to 3
- modulation: float32 [4, 4, 1536], P('section'), may hold values from -0.6 to 0.6
- up_weight: bfloat16 [4, 36864, 128], P('section', 'dp'), may hold values from -0.21875 to 0.21875
- up_rows: int32 [4, 48, 6], P('section'), may hold values from 0 to 11, as said below
- down_weight: bfloat16 [4, 36864, 128], P('section'), may hold values from -0.109375 to 0.109375
- down_rows: int32 [4, 12, 24], P('section'), may hold values from 0 to 47, as said below
Outputs:
- grad_down: float32 [4, 36864, 128], P('section', 'dp')
Inputs may be any that keep to these rules, and one draw needn't show every extreme that they name: For every section s and hidden block c, up_rows[s, c] holds 6 different feature blocks. For every section s and feature block e, down_rows[s, e] holds 24 different hidden blocks.
All inputs are finite; a program needn't handle non-finite values.
Results may differ from a plain program's by a relative error of at most 0.004.
Values may be sent and summed in bfloat16 or wider, within the bound.
No kernel may reach another device: no remote copies, remote signals or barrier semaphores. Data moves between devices by JAX's collectives and lax.ppermute only.
A program may use at most 128 MiB of HBM per device.

v0:
```python
import math

import jax
import jax.numpy as jnp
from jax import lax
from jax.sharding import PartitionSpec as P

MICRO = 2


EPSILON = 1e-06


def from_behind(block, axis, distance):
    devices = range(lax.axis_size(axis))
    route = [(i - distance, i) for i in devices if i - distance in devices]
    return lax.ppermute(block, axis, route)


def activation(values):
    return jax.nn.gelu(values, approximate=True)


def lookup(step_values, table):
    onehot = (step_values[:, None] == jnp.arange(table.shape[0], dtype=jnp.int32)[None, :]).astype(
        jnp.float32
    )
    return jnp.sum(onehot[:, :, None] * table[None, :, :], axis=1)


def section_forward(stream, scale_rows, up_blocks, up_index, down_blocks, down_index):
    row_count, feature_count = stream.shape
    block_size = up_blocks.shape[-1]
    stream_wide = stream.astype(jnp.float32)
    inverse = lax.rsqrt(jnp.mean(stream_wide * stream_wide, axis=-1, keepdims=True) + EPSILON)
    normed = (stream_wide * inverse * (1.0 + scale_rows)).astype(jnp.bfloat16)
    picked = normed.reshape(row_count, feature_count // block_size, block_size)[:, up_index, :]
    preact = jnp.einsum("rcki,ckij->rcj", picked, up_blocks, preferred_element_type=jnp.float32)
    hidden = activation(preact).astype(jnp.bfloat16)
    gathered = hidden[:, down_index, :]
    mixed_out = jnp.einsum(
        "rekj,ekjf->ref", gathered, down_blocks, preferred_element_type=jnp.float32
    )
    result = (stream_wide + mixed_out.reshape(row_count, feature_count)).astype(jnp.bfloat16)
    return (result, preact.reshape(row_count, -1), hidden.reshape(row_count, -1))


def section_backward(
    cotangent, stream, scale_rows, preact, up_blocks, up_index, down_blocks, down_index
):
    row_count, feature_count = stream.shape
    block_size = up_blocks.shape[-1]
    hidden_count = preact.shape[1]
    grad_blocks = cotangent.reshape(row_count, feature_count // block_size, block_size)
    grad_gathered = jnp.einsum(
        "ref,ekjf->rekj", grad_blocks, down_blocks, preferred_element_type=jnp.float32
    )
    grad_hidden = (
        jnp.zeros((row_count, hidden_count // block_size, block_size), jnp.float32)
        .at[:, down_index, :]
        .add(grad_gathered)
    )
    activated, pullback = jax.vjp(
        activation, preact.reshape(row_count, hidden_count // block_size, block_size)
    )
    grad_preact = pullback(grad_hidden)[0].astype(jnp.bfloat16)
    grad_picked = jnp.einsum(
        "rcj,ckij->rcki", grad_preact, up_blocks, preferred_element_type=jnp.float32
    )
    grad_normed = (
        jnp.zeros((row_count, feature_count // block_size, block_size), jnp.float32)
        .at[:, up_index, :]
        .add(grad_picked)
    )
    grad_normed = grad_normed.reshape(row_count, feature_count)
    stream_wide = stream.astype(jnp.float32)
    inverse = lax.rsqrt(jnp.mean(stream_wide * stream_wide, axis=-1, keepdims=True) + EPSILON)
    scaled = grad_normed * (1.0 + scale_rows)
    grad_stream = inverse * scaled - stream_wide * inverse * inverse * inverse * jnp.mean(
        scaled * stream_wide, axis=-1, keepdims=True
    )
    return (cotangent.astype(jnp.float32) + grad_stream).astype(jnp.bfloat16)


def pick_slot(stack, index):
    return lax.dynamic_index_in_dim(stack, index, 0, keepdims=False)


def store_slot(stack, index, value, valid):
    previous = pick_slot(stack, index)
    return lax.dynamic_update_index_in_dim(stack, jnp.where(valid, value, previous), index, 0)


def per_device(
    clean_latent,
    noise_latent,
    teacher_velocity,
    step_index,
    modulation,
    up_weight,
    up_rows,
    down_weight,
    down_rows,
):
    section_count = lax.axis_size("section")
    section_number = lax.axis_index("section")
    owner_count = lax.axis_size("dp")
    row_total, feature_count = clean_latent.shape
    block_size = up_weight.shape[2]
    hidden_blocks, keep_up = (up_rows.shape[1], up_rows.shape[2])
    width_blocks, keep_down = (down_rows.shape[1], down_rows.shape[2])
    hidden_count = hidden_blocks * block_size
    micro_rows = row_total // MICRO
    turn_count = MICRO + section_count - 1
    loss_scale = 1.0 / math.sqrt(row_total * owner_count)
    gathered_up = lax.all_gather(up_weight, "dp", axis=1, tiled=True)
    up_blocks = gathered_up.reshape(hidden_blocks, keep_up, block_size, block_size)
    up_index = up_rows[0]
    down_blocks = down_weight.reshape(width_blocks, keep_down, block_size, block_size)
    down_index = down_rows[0]
    table = modulation[0]
    fraction = (step_index.astype(jnp.float32) + 1.0) / table.shape[0]
    entry = (
        (1.0 - fraction)[:, None] * clean_latent.astype(jnp.float32)
        + fraction[:, None] * noise_latent.astype(jnp.float32)
    ).astype(jnp.bfloat16)
    entry = entry.reshape(MICRO, micro_rows, feature_count)
    scale_all = lookup(step_index, table).reshape(MICRO, micro_rows, feature_count)
    targets = teacher_velocity.reshape(MICRO, micro_rows, feature_count)

    def forward_turn(turn_index, carry):
        arrived, kept_stream, kept_preact, kept_hidden, kept_grad = carry
        micro_index = turn_index - section_number
        valid = (micro_index >= 0) & (micro_index < MICRO)
        clipped = jnp.clip(micro_index, 0, MICRO - 1)
        stream_in = jnp.where(section_number == 0, pick_slot(entry, clipped), arrived)
        scale_rows = pick_slot(scale_all, clipped)

        def forward_active(operand):
            return section_forward(
                stream_in, scale_rows, up_blocks, up_index, down_blocks, down_index
            )

        def forward_resting(operand):
            return (
                jnp.zeros_like(stream_in),
                jnp.zeros((micro_rows, hidden_count), jnp.float32),
                jnp.zeros((micro_rows, hidden_count), jnp.bfloat16),
            )

        result, preact, hidden = lax.cond(valid, forward_active, forward_resting, 0)
        cotangent = (
            (result.astype(jnp.float32) - pick_slot(targets, clipped).astype(jnp.float32))
            * loss_scale
        ).astype(jnp.bfloat16)
        kept_stream = store_slot(kept_stream, clipped, stream_in, valid)
        kept_preact = store_slot(kept_preact, clipped, preact, valid)
        kept_hidden = store_slot(kept_hidden, clipped, hidden, valid)
        kept_grad = store_slot(
            kept_grad, clipped, cotangent, valid & (section_number == section_count - 1)
        )
        arrived = from_behind(result, "section", 1)
        return (arrived, kept_stream, kept_preact, kept_hidden, kept_grad)

    start = (
        jnp.zeros((micro_rows, feature_count), jnp.bfloat16),
        jnp.zeros((MICRO, micro_rows, feature_count), jnp.bfloat16),
        jnp.zeros((MICRO, micro_rows, hidden_count), jnp.float32),
        jnp.zeros((MICRO, micro_rows, hidden_count), jnp.bfloat16),
        jnp.zeros((MICRO, micro_rows, feature_count), jnp.bfloat16),
    )
    arrived, kept_stream, kept_preact, kept_hidden, kept_grad = lax.fori_loop(
        0, turn_count, forward_turn, start
    )

    def backward_turn(turn_index, carry):
        arrived_grad, kept_cotangent = carry
        micro_index = turn_index - (section_count - 1 - section_number)
        valid = (micro_index >= 0) & (micro_index < MICRO)
        clipped = jnp.clip(micro_index, 0, MICRO - 1)
        incoming = jnp.where(
            section_number == section_count - 1, pick_slot(kept_grad, clipped), arrived_grad
        )

        def backward_active(operand):
            return section_backward(
                incoming,
                pick_slot(kept_stream, clipped),
                pick_slot(scale_all, clipped),
                pick_slot(kept_preact, clipped),
                up_blocks,
                up_index,
                down_blocks,
                down_index,
            )

        def backward_resting(operand):
            return jnp.zeros_like(incoming)

        grad_stream = lax.cond(valid, backward_active, backward_resting, 0)
        kept_cotangent = store_slot(kept_cotangent, clipped, incoming, valid)
        arrived_grad = from_behind(grad_stream, "section", -1)
        return (arrived_grad, kept_cotangent)

    start_back = (
        jnp.zeros((micro_rows, feature_count), jnp.bfloat16),
        jnp.zeros((MICRO, micro_rows, feature_count), jnp.bfloat16),
    )
    arrived_grad, kept_cotangent = lax.fori_loop(0, turn_count, backward_turn, start_back)
    all_rows = MICRO * micro_rows
    hidden_rows = kept_hidden.reshape(all_rows, hidden_count)
    grad_rows_all = kept_cotangent.reshape(all_rows, feature_count)
    packed_rows = width_blocks * keep_down * block_size
    gathered = hidden_rows.reshape(all_rows, hidden_blocks, block_size)[:, down_index, :]
    weight_term = jnp.einsum(
        "tejh,tef->ejhf",
        gathered,
        grad_rows_all.reshape(all_rows, width_blocks, block_size),
        preferred_element_type=jnp.float32,
    )
    grad_down = lax.psum_scatter(
        weight_term.reshape(1, packed_rows, block_size), "dp", scatter_dimension=1, tiled=True
    )
    return grad_down


def solution(mesh):
    in_specs = (
        P("dp", None),
        P("dp", None),
        P("dp", None),
        P("dp"),
        P("section", None, None),
        P("section", "dp", None),
        P("section", None, None),
        P("section", None, None),
        P("section", None, None),
    )
    out_specs = P("section", "dp", None)
    return jax.shard_map(
        per_device, mesh=mesh, in_specs=in_specs, out_specs=out_specs, check_vma=False
    )
```

profile of v0, /device:TPU:5, one launch (start us, length us, event | category | flops | bytes accessed | tf_op | source)
XLA Modules:
  0.0 1119.4 jit_solution(2123157267478633781)
XLA Ops:
  16.2 82.4 %all-gather.2.cloned.1.call-done = bf16[1,36864,128]{2,1,0:T(8,128)(2,1)} async-done(((bf16[1,576,128]{2,1,0:T(8,128)(2,1)}), bf16[1,36864,128]{2,1,0:T(8,128)(2,1)}) %all-gather.2.cloned.1.call-update) | async-done | bytes 9437200 | tf_op jit(solution)/shard_map/all_gather | solution.py:116
  103.5 285.1 %while.39 = (s32[]{:T(128)}, bf16[64,1536]{1,0:T(8,128)(2,1)S(1)}, bf16[2,64,1536]{2,1,0:T(8,128)(2,1)}, f32[2,64,6144]{2,1,0:T(8,128)}, bf16[2,64,6144]{2,1,0:T...) while((s32[]{:T(128)}, bf16[64,1536]{1,0:T(8,128)(2,1)S(1)}, ...), condition=%wide.region_5.6_spmd, body=%wide.region_1.5_spmd.sunk | while | flops 1214156544 | bytes 98133112 | solution.py:172
  134.4 80.1 %collective-permute-done = bf16[64,1536]{1,0:T(8,128)(2,1)S(1)} collective-permute-done((bf16[64,1536]{1,0:T(8,128)(2,1)}, bf16[64,1536]{1,0:T(8,128)(2,1)S(1)}, u32[]{:S(2)}, u32[]{:S(2)}) %collective-permute-start) | collective-permute-done | bytes 196640 | tf_op jit(solution)/shard_map/while/body/eval_jaxpr/ppermute | solution.py:17
  217.2 45.3 %conditional.4 = (bf16[64,1536]{1,0:T(8,128)(2,1)S(1)}, f32[64,6144]{1,0:T(8,128)}, bf16[64,6144]{1,0:T(8,128)(2,1)S(1)}, f32[64,1536]{1,0:T(8,128)}) conditional(s32[]{:T(128)} %convert_element_type.162, () %tuple.92, (bf16[64,1536]{1,0:T(8,128)(2,1)S(1)}, f32[2,64,1536]{2,1,0:T(8,128)}, s32[]{:T(128)}, s32[48,6]{1,0:T(8,128)}, ...), branch_computations={%region_2.2_spmd, %region_3.4_spmd} | conditional | flops 1212681984 | bytes 56843296 | solution.py:151
  219.3 13.3 %gather_fusion = bf16[288,64,128]{2,1,0:T(8,128)(2,1)} fusion(bf16[64,12,128]{2,0,1:T(8,128)(2,1)S(1)} %copy_bitcast_fusion.2, s32[1024]{0:T(1024)S(1)} %pad_clamp_fusion.1), kind=kCustom, calls=%fused_computation | custom fusion | bytes 9438336 | tf_op jit(solution)/shard_map/while/body/eval_jaxpr/cond/branch_1_fun/gather | solution.py:37
  232.6 7.1 fusion.7
  239.9 13.3 %gather_fusion.1 = bf16[288,64,128]{2,1,0:T(8,128)(2,1)} fusion(bf16[64,48,128]{2,0,1:T(8,128)(2,1)S(1)} %get-tuple-element.731, s32[1024]{0:T(1024)S(1)} %pad_clamp_fusion), kind=kCustom, calls=%fused_computation.1 | custom fusion | bytes 9438336 | tf_op jit(solution)/shard_map/while/body/eval_jaxpr/cond/branch_1_fun/gather | solution.py:40
  253.2 7.0 convolution_bitcast_fusion
  276.6 45.3 %conditional.4 = (bf16[64,1536]{1,0:T(8,128)(2,1)S(1)}, f32[64,6144]{1,0:T(8,128)}, bf16[64,6144]{1,0:T(8,128)(2,1)S(1)}, f32[64,1536]{1,0:T(8,128)}) conditional(s32[]{:T(128)} %convert_element_type.162, () %tuple.92, (bf16[64,1536]{1,0:T(8,128)(2,1)S(1)}, f32[2,64,1536]{2,1,0:T(8,128)}, s32[]{:T(128)}, s32[48,6]{1,0:T(8,128)}, ...), branch_computations={%region_2.2_spmd, %region_3.4_spmd} | conditional | flops 1212681984 | bytes 56843296 | solution.py:151
  278.8 13.3 %gather_fusion = bf16[288,64,128]{2,1,0:T(8,128)(2,1)} fusion(bf16[64,12,128]{2,0,1:T(8,128)(2,1)S(1)} %copy_bitcast_fusion.2, s32[1024]{0:T(1024)S(1)} %pad_clamp_fusion.1), kind=kCustom, calls=%fused_computation | custom fusion | bytes 9438336 | tf_op jit(solution)/shard_map/while/body/eval_jaxpr/cond/branch_1_fun/gather | solution.py:37
  292.1 7.1 fusion.7
  299.3 13.3 %gather_fusion.1 = bf16[288,64,128]{2,1,0:T(8,128)(2,1)} fusion(bf16[64,48,128]{2,0,1:T(8,128)(2,1)S(1)} %get-tuple-element.731, s32[1024]{0:T(1024)S(1)} %pad_clamp_fusion), kind=kCustom, calls=%fused_computation.1 | custom fusion | bytes 9438336 | tf_op jit(solution)/shard_map/while/body/eval_jaxpr/cond/branch_1_fun/gather | solution.py:40
  312.7 7.1 convolution_bitcast_fusion
  338.9 41.7 %collective-permute-start = (bf16[64,1536]{1,0:T(8,128)(2,1)}, bf16[64,1536]{1,0:T(8,128)(2,1)S(1)}, u32[]{:S(2)}, u32[]{:S(2)}) collective-permute-start(bf16[64,1536]{1,0:T(8,128)(2,1)} %copy-done.6), channel_id=1, source_target_pairs={{0,64},{64,128},{128,192},{1,65},{65,129},{129,193},{2,66},{66,130... | collective-permute-start | bytes 589832 | tf_op jit(solution)/shard_map/while/body/eval_jaxpr/ppermute | solution.py:17
  389.4 402.4 %while.40 = (s32[]{:T(128)}, bf16[64,1536]{1,0:T(8,128)(2,1)S(1)}, bf16[2,64,1536]{2,1,0:T(8,128)(2,1)}, s32[]{:T(128)}, pred[]{:T(512)}, /*index=5*/bf16[2,64,1...) while((s32[]{:T(128)}, bf16[64,1536]{1,0:T(8,128)(2,1)S(1)}, ...), condition=%wide.region_13.14_spmd, body=%wide.region_6.13_spmd.sunk | while | flops 1222706944 | bytes 115030680 | solution.py:209
  394.7 91.9 %collective-permute-done.1 = bf16[64,1536]{1,0:T(8,128)(2,1)S(1)} collective-permute-done((bf16[64,1536]{1,0:T(8,128)(2,1)}, bf16[64,1536]{1,0:T(8,128)(2,1)S(1)}, u32[]{:S(2)}, u32[]{:S(2)}) %collective-permute-start.1) | collective-permute-done | bytes 196640 | tf_op jit(solution)/shard_map/while/body/eval_jaxpr/ppermute | solution.py:17
  489.3 89.1 %conditional.5 = (bf16[64,1536]{1,0:T(8,128)(2,1)S(1)}) conditional(s32[]{:T(128)} %convert_element_type.163, () %tuple.96, (bf16[64,1536]{1,0:T(8,128)(2,1)S(1)}, s32[]{:T(128)}, bf16[2,64,1536]{2,1,0:T(8,128)(2,1)}, s32[48,6]{1,0:T(8,128)}, s32[12,24]{1,0:T(8,128)S(1)}, /*index=5*/bf16[12,24,128,128]{3,2,1,0:T(8,128)(2,1)}, ...), branch_computations={%region_7.7_spmd, %region_8.12_spmd} | conditional | flops 1222510336 | bytes 112080184 | solution.py:200
  491.2 10.7 fusion.42
  502.2 29.7 %scatter_fusion = f32[64,48,128]{2,0,1:T(8,128)S(1)} fusion(f32[64,48,128]{2,0,1:T(8,128)S(1)} %broadcast.178, s32[288]{0:T(512)S(1)} %reshape.165, f32[288,64,128]{2,1,0:T(8,128)} %bitcast.172), kind=kCustom, calls=%fused_computation.3 | custom fusion | flops 2359296 | bytes 28312704 | tf_op jit(solution)/shard_map/while/body/eval_jaxpr/cond/branch_1_fun/scatter-add | solution.py:61
  532.0 10.7 fusion.25
  543.6 29.9 %scatter_fusion.1 = f32[64,12,128]{2,0,1:T(8,128)S(1)} fusion(f32[64,12,128]{2,0,1:T(8,128)S(1)} %broadcast.175, s32[288]{0:T(512)S(1)} %reshape.173, f32[288,64,128]{2,1,0:T(8,128)} %bitcast.174), kind=kCustom, calls=%fused_computation.4 | custom fusion | flops 2359296 | bytes 28312704 | tf_op jit(solution)/shard_map/while/body/eval_jaxpr/cond/branch_1_fun/scatter-add | solution.py:73
  580.9 4.7 collective-permute-done.1
  588.3 89.1 %conditional.5 = (bf16[64,1536]{1,0:T(8,128)(2,1)S(1)}) conditional(s32[]{:T(128)} %convert_element_type.163, () %tuple.96, (bf16[64,1536]{1,0:T(8,128)(2,1)S(1)}, s32[]{:T(128)}, bf16[2,64,1536]{2,1,0:T(8,128)(2,1)}, s32[48,6]{1,0:T(8,128)}, s32[12,24]{1,0:T(8,128)S(1)}, /*index=5*/bf16[12,24,128,128]{3,2,1,0:T(8,128)(2,1)}, ...), branch_computations={%region_7.7_spmd, %region_8.12_spmd} | conditional | flops 1222510336 | bytes 112080184 | solution.py:200
  590.2 10.7 fusion.42
  601.2 29.7 %scatter_fusion = f32[64,48,128]{2,0,1:T(8,128)S(1)} fusion(f32[64,48,128]{2,0,1:T(8,128)S(1)} %broadcast.178, s32[288]{0:T(512)S(1)} %reshape.165, f32[288,64,128]{2,1,0:T(8,128)} %bitcast.172), kind=kCustom, calls=%fused_computation.3 | custom fusion | flops 2359296 | bytes 28312704 | tf_op jit(solution)/shard_map/while/body/eval_jaxpr/cond/branch_1_fun/scatter-add | solution.py:61
  631.0 10.7 fusion.25
  642.6 29.9 %scatter_fusion.1 = f32[64,12,128]{2,0,1:T(8,128)S(1)} fusion(f32[64,12,128]{2,0,1:T(8,128)S(1)} %broadcast.175, s32[288]{0:T(512)S(1)} %reshape.173, f32[288,64,128]{2,1,0:T(8,128)} %bitcast.174), kind=kCustom, calls=%fused_computation.4 | custom fusion | flops 2359296 | bytes 28312704 | tf_op jit(solution)/shard_map/while/body/eval_jaxpr/cond/branch_1_fun/scatter-add | solution.py:73
  688.0 91.0 %collective-permute-start.1 = (bf16[64,1536]{1,0:T(8,128)(2,1)}, bf16[64,1536]{1,0:T(8,128)(2,1)S(1)}, u32[]{:S(2)}, u32[]{:S(2)}) collective-permute-start(bf16[64,1536]{1,0:T(8,128)(2,1)} %copy-done.7), channel_id=1, source_target_pairs={{64,0},{128,64},{192,128},{65,1},{129,65},{193,129},{66,2},{130,66... | collective-permute-start | bytes 589832 | tf_op jit(solution)/shard_map/while/body/eval_jaxpr/ppermute | solution.py:17
  795.5 10.3 gather_fusion.2
  805.9 12.7 %copy.62 = bf16[12,24,128,128]{2,3,1,0:T(8,128)(2,1)} copy(bf16[12,24,128,128]{3,2,1,0:T(8,128)(2,1)} %bitcast.180) | data formatting | bytes 18874368 | tf_op jit(solution)/shard_map/gather | solution.py:214
  818.6 10.2 fusion.50
  828.8 283.8 %reduce-scatter.2.cloned.1.call-done = f32[1,576,128]{2,1,0:T(8,128)} async-done(((f32[1,36864,128]{2,1,0:T(8,128)}), f32[1,576,128]{2,1,0:T(8,128)}) %reduce-scatter.2.cloned.1.call-update) | async-done | bytes 294928 | tf_op jit(solution)/shard_map/reduce_scatter | solution.py:221
  (259 shorter events, 159.1 us)
Async XLA Ops:
  6.5 92.0 %all-gather.2.cloned.1.call-start = ((), (), s32[]{:S(2)}) async-start(), calls=%async_computation.1 | async-start | bytes 9584640 | tf_op jit(solution)/shard_map/all_gather | solution.py:116
  7.3 1105.3 %reduce-scatter.2.cloned.1.call-start = ((), (), s32[]{:S(2)}) async-start(), calls=%async_computation.2 | async-start | bytes 19169280 | tf_op jit(solution)/shard_map/reduce_scatter | solution.py:221
  109.0 10.0 collective-permute-start
  111.8 1.9 copy-start
  114.5 2.0 copy-start.1
  115.9 2.0 copy-start.4
  115.9 2.0 copy-start.8
  125.3 89.2 %collective-permute-start = (bf16[64,1536]{1,0:T(8,128)(2,1)}, bf16[64,1536]{1,0:T(8,128)(2,1)S(1)}, u32[]{:S(2)}, u32[]{:S(2)}) collective-permute-start(bf16[64,1536]{1,0:T(8,128)(2,1)} %copy-done.6), channel_id=1, source_target_pairs={{0,64},{64,128},{128,192},{1,65},{65,129},{129,193},{2,66},{66,130... | collective-permute-start | bytes 589832 | tf_op jit(solution)/shard_map/while/body/eval_jaxpr/ppermute | solution.py:17
  127.2 1.9 copy-start
  129.9 2.0 copy-start.1
  131.3 2.0 copy-start.4
  131.3 2.0 copy-start.8
  134.4 80.1 %copy-start.5 = (bf16[2,64,1536]{2,1,0:T(8,128)(2,1)}, bf16[2,64,1536]{2,1,0:T(8,128)(2,1)S(1)}, u32[]{:S(2)}) copy-start(bf16[2,64,1536]{2,1,0:T(8,128)(2,1)S(1)} %fusion.68) | copy-start | bytes 1179652 | tf_op jit(solution)/shard_map/while
  263.1 10.8 collective-permute-start
  265.1 1.9 copy-start
  267.8 2.9 copy-start.1
  270.7 1.4 copy-start.4
  270.7 1.4 copy-start.8
  322.6 10.0 collective-permute-start
  324.5 1.9 copy-start
  327.2 2.9 copy-start.1
  330.1 1.4 copy-start.8
  338.9 48.9 %collective-permute-start = (bf16[64,1536]{1,0:T(8,128)(2,1)}, bf16[64,1536]{1,0:T(8,128)(2,1)S(1)}, u32[]{:S(2)}, u32[]{:S(2)}) collective-permute-start(bf16[64,1536]{1,0:T(8,128)(2,1)} %copy-done.6), channel_id=1, source_target_pairs={{0,64},{64,128},{128,192},{1,65},{65,129},{129,193},{2,66},{66,130... | collective-permute-start | bytes 589832 | tf_op jit(solution)/shard_map/while/body/eval_jaxpr/ppermute | solution.py:17
  380.6 1.9 copy-start
  383.3 2.0 copy-start.1
  384.6 2.1 copy-start.4
  384.6 2.1 copy-start.8
  392.8 93.9 %collective-permute-start.1 = (bf16[64,1536]{1,0:T(8,128)(2,1)}, bf16[64,1536]{1,0:T(8,128)(2,1)S(1)}, u32[]{:S(2)}, u32[]{:S(2)}) collective-permute-start(bf16[64,1536]{1,0:T(8,128)(2,1)} %copy-done.7), channel_id=1, source_target_pairs={{64,0},{128,64},{192,128},{65,1},{129,65},{193,129},{66,2},{130,66... | collective-permute-start | bytes 589832 | tf_op jit(solution)/shard_map/while/body/eval_jaxpr/ppermute | solution.py:17
  579.0 6.6 collective-permute-start.1
  678.0 6.6 collective-permute-start.1
  688.0 93.9 %collective-permute-start.1 = (bf16[64,1536]{1,0:T(8,128)(2,1)}, bf16[64,1536]{1,0:T(8,128)(2,1)S(1)}, u32[]{:S(2)}, u32[]{:S(2)}) collective-permute-start(bf16[64,1536]{1,0:T(8,128)(2,1)} %copy-done.7), channel_id=1, source_target_pairs={{64,0},{128,64},{192,128},{65,1},{129,65},{193,129},{66,2},{130,66... | collective-permute-start | bytes 589832 | tf_op jit(solution)/shard_map/while/body/eval_jaxpr/ppermute | solution.py:17
  785.2 6.6 collective-permute-start.1
  (26 other events, 23.3 us)
Sparse Core Ops, SparseCore 0:
  10.1 88.3 all-gather.1
  828.9 283.6 reduce-scatter.1
where the time goes:
time: 1130 us; the launch traced here: 1120 us
  waiting for transfers between devices  555 us (49%)
  other arithmetic  176 us (16%)
  starting transfers between devices  151 us (13%)
  local copies, waits for them, and re-layouts  143 us (13%)
  matrix products  81.4 us (7%)
  between operations  13.5 us (1%)
    reduce_scatter x1, waiting for transfers between devices, per_device(): lax.psum_scatter(weight_term.reshape(1, packed_rows, block_size), 'dp', s...  284 us
    ppermute x10, waiting for transfers between devices, from_behind(): return lax.ppermute(block, axis, route)  188 us
    ppermute x10, starting transfers between devices, from_behind(): return lax.ppermute(block, axis, route)  151 us
    all_gather x1, waiting for transfers between devices, per_device(): gathered_up = lax.all_gather(up_weight, 'dp', axis=1, tiled=True)  82.4 us
    scatter-add x2, other arithmetic, section_backward(): grad_normed = jnp.zeros((row_count, feature_count // block_size, block_si...  59.7 us
    scatter-add x2, other arithmetic, section_backward(): grad_hidden = jnp.zeros((row_count, hidden_count // block_size, block_siz...  59.5 us
    dynamic_update_slice x25, other arithmetic, store_slot(): lax.dynamic_update_index_in_dim(stack, jnp.where(valid, value, previous),...  33 us
    gather x2, local copies, waits for them, and re-layouts, section_forward(): gathered = hidden[:, down_index, :]  26.7 us
  transfers between devices with their start and end apart: 12, of which 9 were waited for; matrix products, arithmetic and copies ran while one was open for 3% of the time, Pallas kernels for 0%

commit v1 on v0

v1 whole, which is shorter than its diff:
```python
import math

import jax
import jax.numpy as jnp
from jax import lax
from jax.experimental import pallas as pl
from jax.experimental.pallas import tpu as pltpu
from jax.sharding import PartitionSpec as P

EPSILON = 1e-06
F32 = jnp.float32
BF16 = jnp.bfloat16
STEPS_EACH = 4
GELU_A = math.sqrt(2.0 / math.pi)
GELU_B = 0.044715


def lane_block(index, size):
    return pl.ds(pl.multiple_of(index * size, size), size)


def split_range(total, parts):
    assert total % parts == 0
    return total // parts


def gelu_parts(v):
    squared = v * v
    t = jnp.tanh(v * (GELU_A + (GELU_A * GELU_B) * squared))
    half = 0.5 * (1.0 + t)
    slope = half + (0.5 * v) * (1.0 - t * t) * (GELU_A + (3.0 * GELU_A * GELU_B) * squared)
    return v * half, slope


def forward_kernel(
    keep_up, keep_down, up_per, down_per, full, up_index, down_index, x_ref, s_ref, uw_ref, dw_ref, *rest
):
    if full:
        out_ref, slope_ref, hidden_out_ref, normed, hidden = rest
    else:
        out_ref, normed, hidden = rest
    size = normed.shape[-1]
    width_blocks = normed.shape[0]
    step = pl.program_id(0)

    @pl.when(step == 0)
    def _():
        x = x_ref[...].astype(F32)
        inverse = lax.rsqrt(jnp.mean(x * x, axis=-1, keepdims=True) + EPSILON)
        for b in range(width_blocks):
            cols = slice(b * size, (b + 1) * size)
            piece = x_ref[:, cols].astype(F32)
            normed[b] = (piece * inverse * s_ref[:, cols]).astype(BF16)

    @pl.when(step < STEPS_EACH)
    def _():
        for cc in range(up_per):
            c = step * up_per + cc
            left = jnp.concatenate(
                [normed[up_index[c * keep_up + k]] for k in range(keep_up)], axis=1
            )
            rows = keep_up * size
            pre = jnp.dot(left, uw_ref[cc * rows : (cc + 1) * rows, :], preferred_element_type=F32)
            act, slope = gelu_parts(pre)
            act = act.astype(BF16)
            hidden[c] = act
            if full:
                slope_ref[cc] = slope
                hidden_out_ref[cc] = act

    @pl.when(step >= STEPS_EACH)
    def _():
        group = 4
        for ee in range(down_per):
            e = (step - STEPS_EACH) * down_per + ee
            total = x_ref[:, lane_block(e, size)].astype(F32)
            acc = None
            for k in range(0, keep_down, group):
                left = jnp.concatenate(
                    [hidden[down_index[e * keep_down + k + q]] for q in range(group)], axis=1
                )
                first = (ee * keep_down + k) * size
                term = jnp.dot(
                    left, dw_ref[first : first + group * size, :], preferred_element_type=F32
                )
                acc = term if acc is None else acc + term
            out_ref[:, lane_block(e, size)] = (total + acc).astype(BF16)


def first_half(i, *_):
    return (jnp.minimum(i, STEPS_EACH - 1), 0)


def second_half(i, *_):
    return (jnp.maximum(i - STEPS_EACH, 0), 0)


def whole(i, *_):
    return (0, 0)


def section_forward(stream, scale_plus, up_flat, up_index, down_flat, down_index, full):
    rows, features = stream.shape
    size = up_flat.shape[1]
    hidden_blocks, keep_up = up_index.shape
    width_blocks, keep_down = down_index.shape
    up_per = split_range(hidden_blocks, STEPS_EACH)
    down_per = split_range(width_blocks, STEPS_EACH)
    out_shape = [jax.ShapeDtypeStruct((rows, features), BF16)]
    out_specs = [pl.BlockSpec((rows, features), whole)]
    if full:
        part = lambda i, *_: (jnp.minimum(i, STEPS_EACH - 1), 0, 0)
        out_shape += [
            jax.ShapeDtypeStruct((hidden_blocks, rows, size), F32),
            jax.ShapeDtypeStruct((hidden_blocks, rows, size), BF16),
        ]
        out_specs += [pl.BlockSpec((up_per, rows, size), part)] * 2

    def body(*refs):
        forward_kernel(keep_up, keep_down, up_per, down_per, full, *refs)

    return pl.pallas_call(
        body,
        out_shape=out_shape,
        grid_spec=pltpu.PrefetchScalarGridSpec(
            num_scalar_prefetch=2,
            grid=(2 * STEPS_EACH,),
            in_specs=[
                pl.BlockSpec((rows, features), whole),
                pl.BlockSpec((rows, features), whole),
                pl.BlockSpec((up_flat.shape[0] // STEPS_EACH, size), first_half),
                pl.BlockSpec((down_flat.shape[0] // STEPS_EACH, size), second_half),
            ],
            out_specs=out_specs,
            scratch_shapes=[
                pltpu.VMEM((width_blocks, rows, size), BF16),
                pltpu.VMEM((hidden_blocks, rows, size), BF16),
            ],
        ),
        compiler_params=pltpu.CompilerParams(
            dimension_semantics=("arbitrary",), vmem_limit_bytes=36 << 20
        ),
        cost_estimate=pl.CostEstimate(
            flops=4 * rows * up_flat.size, bytes_accessed=4 * up_flat.size, transcendentals=0
        ),
        name="forward_full" if full else "forward",
    )(up_index.reshape(-1), down_index.reshape(-1), stream, scale_plus, up_flat, down_flat)


def contract_last(left, right):
    return lax.dot_general(left, right, (((1,), (1,)), ((), ())), preferred_element_type=F32)


def backward_kernel(
    keep_up, keep_down, up_per, down_per, up_index, down_index,
    cot_ref, x_ref, s_ref, slope_ref, uw_ref, dw_ref, out_ref, grad_hidden, grad_normed,
):
    size = grad_hidden.shape[-1]
    width_blocks = grad_normed.shape[0]
    step = pl.program_id(0)

    @pl.when(step == 0)
    def _():
        grad_hidden[...] = jnp.zeros_like(grad_hidden)
        grad_normed[...] = jnp.zeros_like(grad_normed)

    @pl.when(step < STEPS_EACH)
    def _():
        group = 4
        for ee in range(down_per):
            e = step * down_per + ee
            left = cot_ref[:, lane_block(e, size)]
            for k in range(0, keep_down, group):
                first = (ee * keep_down + k) * size
                term = contract_last(left, dw_ref[first : first + group * size, :])
                for q in range(group):
                    h = down_index[e * keep_down + k + q]
                    grad_hidden[h] += term[:, q * size : (q + 1) * size]

    @pl.when(step >= STEPS_EACH)
    def _():
        group = 3
        for cc in range(up_per):
            c = (step - STEPS_EACH) * up_per + cc
            left = (slope_ref[cc] * grad_hidden[c]).astype(BF16)
            for k in range(0, keep_up, group):
                first = (cc * keep_up + k) * size
                term = contract_last(left, uw_ref[first : first + group * size, :])
                for q in range(group):
                    w = up_index[c * keep_up + k + q]
                    grad_normed[w] += term[:, q * size : (q + 1) * size]

    @pl.when(step == 2 * STEPS_EACH - 1)
    def _():
        x = x_ref[...].astype(F32)
        features = x.shape[1]
        inverse = lax.rsqrt(jnp.mean(x * x, axis=-1, keepdims=True) + EPSILON)
        along = jnp.zeros((x.shape[0], size), F32)
        for b in range(width_blocks):
            cols = slice(b * size, (b + 1) * size)
            scaled = grad_normed[b] * s_ref[:, cols]
            grad_normed[b] = scaled
            along += scaled * x_ref[:, cols].astype(F32)
        mean = jnp.sum(along, axis=-1, keepdims=True) * (1.0 / features)
        factor = inverse * inverse * inverse * mean
        for b in range(width_blocks):
            cols = slice(b * size, (b + 1) * size)
            grad = inverse * grad_normed[b] - x_ref[:, cols].astype(F32) * factor
            out_ref[:, cols] = (cot_ref[:, cols].astype(F32) + grad).astype(BF16)


def section_backward(cot, stream, scale_plus, slope, up_flat, up_index, down_flat, down_index):
    rows, features = stream.shape
    size = up_flat.shape[1]
    hidden_blocks, keep_up = up_index.shape
    width_blocks, keep_down = down_index.shape
    up_per = split_range(hidden_blocks, STEPS_EACH)
    down_per = split_range(width_blocks, STEPS_EACH)

    def body(*refs):
        backward_kernel(keep_up, keep_down, up_per, down_per, *refs)

    flat = pl.BlockSpec((rows, features), whole)
    return pl.pallas_call(
        body,
        out_shape=jax.ShapeDtypeStruct((rows, features), BF16),
        grid_spec=pltpu.PrefetchScalarGridSpec(
            num_scalar_prefetch=2,
            grid=(2 * STEPS_EACH,),
            in_specs=[
                flat,
                flat,
                flat,
                pl.BlockSpec(
                    (up_per, rows, size), lambda i, *_: (jnp.maximum(i - STEPS_EACH, 0), 0, 0)
                ),
                pl.BlockSpec((up_flat.shape[0] // STEPS_EACH, size), second_half),
                pl.BlockSpec((down_flat.shape[0] // STEPS_EACH, size), first_half),
            ],
            out_specs=flat,
            scratch_shapes=[
                pltpu.VMEM((hidden_blocks, rows, size), F32),
                pltpu.VMEM((width_blocks, rows, size), F32),
            ],
        ),
        compiler_params=pltpu.CompilerParams(
            dimension_semantics=("arbitrary",), vmem_limit_bytes=36 << 20
        ),
        cost_estimate=pl.CostEstimate(
            flops=4 * rows * up_flat.size, bytes_accessed=4 * up_flat.size, transcendentals=0
        ),
        name="backward",
    )(up_index.reshape(-1), down_index.reshape(-1), cot, stream, scale_plus, slope, up_flat, down_flat)


def weight_kernel(keep_down, down_index, turned_ref, cot_ref, out_ref):
    size = out_ref.shape[1]
    e = pl.program_id(0)
    right = cot_ref[...]
    for k in range(keep_down):
        h = down_index[e * keep_down + k]
        out_ref[k * size : (k + 1) * size, :] = jnp.dot(
            turned_ref[h], right, preferred_element_type=F32
        )


def weight_gradient(turned, cot, down_index):
    hidden_blocks, size, rows = turned.shape
    width_blocks, keep_down = down_index.shape

    def body(*refs):
        weight_kernel(keep_down, *refs)

    return pl.pallas_call(
        body,
        out_shape=jax.ShapeDtypeStruct((width_blocks * keep_down * size, size), F32),
        grid_spec=pltpu.PrefetchScalarGridSpec(
            num_scalar_prefetch=1,
            grid=(width_blocks,),
            in_specs=[
                pl.BlockSpec((hidden_blocks, size, rows), lambda i, *_: (0, 0, 0)),
                pl.BlockSpec((rows, size), lambda i, *_: (0, i)),
            ],
            out_specs=pl.BlockSpec((keep_down * size, size), lambda i, *_: (i, 0)),
        ),
        compiler_params=pltpu.CompilerParams(
            dimension_semantics=("arbitrary",), vmem_limit_bytes=36 << 20
        ),
        cost_estimate=pl.CostEstimate(
            flops=2 * rows * width_blocks * keep_down * size * size,
            bytes_accessed=4 * width_blocks * keep_down * size * size,
            transcendentals=0,
        ),
        name="weight_gradient",
    )(down_index.reshape(-1), turned, cot)


def lookup(step_values, table):
    rows = step_values.shape[0]
    result = jnp.broadcast_to(table[0][None, :], (rows, table.shape[1]))
    for i in range(1, table.shape[0]):
        result = jnp.where((step_values == i)[:, None], table[i][None, :], result)
    return result


def per_device(
    clean_latent,
    noise_latent,
    teacher_velocity,
    step_index,
    modulation,
    up_weight,
    up_rows,
    down_weight,
    down_rows,
):
    section_count = lax.axis_size("section")
    section_number = lax.axis_index("section")
    owner_count = lax.axis_size("dp")
    row_total, feature_count = clean_latent.shape
    size = up_weight.shape[2]
    loss_scale = 1.0 / math.sqrt(row_total * owner_count)
    up_flat = lax.all_gather(up_weight, "dp", axis=1, tiled=True)[0]
    up_index = up_rows[0]
    down_flat = down_weight[0]
    down_index = down_rows[0]
    table = modulation[0]
    fraction = (step_index.astype(F32) + 1.0) / table.shape[0]
    entry = (
        (1.0 - fraction)[:, None] * clean_latent.astype(F32)
        + fraction[:, None] * noise_latent.astype(F32)
    ).astype(BF16)
    scale_plus = 1.0 + lookup(step_index, table)
    weights = (up_flat, up_index, down_flat, down_index)

    mine = entry
    for turn in range(section_count - 1):
        (result,) = section_forward(mine, scale_plus, *weights, False)
        arrived = lax.ppermute(result, "section", [(turn, turn + 1)])
        mine = jnp.where(section_number == turn + 1, arrived, mine)
    result, slope, hidden = section_forward(mine, scale_plus, *weights, True)

    cotangent = (
        (result.astype(F32) - teacher_velocity.astype(F32)) * loss_scale
    ).astype(BF16)
    for turn in range(section_count - 1, 0, -1):
        sent = section_backward(cotangent, mine, scale_plus, slope, *weights)
        arrived = lax.ppermute(sent, "section", [(turn, turn - 1)])
        cotangent = jnp.where(section_number == turn - 1, arrived, cotangent)

    turned = jnp.swapaxes(hidden, 1, 2)
    term = weight_gradient(turned, cotangent, down_index)
    return lax.psum_scatter(term[None], "dp", scatter_dimension=1, tiled=True)


def solution(mesh):
    in_specs = (
        P("dp", None),
        P("dp", None),
        P("dp", None),
        P("dp"),
        P("section", None, None),
        P("section", "dp", None),
        P("section", None, None),
        P("section", None, None),
        P("section", None, None),
    )
    out_specs = P("section", "dp", None)
    return jax.shard_map(
        per_device, mesh=mesh, in_specs=in_specs, out_specs=out_specs, check_vma=False
    )
```

time: 1130 us -> 467 us (0.41)
  waiting for transfers between devices: 555 us -> 328 us
  other arithmetic: 176 us -> 3.97 us
  starting transfers between devices: 151 us -> 7.53 us
  local copies, waits for them, and re-layouts: 143 us -> 17.5 us
  Pallas kernels: 0 us -> 90.6 us
  matrix products: 81.4 us -> 0 us
    ppermute x10 -> x6, waiting for transfers between devices: 188 us -> 41.7 us  [the longest x3 27.3 us: per_device(): arrived = lax.ppermute(result, 'section', [(turn, turn + 1)])]
    ppermute x10 -> x6, starting transfers between devices: 151 us -> 7.49 us  [the longest x3 4.2 us: per_device(): arrived = lax.ppermute(sent, 'section', [(turn, turn - 1)])]
    scatter-add x4 -> x0, other arithmetic: 119 us -> none  [the longest x2 59.7 us: section_backward(): grad_normed = jnp.zeros((row_count, feature_count // block_size, block_si...]
    pallas_call x0 -> x8, Pallas kernels: none -> 90.6 us  [the longest x4 43.5 us: section_forward(): pl.pallas_call(body, out_shape=out_shape, grid_spec=pltpu.PrefetchScalarG...]
    reduce_scatter x1, waiting for transfers between devices: 284 us -> 200 us  [per_device(): return lax.psum_scatter(term[None], 'dp', scatter_dimension=1, tiled=True)]
    dot_general x9 -> x0, matrix products: 81.4 us -> none  [the longest x2 21.4 us: section_backward(): jnp.einsum('ref,ekjf->rekj', grad_blocks, down_blocks, preferred_element_...]
    gather x6 -> x0, local copies, waits for them, and re-layouts: 76.3 us -> none  [the longest x2 26.7 us: section_forward(): gathered = hidden[:, down_index, :]]
    dynamic_update_slice x25 -> x0, other arithmetic: 33 us -> none  [store_slot(): lax.dynamic_update_index_in_dim(stack, jnp.where(valid, value, previous),...]
  transfers between devices with their start and end apart: 12 -> 8, of which waited for: 9 -> 6; matrix products, arithmetic and copies ran while one was open for 3% -> 1% of each run, Pallas kernels for 0% -> 0%
where the time goes in v1:
time: 467 us; the launch traced here: 462 us
  waiting for transfers between devices  328 us (70%)
  Pallas kernels  90.6 us (19%)
  local copies, waits for them, and re-layouts  17.5 us (4%)
  between operations  13.6 us (3%)
  starting transfers between devices  7.53 us (2%)
    reduce_scatter x1, waiting for transfers between devices, per_device(): return lax.psum_scatter(term[None], 'dp', scatter_dimension=1, tiled=True)  200 us
    all_gather x1, waiting for transfers between devices, per_device(): up_flat = lax.all_gather(up_weight, 'dp', axis=1, tiled=True)[0]  85.7 us
    pallas_call x4, Pallas kernels, section_forward(): pl.pallas_call(body, out_shape=out_shape, grid_spec=pltpu.PrefetchScalarG...  43.5 us
    pallas_call x3, Pallas kernels, section_backward(): pl.pallas_call(body, out_shape=jax.ShapeDtypeStruct((rows, features), BF1...  36.8 us
    ppermute x3, waiting for transfers between devices, per_device(): arrived = lax.ppermute(result, 'section', [(turn, turn + 1)])  27.3 us
    unnamed x11, local copies, waits for them, and re-layouts  15.5 us
    ppermute x3, waiting for transfers between devices, per_device(): arrived = lax.ppermute(sent, 'section', [(turn, turn - 1)])  14.4 us
    pallas_call x1, Pallas kernels, weight_gradient(): pl.pallas_call(body, out_shape=jax.ShapeDtypeStruct((width_blocks * keep_...  10.3 us
  transfers between devices with their start and end apart: 8, of which 6 were waited for; matrix products, arithmetic and copies ran while one was open for 1% of the time, Pallas kernels for 0%

profile of v1, /device:TPU:5, one launch (start us, length us, event | category | flops | bytes accessed | tf_op | source)
XLA Modules:
  0.0 461.6 jit_solution(1885435190595922101)
XLA Ops:
  6.5 0.7 all-gather.2.cloned.1.call-update
  7.3 0.7 reduce
  8.1 0.8 copy.11
  9.0 1.0 slice_reduce_fusion.3
  10.0 0.7 broadcast_subtract_fusion
  10.6 0.7 broadcast_compare_fusion.2
  11.3 1.5 select_add_fusion
  12.8 85.7 %all-gather.2.cloned.1.call-done = bf16[1,36864,128]{2,1,0:T(8,128)(2,1)} async-done(((bf16[1,576,128]{2,1,0:T(8,128)(2,1)}), bf16[1,36864,128]{2,1,0:T(8,128)(2,1)}) %all-gather.2.cloned.1.call-update) | async-done | bytes 9437200 | tf_op jit(solution)/shard_map/all_gather | solution.py:323
  98.5 3.7 copy-done
  102.2 10.8 %forward.3 = bf16[128,1536]{1,0:T(8,128)(2,1)S(1)} custom-call(s32[288]{0:T(512)S(1)} %reshape_squeeze.5.refs_0_, s32[288]{0:T(512)S(1)} %reshape_squeeze.4.refs_1_.refs_0_, bf16[128,1536]{1,0:T(8,128)(2,1)S(1)} %get-tuple-element.21.refs_2_, f32[128,1536]{1,0:T(8,128)S(1)} %get-tuple-element.20.refs_3_.refs_4_, bf16[36864,128]{1,0:T(8,128)(2,1)S(1)} %bitcast.4, ...), custom_call_target="tpu_custom_call" | custom-call | flops 2415919104 | bytes 18874368 | tf_op jit(solution)/shard_map/forward/pallas_call | solution.py:122
  113.0 0.7 collective-permute-start
  113.8 3.7 copy-done.1
  117.4 10.8 %forward.4 = bf16[128,1536]{1,0:T(8,128)(2,1)S(1)} custom-call(s32[288]{0:T(512)S(1)} %reshape_squeeze.5.refs_0_, s32[288]{0:T(512)S(1)} %reshape_squeeze.4.refs_1_.refs_0_, bf16[128,1536]{1,0:T(8,128)(2,1)S(1)} %broadcast_select_fusion.2.refs_2_, f32[128,1536]{1,0:T(8,128)S(1)} %get-tuple-element.20.refs_3_.refs_4_, bf16[36864,128]{1,0:T(8,128)(2,1)S(1)} %bitcast.5, ...), custom_call_target="tpu_custom_call" | custom-call | flops 2415919104 | bytes 18874368 | tf_op jit(solution)/shard_map/forward/pallas_call | solution.py:122
  128.2 1.3 collective-permute-start.1
  129.5 20.3 %collective-permute-done.1 = bf16[128,1536]{1,0:T(8,128)(2,1)S(1)} collective-permute-done((bf16[128,1536]{1,0:T(8,128)(2,1)S(1)}, bf16[128,1536]{1,0:T(8,128)(2,1)S(1)}, u32[]{:S(2)}, u32[]{:S(2)}) %collective-permute-start.1) | collective-permute-done | bytes 393248 | tf_op jit(solution)/shard_map/ppermute | solution.py:339
  149.9 3.7 copy-done.2
  153.5 10.8 %forward.5 = bf16[128,1536]{1,0:T(8,128)(2,1)S(1)} custom-call(s32[288]{0:T(512)S(1)} %reshape_squeeze.5.refs_0_, s32[288]{0:T(512)S(1)} %reshape_squeeze.4.refs_1_.refs_0_, bf16[128,1536]{1,0:T(8,128)(2,1)S(1)} %broadcast_select_fusion.4.refs_2_, f32[128,1536]{1,0:T(8,128)S(1)} %get-tuple-element.20.refs_3_.refs_4_, bf16[36864,128]{1,0:T(8,128)(2,1)S(1)} %bitcast.6, ...), custom_call_target="tpu_custom_call" | custom-call | flops 2415919104 | bytes 18874368 | tf_op jit(solution)/shard_map/forward/pallas_call | solution.py:122
  164.3 1.3 collective-permute-start.2
  165.7 7.0 %collective-permute-done.2 = bf16[128,1536]{1,0:T(8,128)(2,1)S(1)} collective-permute-done((bf16[128,1536]{1,0:T(8,128)(2,1)S(1)}, bf16[128,1536]{1,0:T(8,128)(2,1)S(1)}, u32[]{:S(2)}, u32[]{:S(2)}) %collective-permute-start.2) | collective-permute-done | bytes 393248 | tf_op jit(solution)/shard_map/ppermute | solution.py:339
  172.7 3.7 copy-done.3
  176.3 11.1 %forward_full.1 = (bf16[128,1536]{1,0:T(8,128)(2,1)S(1)}, f32[48,128,128]{2,1,0:T(8,128)S(1)}, bf16[48,128,128]{2,1,0:T(8,128)(2,1)S(1)}) custom-call(s32[288]{0:T(512)S(1)} %reshape_squeeze.5.refs_0_, s32[288]{0:T(512)S(1)} %reshape_squeeze.4.refs_1_.refs_0_, bf16[128,1536]{1,0:T(8,128)(2,1)S(1)} %broadcast_select_fusion.5.refs_2_.refs_3_, ...), custom_call_target="tpu_custom_call" | custom-call | flops 2415919104 | bytes 18874368 | tf_op jit(solution)/shard_map/forward_full/pallas_call | solution.py:122
  187.6 12.0 %backward.3 = bf16[128,1536]{1,0:T(8,128)(2,1)S(1)} custom-call(s32[288]{0:T(512)S(1)} %reshape_squeeze.5.refs_0_, s32[288]{0:T(512)S(1)} %reshape_squeeze.4.refs_1_.refs_0_, bf16[128,1536]{1,0:T(8,128)(2,1)S(1)} %multiply_convert_fusion.refs_2_, bf16[128,1536]{1,0:T(8,128)(2,1)S(1)} %broadcast_select_fusion.5.refs_2_.refs_3_, ...), custom_call_target="tpu_custom_call" | custom-call | flops 2415919104 | bytes 18874368 | tf_op jit(solution)/shard_map/backward/pallas_call | solution.py:224
  199.7 1.5 collective-permute-start.3
  201.1 8.9 %collective-permute-done.3 = bf16[128,1536]{1,0:T(8,128)(2,1)S(1)} collective-permute-done((bf16[128,1536]{1,0:T(8,128)(2,1)S(1)}, bf16[128,1536]{1,0:T(8,128)(2,1)S(1)}, u32[]{:S(2)}, u32[]{:S(2)}) %collective-permute-start.3) | collective-permute-done | bytes 393248 | tf_op jit(solution)/shard_map/ppermute | solution.py:348
  210.1 12.0 %backward.4 = bf16[128,1536]{1,0:T(8,128)(2,1)S(1)} custom-call(s32[288]{0:T(512)S(1)} %reshape_squeeze.5.refs_0_, s32[288]{0:T(512)S(1)} %reshape_squeeze.4.refs_1_.refs_0_, bf16[128,1536]{1,0:T(8,128)(2,1)S(1)} %broadcast_select_fusion.3.refs_2_, bf16[128,1536]{1,0:T(8,128)(2,1)S(1)} %broadcast_select_fusion.5.refs_2_.refs_3_, ...), custom_call_target="tpu_custom_call" | custom-call | flops 2415919104 | bytes 18874368 | tf_op jit(solution)/shard_map/backward/pallas_call | solution.py:224
  222.1 1.3 collective-permute-start.4
  223.5 5.5 %collective-permute-done.4 = bf16[128,1536]{1,0:T(8,128)(2,1)S(1)} collective-permute-done((bf16[128,1536]{1,0:T(8,128)(2,1)S(1)}, bf16[128,1536]{1,0:T(8,128)(2,1)S(1)}, u32[]{:S(2)}, u32[]{:S(2)}) %collective-permute-start.4) | collective-permute-done | bytes 393248 | tf_op jit(solution)/shard_map/ppermute | solution.py:348
  229.0 12.8 %backward.5 = bf16[128,1536]{1,0:T(8,128)(2,1)} custom-call(s32[288]{0:T(512)S(1)} %reshape_squeeze.5.refs_0_, s32[288]{0:T(512)S(1)} %reshape_squeeze.4.refs_1_.refs_0_, bf16[128,1536]{1,0:T(8,128)(2,1)S(1)} %broadcast_select_fusion.1.refs_2_, bf16[128,1536]{1,0:T(8,128)(2,1)S(1)} %broadcast_select_fusion.5.refs_2_.refs_3_, ...), custom_call_target="tpu_custom_call" | custom-call | flops 2415919104 | bytes 18874368 | tf_op jit(solution)/shard_map/backward/pallas_call | solution.py:224
  241.8 1.4 collective-permute-start.5
  243.2 0.9 copy.12
  244.2 10.3 %weight_gradient.1 = f32[36864,128]{1,0:T(8,128)} custom-call(s32[288]{0:T(512)S(1)} %reshape_squeeze.4.refs_1_.refs_0_, bf16[48,128,128]{2,1,0:T(8,128)(2,1)S(1)} %bitcast.11, bf16[128,1536]{1,0:T(8,128)(2,1)S(1)} %broadcast_select_fusion.refs_2_), custom_call_target="tpu_custom_call" | custom-call | flops 1207959552 | bytes 18874368 | tf_op jit(solution)/shard_map/weight_gradient/pallas_call | solution.py:274
  254.5 200.2 %reduce-scatter.2.cloned.1.call-done = f32[1,576,128]{2,1,0:T(8,128)} async-done(((f32[1,36864,128]{2,1,0:T(8,128)}), f32[1,576,128]{2,1,0:T(8,128)}) %reduce-scatter.2.cloned.1.call-update) | async-done | bytes 294928 | tf_op jit(solution)/shard_map/reduce_scatter | solution.py:353
  (20 shorter events, 0.7 us)
Async XLA Ops:
  6.5 92.0 %all-gather.2.cloned.1.call-start = ((), (), s32[]{:S(2)}) async-start(), calls=%async_computation.1 | async-start | bytes 9584640 | tf_op jit(solution)/shard_map/all_gather | solution.py:323
  7.3 447.5 %reduce-scatter.2.cloned.1.call-start = ((), (), s32[]{:S(2)}) async-start(), calls=%async_computation.2 | async-start | bytes 19169280 | tf_op jit(solution)/shard_map/reduce_scatter | solution.py:353
  98.5 3.7 copy-start
  113.0 0.7 collective-permute-start
  113.8 3.7 copy-start.1
  128.2 21.6 %collective-permute-start.1 = (bf16[128,1536]{1,0:T(8,128)(2,1)S(1)}, bf16[128,1536]{1,0:T(8,128)(2,1)S(1)}, u32[]{:S(2)}, u32[]{:S(2)}) collective-permute-start(bf16[128,1536]{1,0:T(8,128)(2,1)S(1)} %forward.4), channel_id=1, source_target_pairs={{64,128},{65,129},{66,130},{67,131},{68,132},{69,133},{70,134},{71... | collective-permute-start | bytes 1179656 | tf_op jit(solution)/shard_map/ppermute | solution.py:339
  149.9 3.7 copy-start.2
  164.3 8.3 %collective-permute-start.2 = (bf16[128,1536]{1,0:T(8,128)(2,1)S(1)}, bf16[128,1536]{1,0:T(8,128)(2,1)S(1)}, u32[]{:S(2)}, u32[]{:S(2)}) collective-permute-start(bf16[128,1536]{1,0:T(8,128)(2,1)S(1)} %forward.5), channel_id=1, source_target_pairs={{128,192},{129,193},{130,194},{131,195},{132,196},{133,197},{134,1... | collective-permute-start | bytes 1179656 | tf_op jit(solution)/shard_map/ppermute | solution.py:339
  172.7 3.7 copy-start.3
  176.3 11.1 %copy-start.4 = (bf16[128,1536]{1,0:T(8,128)(2,1)S(1)}, bf16[128,1536]{1,0:T(8,128)(2,1)}, u32[]{:S(2)}) copy-start(bf16[128,1536]{1,0:T(8,128)(2,1)} %param.11) | copy-start | bytes 1179652
  199.7 10.4 %collective-permute-start.3 = (bf16[128,1536]{1,0:T(8,128)(2,1)S(1)}, bf16[128,1536]{1,0:T(8,128)(2,1)S(1)}, u32[]{:S(2)}, u32[]{:S(2)}) collective-permute-start(bf16[128,1536]{1,0:T(8,128)(2,1)S(1)} %backward.3), channel_id=1, source_target_pairs={{192,128},{193,129},{194,130},{195,131},{196,132},{197,133},{198,1... | collective-permute-start | bytes 1179656 | tf_op jit(solution)/shard_map/ppermute | solution.py:348
  222.1 6.8 %collective-permute-start.4 = (bf16[128,1536]{1,0:T(8,128)(2,1)S(1)}, bf16[128,1536]{1,0:T(8,128)(2,1)S(1)}, u32[]{:S(2)}, u32[]{:S(2)}) collective-permute-start(bf16[128,1536]{1,0:T(8,128)(2,1)S(1)} %backward.4), channel_id=1, source_target_pairs={{128,64},{129,65},{130,66},{131,67},{132,68},{133,69},{134,70},{13... | collective-permute-start | bytes 1179656 | tf_op jit(solution)/shard_map/ppermute | solution.py:348
  241.8 2.3 collective-permute-start.5
Sparse Core Ops, SparseCore 0:
  10.1 88.3 all-gather.1
  254.6 200.0 reduce-scatter.1

commit v2 on v1

--- a/solution.py
+++ b/solution.py
@@ -10,6 +10,9 @@
 EPSILON = 1e-06
 F32 = jnp.float32
 BF16 = jnp.bfloat16
+F16 = jnp.float16
+CORES = 2
+CHIPS = 8
 STEPS_EACH = 4
 GELU_A = math.sqrt(2.0 / math.pi)
 GELU_B = 0.044715
@@ -138,7 +141,7 @@
             ],
         ),
         compiler_params=pltpu.CompilerParams(
-            dimension_semantics=("arbitrary",), vmem_limit_bytes=36 << 20
+            dimension_semantics=("arbitrary",), vmem_limit_bytes=56 << 20
         ),
         cost_estimate=pl.CostEstimate(
             flops=4 * rows * up_flat.size, bytes_accessed=4 * up_flat.size, transcendentals=0
@@ -244,7 +247,7 @@
             ],
         ),
         compiler_params=pltpu.CompilerParams(
-            dimension_semantics=("arbitrary",), vmem_limit_bytes=36 << 20
+            dimension_semantics=("arbitrary",), vmem_limit_bytes=56 << 20
         ),
         cost_estimate=pl.CostEstimate(
             flops=4 * rows * up_flat.size, bytes_accessed=4 * up_flat.size, transcendentals=0
@@ -253,46 +256,131 @@
     )(up_index.reshape(-1), down_index.reshape(-1), cot, stream, scale_plus, slope, up_flat, down_flat)
 
 
-def weight_kernel(keep_down, down_index, turned_ref, cot_ref, out_ref):
-    size = out_ref.shape[1]
-    e = pl.program_id(0)
-    right = cot_ref[...]
-    for k in range(keep_down):
-        h = down_index[e * keep_down + k]
-        out_ref[k * size : (k + 1) * size, :] = jnp.dot(
-            turned_ref[h], right, preferred_element_type=F32
-        )
-
-
-def weight_gradient(turned, cot, down_index):
-    hidden_blocks, size, rows = turned.shape
+def weight_kernel(keep_down, columns, place, down_index, *refs):
+    pieces, (cot_ref, keep_ref, give_ref, block_sum, largest) = refs[:-5], refs[-5:]
+    size = cot_ref.shape[1] // columns
+    chunk = block_sum.shape[0] // CORES
+    blocks = block_sum.shape[0] // size
+    far = pl.program_id(0)
+    y, z, core = place[0], place[1], place[2]
+    chips = pl.num_programs(0)
+    owner = y * chips + lax.rem(z + far, chips)
+
+    @pl.when(far == 0)
+    def _():
+        largest[...] = jnp.zeros_like(largest)
+
+    top = largest[...]
+    for g in range(blocks):
+        b = owner * blocks + g
+        e = lax.div(b, keep_down) - y * columns
+        h = down_index[b]
+        left = jnp.concatenate([piece[h] for piece in pieces], axis=1)
+        term = jnp.dot(left, cot_ref[:, lane_block(e, size)], preferred_element_type=F32)
+        block_sum[g * size : (g + 1) * size, :] = term
+        top = jnp.maximum(top, jnp.max(jnp.abs(term).reshape(-1, 8, size), axis=0))
+    largest[...] = top
+    rows = pl.ds(pl.multiple_of(far * chunk, 8), chunk)
+    keep_ref[rows, :] = block_sum[pl.ds(pl.multiple_of(core * chunk, 8), chunk), :]
+    give_ref[rows, :] = block_sum[pl.ds(pl.multiple_of((1 - core) * chunk, 8), chunk), :]
+
+    @pl.when(far == chips - 1)
+    def _():
+        peak = jnp.broadcast_to(jnp.max(top), (8, size))
+        keep_ref[chips * chunk :, :] = peak
+        give_ref[chips * chunk :, :] = peak
+
+
+def weight_gradient(pieces, cot, down_index, place, chips, owners):
+    hidden_blocks, size, rows = pieces[0].shape
     width_blocks, keep_down = down_index.shape
+    columns = cot.shape[1] // size
+    total_rows = width_blocks * keep_down * size
+    chunk = split_range(total_rows, owners)
 
     def body(*refs):
-        weight_kernel(keep_down, *refs)
-
+        weight_kernel(keep_down, columns, *refs)
+
+    held = pl.BlockSpec(
+        (hidden_blocks, size, rows), lambda i, *_: (0, 0, 0), pipeline_mode=pl.Buffered(1)
+    )
+    shape = jax.ShapeDtypeStruct((chips * chunk + 8, size), F32)
     return pl.pallas_call(
         body,
-        out_shape=jax.ShapeDtypeStruct((width_blocks * keep_down * size, size), F32),
+        out_shape=[shape, shape],
         grid_spec=pltpu.PrefetchScalarGridSpec(
-            num_scalar_prefetch=1,
-            grid=(width_blocks,),
-            in_specs=[
-                pl.BlockSpec((hidden_blocks, size, rows), lambda i, *_: (0, 0, 0)),
-                pl.BlockSpec((rows, size), lambda i, *_: (0, i)),
+            num_scalar_prefetch=2,
+            grid=(chips,),
+            in_specs=[held] * len(pieces) + [pl.BlockSpec(cot.shape, whole)],
+            out_specs=[pl.BlockSpec(shape.shape, whole)] * 2,
+            scratch_shapes=[
+                pltpu.VMEM((CORES * chunk, size), F32),
+                pltpu.VMEM((8, size), F32),
             ],
-            out_specs=pl.BlockSpec((keep_down * size, size), lambda i, *_: (i, 0)),
         ),
         compiler_params=pltpu.CompilerParams(
-            dimension_semantics=("arbitrary",), vmem_limit_bytes=36 << 20
+            dimension_semantics=("arbitrary",), vmem_limit_bytes=40 << 20
         ),
         cost_estimate=pl.CostEstimate(
-            flops=2 * rows * width_blocks * keep_down * size * size,
-            bytes_accessed=4 * width_blocks * keep_down * size * size,
+            flops=2 * rows * len(pieces) * chips * CORES * chunk * size,
+            bytes_accessed=2 * len(pieces) * pieces[0].size,
             transcendentals=0,
         ),
         name="weight_gradient",
-    )(down_index.reshape(-1), turned, cot)
+    )(place, down_index.reshape(-1), *pieces, cot)
+
+
+def dp_route(rows, chips, move):
+    owners = rows * chips * CORES
+    route = []
+    for source in range(owners):
+        y, rest = divmod(source, chips * CORES)
+        z, core = divmod(rest, CORES)
+        y, z, core = move(y, z, core)
+        route.append((source, (y % rows * chips + z % chips) * CORES + core % CORES))
+    return route
+
+
+def hidden_pieces(turned, rows, chips):
+    pieces = [turned]
+    for r in range(1, rows):
+        route = dp_route(rows, chips, lambda y, z, core: (y - r, z, core))
+        pieces.append(lax.ppermute(turned, "dp", route))
+    return pieces
+
+
+def reduce_weight_gradient(pieces, cot, down_index, rows, chips):
+    owners = rows * chips * CORES
+    number = lax.axis_index("dp")
+    y = lax.div(number, chips * CORES)
+    place = jnp.stack([y, lax.rem(lax.div(number, CORES), chips), lax.rem(number, CORES)])
+    columns = split_range(cot.shape[1], rows)
+    received = []
+    for r in range(rows):
+        first = lax.rem(y + rows - r, rows) * columns
+        part = lax.dynamic_slice_in_dim(cot, first, columns, 1)
+        if r:
+            route = dp_route(rows, chips, lambda y, z, core: (y - r, z, core))
+            part = lax.ppermute(part, "dp", route)
+        received.append(part)
+    keep, give = weight_gradient(
+        pieces, jnp.concatenate(received, axis=0), down_index, place, chips, owners
+    )
+    swap = dp_route(rows, chips, lambda y, z, core: (y, z, core + 1))
+    total = keep + lax.ppermute(give, "dp", swap)
+    chunk = split_range(keep.shape[0] - 8, chips)
+    bound = jnp.maximum(total[chips * chunk : chips * chunk + 1], 1e-30)
+    power = jnp.floor(13.0 - jnp.log2(bound))
+    factor = jnp.exp2(power)
+    tag = jnp.broadcast_to(power, (16, power.shape[1])).astype(F16)
+    result = total[:chunk]
+    for r in range(1, chips):
+        coded = (total[r * chunk : (r + 1) * chunk] * factor).astype(F16)
+        route = dp_route(rows, chips, lambda y, z, core: (y, z + r, core))
+        got = lax.ppermute(jnp.concatenate([coded, tag], axis=0), "dp", route)
+        got = got.astype(F32)
+        result = result + got[:chunk] * jnp.exp2(-got[chunk : chunk + 1])
+    return result
 
 
 def lookup(step_values, table):
@@ -343,14 +431,17 @@
     cotangent = (
         (result.astype(F32) - teacher_velocity.astype(F32)) * loss_scale
     ).astype(BF16)
+    rows = split_range(owner_count, CHIPS * CORES)
+    pieces = None
     for turn in range(section_count - 1, 0, -1):
         sent = section_backward(cotangent, mine, scale_plus, slope, *weights)
+        if pieces is None:
+            hidden, sent = lax.optimization_barrier((hidden, sent))
+            pieces = hidden_pieces(jnp.swapaxes(hidden, 1, 2), rows, CHIPS)
         arrived = lax.ppermute(sent, "section", [(turn, turn - 1)])
         cotangent = jnp.where(section_number == turn - 1, arrived, cotangent)
 
-    turned = jnp.swapaxes(hidden, 1, 2)
-    term = weight_gradient(turned, cotangent, down_index)
-    return lax.psum_scatter(term[None], "dp", scatter_dimension=1, tiled=True)
+    return reduce_weight_gradient(pieces, cotangent, down_index, rows, CHIPS)[None]
 
 
 def solution(mesh):

time: 467 us -> 374 us (0.80)
  waiting for transfers between devices: 328 us -> 203 us
  starting transfers between devices: 7.53 us -> 28.8 us
  Pallas kernels: 90.6 us -> 111 us
  local copies, waits for them, and re-layouts: 17.5 us -> 4.68 us
  other arithmetic: 3.97 us -> 12.4 us
    reduce_scatter x1 -> x0, waiting for transfers between devices: 200 us -> none  [per_device(): return lax.psum_scatter(term[None], 'dp', scatter_dimension=1, tiled=True)]
    ppermute x0 -> x14, waiting for transfers between devices: none -> 79.3 us  [the longest x3 51.3 us: reduce_weight_gradient(): part = lax.ppermute(part, 'dp', route)]
    ppermute x0 -> x14, starting transfers between devices: none -> 20.3 us  [the longest x7 11.8 us: reduce_weight_gradient(): got = lax.ppermute(jnp.concatenate([coded, tag], axis=0), 'dp', route)]
    unnamed x11 -> x19, local copies, waits for them, and re-layouts: 15.5 us -> 0.8 us
    pallas_call x4, Pallas kernels: 43.5 us -> 56.5 us  [section_forward(): pl.pallas_call(body, out_shape=out_shape, grid_spec=pltpu.PrefetchScalarG...]
    pallas_call x3, Pallas kernels: 36.8 us -> 47.2 us  [section_backward(): pl.pallas_call(body, out_shape=jax.ShapeDtypeStruct((rows, features), BF1...]
  transfers between devices with their start and end apart: 8 -> 21, of which waited for: 6 -> 13; matrix products, arithmetic and copies ran while one was open for 1% -> 3% of each run, Pallas kernels for 0% -> 4%
where the time goes in v2:
time: 374 us; the launch traced here: 373 us
  waiting for transfers between devices  203 us (54%)
  Pallas kernels  111 us (30%)
  starting transfers between devices  28.8 us (8%)
  between operations  13.7 us (4%)
  other arithmetic  12.4 us (3%)
  local copies, waits for them, and re-layouts  4.68 us (1%)
    all_gather x1, waiting for transfers between devices, per_device(): up_flat = lax.all_gather(up_weight, 'dp', axis=1, tiled=True)[0]  83.7 us
    pallas_call x4, Pallas kernels, section_forward(): pl.pallas_call(body, out_shape=out_shape, grid_spec=pltpu.PrefetchScalarG...  56.5 us
    ppermute x3, waiting for transfers between devices, reduce_weight_gradient(): part = lax.ppermute(part, 'dp', route)  51.3 us
    pallas_call x3, Pallas kernels, section_backward(): pl.pallas_call(body, out_shape=jax.ShapeDtypeStruct((rows, features), BF1...  47.2 us
    ppermute x3, waiting for transfers between devices, per_device(): arrived = lax.ppermute(result, 'section', [(turn, turn + 1)])  28 us
    ppermute x7, waiting for transfers between devices, reduce_weight_gradient(): got = lax.ppermute(jnp.concatenate([coded, tag], axis=0), 'dp', route)  23.9 us
    ppermute x7, starting transfers between devices, reduce_weight_gradient(): got = lax.ppermute(jnp.concatenate([coded, tag], axis=0), 'dp', route)  11.8 us
    ppermute x3, waiting for transfers between devices, per_device(): arrived = lax.ppermute(sent, 'section', [(turn, turn - 1)])  10.9 us
  transfers between devices with their start and end apart: 21, of which 13 were waited for; matrix products, arithmetic and copies ran while one was open for 3% of the time, Pallas kernels for 4%

profile of v2, /device:TPU:5, one launch (start us, length us, event | category | flops | bytes accessed | tf_op | source)
XLA Modules:
  0.0 372.8 jit_solution(17494022051516867217)
XLA Ops:
  12.4 2.4 select_add_fusion
  14.8 83.7 %all-gather.2.cloned.1.call-done = bf16[1,36864,128]{2,1,0:T(8,128)(2,1)} async-done(((bf16[1,576,128]{2,1,0:T(8,128)(2,1)}), bf16[1,36864,128]{2,1,0:T(8,128)(2,1)}) %all-gather.2.cloned.1.call-update) | async-done | bytes 9437200 | tf_op jit(solution)/shard_map/all_gather | solution.py:411
  98.5 13.8 %forward.3 = bf16[128,1536]{1,0:T(8,128)(2,1)} custom-call(s32[288]{0:T(512)} %reshape_squeeze.5.refs_0_, s32[288]{0:T(512)} %reshape_squeeze.4.refs_1_, bf16[128,1536]{1,0:T(8,128)(2,1)} %get-tuple-element.49.refs_2_, f32[128,1536]{1,0:T(8,128)} %get-tuple-element.48.refs_3_.refs_4_, bf16[36864,128]{1,0:T(8,128)(2,1)} %bitcast.37, bf16[36864,128]{1,0:T(8,128)(2,1)} %bitcast.30), custom_call_target="tpu_custom_call" | custom-call | flops 2415919104 | bytes 18874368 | tf_op jit(solution)/shard_map/forward/pallas_call | solution.py:125
  113.8 13.8 %forward.4 = bf16[128,1536]{1,0:T(8,128)(2,1)} custom-call(s32[288]{0:T(512)} %reshape_squeeze.5.refs_0_, s32[288]{0:T(512)} %reshape_squeeze.4.refs_1_, bf16[128,1536]{1,0:T(8,128)(2,1)} %broadcast_select_fusion.2.refs_2_, f32[128,1536]{1,0:T(8,128)} %get-tuple-element.48.refs_3_.refs_4_, bf16[36864,128]{1,0:T(8,128)(2,1)} %bitcast.38, ...), custom_call_target="tpu_custom_call" | custom-call | flops 2415919104 | bytes 18874368 | tf_op jit(solution)/shard_map/forward/pallas_call | solution.py:125
  128.9 20.7 %collective-permute-done.1 = bf16[128,1536]{1,0:T(8,128)(2,1)S(1)} collective-permute-done((bf16[128,1536]{1,0:T(8,128)(2,1)}, bf16[128,1536]{1,0:T(8,128)(2,1)S(1)}, u32[]{:S(2)}, u32[]{:S(2)}) %collective-permute-start.1) | collective-permute-done | bytes 393248 | tf_op jit(solution)/shard_map/ppermute | solution.py:427
  150.4 13.8 %forward.5 = bf16[128,1536]{1,0:T(8,128)(2,1)} custom-call(s32[288]{0:T(512)} %reshape_squeeze.5.refs_0_, s32[288]{0:T(512)} %reshape_squeeze.4.refs_1_, bf16[128,1536]{1,0:T(8,128)(2,1)} %broadcast_select_fusion.4.refs_2_, f32[128,1536]{1,0:T(8,128)} %get-tuple-element.48.refs_3_.refs_4_, bf16[36864,128]{1,0:T(8,128)(2,1)} %bitcast.39, ...), custom_call_target="tpu_custom_call" | custom-call | flops 2415919104 | bytes 18874368 | tf_op jit(solution)/shard_map/forward/pallas_call | solution.py:125
  164.1 1.3 collective-permute-start.2
  165.4 7.3 %collective-permute-done.2 = bf16[128,1536]{1,0:T(8,128)(2,1)S(1)} collective-permute-done((bf16[128,1536]{1,0:T(8,128)(2,1)}, bf16[128,1536]{1,0:T(8,128)(2,1)S(1)}, u32[]{:S(2)}, u32[]{:S(2)}) %collective-permute-start.2) | collective-permute-done | bytes 393248 | tf_op jit(solution)/shard_map/ppermute | solution.py:427
  173.5 15.2 %forward_full.1 = (bf16[128,1536]{1,0:T(8,128)(2,1)}, f32[48,128,128]{2,1,0:T(8,128)}, bf16[48,128,128]{2,1,0:T(8,128)(2,1)}) custom-call(s32[288]{0:T(512)} %reshape_squeeze.5.refs_0_, s32[288]{0:T(512)} %reshape_squeeze.4.refs_1_, bf16[128,1536]{1,0:T(8,128)(2,1)} %broadcast_select_fusion.5.refs_2_.refs_3_, f32[128,1536]{1,0:T(8,128)} %get-tuple-element.48.refs_3_.refs_4_, ...), custom_call_target="tpu_custom_call" | custom-call | flops 2415919104 | bytes 18874368 | tf_op jit(solution)/shard_map/forward_full/pallas_call | solution.py:125
  188.7 1.9 multiply_convert_fusion.refs_2_
  190.6 15.7 %backward.3 = bf16[128,1536]{1,0:T(8,128)(2,1)} custom-call(s32[288]{0:T(512)} %reshape_squeeze.5.refs_0_, s32[288]{0:T(512)} %reshape_squeeze.4.refs_1_, bf16[128,1536]{1,0:T(8,128)(2,1)} %multiply_convert_fusion.refs_2_, bf16[128,1536]{1,0:T(8,128)(2,1)} %broadcast_select_fusion.5.refs_2_.refs_3_, f32[128,1536]{1,0:T(8,128)} %get-tuple-element.48.refs_3_.refs_4_, ...), custom_call_target="tpu_custom_call" | custom-call | flops 2415919104 | bytes 18874368 | tf_op jit(solution)/shard_map/backward/pallas_call | solution.py:227
  206.3 1.5 collective-permute-start.6
  207.8 8.9 %collective-permute-done.6 = bf16[128,1536]{1,0:T(8,128)(2,1)S(1)} collective-permute-done((bf16[128,1536]{1,0:T(8,128)(2,1)}, bf16[128,1536]{1,0:T(8,128)(2,1)S(1)}, u32[]{:S(2)}, u32[]{:S(2)}) %collective-permute-start.6) | collective-permute-done | bytes 393248 | tf_op jit(solution)/shard_map/ppermute | solution.py:441
  217.5 15.7 %backward.4 = bf16[128,1536]{1,0:T(8,128)(2,1)} custom-call(s32[288]{0:T(512)} %reshape_squeeze.5.refs_0_, s32[288]{0:T(512)} %reshape_squeeze.4.refs_1_, bf16[128,1536]{1,0:T(8,128)(2,1)} %broadcast_select_fusion.3.refs_2_, bf16[128,1536]{1,0:T(8,128)(2,1)} %broadcast_select_fusion.5.refs_2_.refs_3_, f32[128,1536]{1,0:T(8,128)} %get-tuple-element.48.refs_3_.refs_4_, ...), custom_call_target="tpu_custom_call" | custom-call | flops 2415919104 | bytes 18874368 | tf_op jit(solution)/shard_map/backward/pallas_call | solution.py:227
  233.2 2.2 collective-permute-start.7
  238.4 2.0 collective-permute-done.7
  241.2 15.7 %backward.5 = bf16[128,1536]{1,0:T(8,128)(2,1)} custom-call(s32[288]{0:T(512)} %reshape_squeeze.5.refs_0_, s32[288]{0:T(512)} %reshape_squeeze.4.refs_1_, bf16[128,1536]{1,0:T(8,128)(2,1)} %broadcast_select_fusion.1.refs_2_, bf16[128,1536]{1,0:T(8,128)(2,1)} %broadcast_select_fusion.5.refs_2_.refs_3_, f32[128,1536]{1,0:T(8,128)} %get-tuple-element.48.refs_3_.refs_4_, ...), custom_call_target="tpu_custom_call" | custom-call | flops 2415919104 | bytes 18874368 | tf_op jit(solution)/shard_map/backward/pallas_call | solution.py:227
  256.9 1.5 collective-permute-start.8
  260.5 46.0 %collective-permute-done.10 = bf16[128,384]{1,0:T(8,128)(2,1)S(1)} collective-permute-done((bf16[128,384]{1,0:T(8,128)(2,1)}, bf16[128,384]{1,0:T(8,128)(2,1)S(1)}, u32[]{:S(2)}, u32[]{:S(2)}) %collective-permute-start.10) | collective-permute-done | bytes 98336 | tf_op jit(solution)/shard_map/ppermute | solution.py:364
  307.5 5.3 %collective-permute-done.11 = bf16[128,384]{1,0:T(8,128)(2,1)S(1)} collective-permute-done((bf16[128,384]{1,0:T(8,128)(2,1)S(1)}, bf16[128,384]{1,0:T(8,128)(2,1)S(1)}, u32[]{:S(2)}, u32[]{:S(2)}) %collective-permute-start.11) | collective-permute-done | bytes 98336 | tf_op jit(solution)/shard_map/ppermute | solution.py:364
  312.8 6.9 %weight_gradient.1 = (f32[4616,128]{1,0:T(8,128)S(1)}, f32[4616,128]{1,0:T(8,128)S(1)}) custom-call(s32[3]{0:T(128)S(1)} %pad_add_fusion.refs_0_, s32[288]{0:T(512)S(1)} %copy-done, bf16[48,128,128]{2,1,0:T(8,128)(2,1)S(1)} %bitcast.29, bf16[48,128,128]{2,1,0:T(8,128)(2,1)S(1)} %collective-permute-done.3.refs_3_, ...), custom_call_target="tpu_custom_call" | custom-call | flops 1207959552 | bytes 6291456 | tf_op jit(solution)/shard_map/weight_gradient/pallas_call | solution.py:308
  319.7 4.3 %collective-permute-start.12 = (f32[4616,128]{1,0:T(8,128)S(1)}, f32[4616,128]{1,0:T(8,128)S(1)}, u32[]{:S(2)}, u32[]{:S(2)}) collective-permute-start(f32[4616,128]{1,0:T(8,128)S(1)} %get-tuple-element.18), channel_id=1, source_target_pairs={{0,1},{1,0},{2,3},{3,2},{4,5},{5,4},{6,7},{7,6},{8,9},{9,8},{10,11... | collective-permute-start | bytes 7090184 | tf_op jit(solution)/shard_map/ppermute | solution.py:370
  324.0 4.2 %collective-permute-done.12 = f32[4616,128]{1,0:T(8,128)S(1)} collective-permute-done((f32[4616,128]{1,0:T(8,128)S(1)}, f32[4616,128]{1,0:T(8,128)S(1)}, u32[]{:S(2)}, u32[]{:S(2)}) %collective-permute-start.12) | collective-permute-done | bytes 2363424 | tf_op jit(solution)/shard_map/ppermute | solution.py:370
  329.0 2.2 collective-permute-start.19
  331.9 2.2 collective-permute-start.17
  334.1 2.6 collective-permute-start.16
  336.7 1.4 collective-permute-start.15
  338.1 2.8 collective-permute-start.14
  340.9 3.0 collective-permute-done.18
  344.0 3.1 collective-permute-done.17
  347.2 9.6 %collective-permute-done.15 = f16[592,128]{1,0:T(8,128)(2,1)S(1)} collective-permute-done((f16[592,128]{1,0:T(8,128)(2,1)S(1)}, f16[592,128]{1,0:T(8,128)(2,1)S(1)}, u32[]{:S(2)}, u32[]{:S(2)}) %collective-permute-start.15) | collective-permute-done | bytes 151584 | tf_op jit(solution)/shard_map/ppermute | solution.py:380
  358.0 7.0 %collective-permute-done.13 = f16[592,128]{1,0:T(8,128)(2,1)S(1)} collective-permute-done((f16[592,128]{1,0:T(8,128)(2,1)S(1)}, f16[592,128]{1,0:T(8,128)(2,1)S(1)}, u32[]{:S(2)}, u32[]{:S(2)}) %collective-permute-start.13) | collective-permute-done | bytes 151584 | tf_op jit(solution)/shard_map/ppermute | solution.py:380
  (77 shorter events, 21.6 us)
Async XLA Ops:
  6.5 92.0 %all-gather.2.cloned.1.call-start = ((), (), s32[]{:S(2)}) async-start(), calls=%async_computation | async-start | bytes 9584640 | tf_op jit(solution)/shard_map/all_gather | solution.py:411
  98.5 14.5 %copy-start.6 = (bf16[128,1536]{1,0:T(8,128)(2,1)S(1)}, bf16[128,1536]{1,0:T(8,128)(2,1)}, u32[]{:S(2)}) copy-start(bf16[128,1536]{1,0:T(8,128)(2,1)} %get-tuple-element.49.refs_2_) | copy-start | bytes 1179652
  112.3 0.7 collective-permute-start
  113.8 35.8 %copy-start.3 = (bf16[128,1536]{1,0:T(8,128)(2,1)S(1)}, bf16[128,1536]{1,0:T(8,128)(2,1)}, u32[]{:S(2)}) copy-start(bf16[128,1536]{1,0:T(8,128)(2,1)} %broadcast_select_fusion.2.refs_2_) | copy-start | bytes 1179652
  127.6 22.0 %collective-permute-start.1 = (bf16[128,1536]{1,0:T(8,128)(2,1)}, bf16[128,1536]{1,0:T(8,128)(2,1)S(1)}, u32[]{:S(2)}, u32[]{:S(2)}) collective-permute-start(bf16[128,1536]{1,0:T(8,128)(2,1)} %forward.4), channel_id=1, source_target_pairs={{64,128},{65,129},{66,130},{67,131},{68,132},{69,133},{70,134},{71... | collective-permute-start | bytes 1179656 | tf_op jit(solution)/shard_map/ppermute | solution.py:427
  150.4 22.4 %copy-start.4 = (bf16[128,1536]{1,0:T(8,128)(2,1)S(1)}, bf16[128,1536]{1,0:T(8,128)(2,1)}, u32[]{:S(2)}) copy-start(bf16[128,1536]{1,0:T(8,128)(2,1)} %broadcast_select_fusion.4.refs_2_) | copy-start | bytes 1179652
  164.1 8.6 %collective-permute-start.2 = (bf16[128,1536]{1,0:T(8,128)(2,1)}, bf16[128,1536]{1,0:T(8,128)(2,1)S(1)}, u32[]{:S(2)}, u32[]{:S(2)}) collective-permute-start(bf16[128,1536]{1,0:T(8,128)(2,1)} %forward.5), channel_id=1, source_target_pairs={{128,192},{129,193},{130,194},{131,195},{132,196},{133,197},{134,1... | collective-permute-start | bytes 1179656 | tf_op jit(solution)/shard_map/ppermute | solution.py:427
  173.5 15.2 %copy-start.8 = (bf16[128,1536]{1,0:T(8,128)(2,1)S(1)}, bf16[128,1536]{1,0:T(8,128)(2,1)}, u32[]{:S(2)}) copy-start(bf16[128,1536]{1,0:T(8,128)(2,1)} %param.11) | copy-start | bytes 1179652
  190.6 26.1 %copy-start.5 = (bf16[128,1536]{1,0:T(8,128)(2,1)S(1)}, bf16[128,1536]{1,0:T(8,128)(2,1)}, u32[]{:S(2)}) copy-start(bf16[128,1536]{1,0:T(8,128)(2,1)} %multiply_convert_fusion.refs_2_) | copy-start | bytes 1179652
  206.3 10.4 %collective-permute-start.6 = (bf16[128,1536]{1,0:T(8,128)(2,1)}, bf16[128,1536]{1,0:T(8,128)(2,1)S(1)}, u32[]{:S(2)}, u32[]{:S(2)}) collective-permute-start(bf16[128,1536]{1,0:T(8,128)(2,1)} %backward.3), channel_id=1, source_target_pairs={{192,128},{193,129},{194,130},{195,131},{196,132},{197,133},{198,1... | collective-permute-start | bytes 1179656 | tf_op jit(solution)/shard_map/ppermute | solution.py:441
  217.5 17.9 %copy-start.7 = (bf16[48,128,128]{2,1,0:T(8,128)(2,1)S(1)}, bf16[48,128,128]{2,1,0:T(8,128)(2,1)}, u32[]{:S(2)}) copy-start(bf16[48,128,128]{2,1,0:T(8,128)(2,1)} %get-tuple-element.15) | copy-start | bytes 4718596
  233.2 7.2 %copy-start.2 = (bf16[128,1536]{1,0:T(8,128)(2,1)S(1)}, bf16[128,1536]{1,0:T(8,128)(2,1)}, u32[]{:S(2)}) copy-start(bf16[128,1536]{1,0:T(8,128)(2,1)} %broadcast_select_fusion.3.refs_2_) | copy-start | bytes 1179652
  233.2 7.2 %collective-permute-start.7 = (bf16[128,1536]{1,0:T(8,128)(2,1)}, bf16[128,1536]{1,0:T(8,128)(2,1)}, u32[]{:S(2)}, u32[]{:S(2)}) collective-permute-start(bf16[128,1536]{1,0:T(8,128)(2,1)} %backward.4), channel_id=1, source_target_pairs={{128,64},{129,65},{130,66},{131,67},{132,68},{133,69},{134,70},{13... | collective-permute-start | bytes 1179656 | tf_op jit(solution)/shard_map/ppermute | solution.py:441
  236.3 76.4 %collective-permute-start.3 = (bf16[48,128,128]{2,1,0:T(8,128)(2,1)S(1)}, bf16[48,128,128]{2,1,0:T(8,128)(2,1)S(1)}, u32[]{:S(2)}, u32[]{:S(2)}) collective-permute-start(bf16[48,128,128]{2,1,0:T(8,128)(2,1)S(1)} %bitcast.26), channel_id=1, source_target_pairs={{0,48},{1,49},{2,50},{3,51},{4,52},{5,53},{6,54},{7,55},{8,56},{9,... | collective-permute-start | bytes 4718600 | tf_op jit(solution)/shard_map/ppermute | solution.py:348
  237.0 75.8 %collective-permute-start.4 = (bf16[48,128,128]{2,1,0:T(8,128)(2,1)S(1)}, bf16[48,128,128]{2,1,0:T(8,128)(2,1)}, u32[]{:S(2)}, u32[]{:S(2)}) collective-permute-start(bf16[48,128,128]{2,1,0:T(8,128)(2,1)S(1)} %bitcast.27), channel_id=1, source_target_pairs={{0,32},{1,33},{2,34},{3,35},{4,36},{5,37},{6,38},{7,39},{8,40},{9,... | collective-permute-start | bytes 4718600 | tf_op jit(solution)/shard_map/ppermute | solution.py:348
  238.1 74.7 %collective-permute-start.5 = (bf16[48,128,128]{2,1,0:T(8,128)(2,1)S(1)}, bf16[48,128,128]{2,1,0:T(8,128)(2,1)}, u32[]{:S(2)}, u32[]{:S(2)}) collective-permute-start(bf16[48,128,128]{2,1,0:T(8,128)(2,1)S(1)} %bitcast.28), channel_id=1, source_target_pairs={{0,16},{1,17},{2,18},{3,19},{4,20},{5,21},{6,22},{7,23},{8,24},{9,... | collective-permute-start | bytes 4718600 | tf_op jit(solution)/shard_map/ppermute | solution.py:348
  241.2 17.3 %copy-start.1 = (bf16[128,1536]{1,0:T(8,128)(2,1)S(1)}, bf16[128,1536]{1,0:T(8,128)(2,1)}, u32[]{:S(2)}) copy-start(bf16[128,1536]{1,0:T(8,128)(2,1)} %broadcast_select_fusion.1.refs_2_) | copy-start | bytes 1179652
  256.9 55.8 %copy-start = (s32[288]{0:T(512)S(1)}, s32[288]{0:T(512)}, u32[]{:S(2)}) copy-start(s32[288]{0:T(512)} %reshape_squeeze.4.refs_1_) | copy-start | bytes 3460
  256.9 1.6 collective-permute-start.8
  259.3 47.2 %collective-permute-start.10 = (bf16[128,384]{1,0:T(8,128)(2,1)}, bf16[128,384]{1,0:T(8,128)(2,1)S(1)}, u32[]{:S(2)}, u32[]{:S(2)}) collective-permute-start(bf16[128,384]{1,0:T(8,128)(2,1)} %get-tuple-element.34), channel_id=1, source_target_pairs={{0,32},{1,33},{2,34},{3,35},{4,36},{5,37},{6,38},{7,39},{8,40},{9,... | collective-permute-start | bytes 294920 | tf_op jit(solution)/shard_map/ppermute | solution.py:364
  260.5 52.3 %collective-permute-start.11 = (bf16[128,384]{1,0:T(8,128)(2,1)S(1)}, bf16[128,384]{1,0:T(8,128)(2,1)S(1)}, u32[]{:S(2)}, u32[]{:S(2)}) collective-permute-start(bf16[128,384]{1,0:T(8,128)(2,1)S(1)} %get-tuple-element.33), channel_id=1, source_target_pairs={{0,16},{1,17},{2,18},{3,19},{4,20},{5,21},{6,22},{7,23},{8,24},{9,... | collective-permute-start | bytes 294920 | tf_op jit(solution)/shard_map/ppermute | solution.py:364
  306.5 6.2 %collective-permute-start.9 = (bf16[128,384]{1,0:T(8,128)(2,1)S(1)}, bf16[128,384]{1,0:T(8,128)(2,1)S(1)}, u32[]{:S(2)}, u32[]{:S(2)}) collective-permute-start(bf16[128,384]{1,0:T(8,128)(2,1)S(1)} %get-tuple-element.35), channel_id=1, source_target_pairs={{0,48},{1,49},{2,50},{3,51},{4,52},{5,53},{6,54},{7,55},{8,56},{9,... | collective-permute-start | bytes 294920 | tf_op jit(solution)/shard_map/ppermute | solution.py:364
  319.7 8.5 %collective-permute-start.12 = (f32[4616,128]{1,0:T(8,128)S(1)}, f32[4616,128]{1,0:T(8,128)S(1)}, u32[]{:S(2)}, u32[]{:S(2)}) collective-permute-start(f32[4616,128]{1,0:T(8,128)S(1)} %get-tuple-element.18), channel_id=1, source_target_pairs={{0,1},{1,0},{2,3},{3,2},{4,5},{5,4},{6,7},{7,6},{8,9},{9,8},{10,11... | collective-permute-start | bytes 7090184 | tf_op jit(solution)/shard_map/ppermute | solution.py:370
  329.0 9.0 %collective-permute-start.19 = (f16[592,128]{1,0:T(8,128)(2,1)S(1)}, f16[592,128]{1,0:T(8,128)(2,1)S(1)}, u32[]{:S(2)}, u32[]{:S(2)}) collective-permute-start(f16[592,128]{1,0:T(8,128)(2,1)S(1)} %get-tuple-element.42), channel_id=1, source_target_pairs={{0,14},{1,15},{2,0},{3,1},{4,2},{5,3},{6,4},{7,5},{8,6},{9,7},{10,... | collective-permute-start | bytes 454664 | tf_op jit(solution)/shard_map/ppermute | solution.py:380
  331.2 12.8 %collective-permute-start.18 = (f16[592,128]{1,0:T(8,128)(2,1)S(1)}, f16[592,128]{1,0:T(8,128)(2,1)S(1)}, u32[]{:S(2)}, u32[]{:S(2)}) collective-permute-start(f16[592,128]{1,0:T(8,128)(2,1)S(1)} %get-tuple-element.41), channel_id=1, source_target_pairs={{0,12},{1,13},{2,14},{3,15},{4,0},{5,1},{6,2},{7,3},{8,4},{9,5},{1... | collective-permute-start | bytes 454664 | tf_op jit(solution)/shard_map/ppermute | solution.py:380
  331.9 15.1 %collective-permute-start.17 = (f16[592,128]{1,0:T(8,128)(2,1)S(1)}, f16[592,128]{1,0:T(8,128)(2,1)S(1)}, u32[]{:S(2)}, u32[]{:S(2)}) collective-permute-start(f16[592,128]{1,0:T(8,128)(2,1)S(1)} %get-tuple-element.40), channel_id=1, source_target_pairs={{0,10},{1,11},{2,12},{3,13},{4,14},{5,15},{6,0},{7,1},{8,2},{9,3},... | collective-permute-start | bytes 454664 | tf_op jit(solution)/shard_map/ppermute | solution.py:380
  334.1 13.0 %collective-permute-start.16 = (f16[592,128]{1,0:T(8,128)(2,1)S(1)}, f16[592,128]{1,0:T(8,128)(2,1)S(1)}, u32[]{:S(2)}, u32[]{:S(2)}) collective-permute-start(f16[592,128]{1,0:T(8,128)(2,1)S(1)} %get-tuple-element.39), channel_id=1, source_target_pairs={{0,8},{1,9},{2,10},{3,11},{4,12},{5,13},{6,14},{7,15},{8,0},{9,1},... | collective-permute-start | bytes 454664 | tf_op jit(solution)/shard_map/ppermute | solution.py:380
  336.7 20.1 %collective-permute-start.15 = (f16[592,128]{1,0:T(8,128)(2,1)S(1)}, f16[592,128]{1,0:T(8,128)(2,1)S(1)}, u32[]{:S(2)}, u32[]{:S(2)}) collective-permute-start(f16[592,128]{1,0:T(8,128)(2,1)S(1)} %get-tuple-element.38), channel_id=1, source_target_pairs={{0,6},{1,7},{2,8},{3,9},{4,10},{5,11},{6,12},{7,13},{8,14},{9,15},... | collective-permute-start | bytes 454664 | tf_op jit(solution)/shard_map/ppermute | solution.py:380
  338.1 19.9 %collective-permute-start.14 = (f16[592,128]{1,0:T(8,128)(2,1)S(1)}, f16[592,128]{1,0:T(8,128)(2,1)S(1)}, u32[]{:S(2)}, u32[]{:S(2)}) collective-permute-start(f16[592,128]{1,0:T(8,128)(2,1)S(1)} %get-tuple-element.37), channel_id=1, source_target_pairs={{0,4},{1,5},{2,6},{3,7},{4,8},{5,9},{6,10},{7,11},{8,12},{9,13},{1... | collective-permute-start | bytes 454664 | tf_op jit(solution)/shard_map/ppermute | solution.py:380
  344.0 21.0 %collective-permute-start.13 = (f16[592,128]{1,0:T(8,128)(2,1)S(1)}, f16[592,128]{1,0:T(8,128)(2,1)S(1)}, u32[]{:S(2)}, u32[]{:S(2)}) collective-permute-start(f16[592,128]{1,0:T(8,128)(2,1)S(1)} %get-tuple-element.36), channel_id=1, source_target_pairs={{0,2},{1,3},{2,4},{3,5},{4,6},{5,7},{6,8},{7,9},{8,10},{9,11},{10,... | collective-permute-start | bytes 454664 | tf_op jit(solution)/shard_map/ppermute | solution.py:380
Sparse Core Ops, SparseCore 0:
  10.1 88.3 all-gather.1

commit v3 on v2

v3 whole, which is shorter than its diff:
```python
import math

import jax
import jax.numpy as jnp
from jax import lax
from jax.experimental import pallas as pl
from jax.experimental.pallas import tpu as pltpu
from jax.sharding import PartitionSpec as P

EPSILON = 1e-06
F32 = jnp.float32
BF16 = jnp.bfloat16
F16 = jnp.float16
CORES = 2
CHIPS = 8
UP_UNROLL = 4
DOWN_UNROLL = 3
LIMIT = 12 << 20
PARTS = 4
ROWS = 4
GELU_A = math.sqrt(2.0 / math.pi)
GELU_B = 0.044715


def lane_block(index, size):
    return pl.ds(pl.multiple_of(index * size, size), size)


def split_range(total, parts):
    assert total % parts == 0
    return total // parts


def gelu_parts(v):
    squared = v * v
    t = jnp.tanh(v * (GELU_A + (GELU_A * GELU_B) * squared))
    half = 0.5 * (1.0 + t)
    slope = half + (0.5 * v) * (1.0 - t * t) * (GELU_A + (3.0 * GELU_A * GELU_B) * squared)
    return v * half, slope


def pick(take, arrived_ref, held_ref, out_ref):
    @pl.when(take)
    def _():
        out_ref[...] = arrived_ref[...]

    @pl.when(jnp.logical_not(take))
    def _():
        out_ref[...] = held_ref[...]


def forward_kernel(keep_up, keep_down, turn, last, loss_scale, *refs):
    refs = list(refs)
    up_index, down_index = refs[:2]
    del refs[:2]
    if turn:
        section, arrived_ref, held_ref = refs[:3]
        del refs[:3]
    else:
        x_ref = refs.pop(0)
    s_ref, uw_ref, dw_ref = refs[:3]
    del refs[:3]
    if last:
        teacher_ref = refs.pop(0)
    out_ref = refs.pop(0)
    if turn:
        x_ref = refs.pop(0)
        pick(section[0] == turn, arrived_ref, held_ref, x_ref)
    copies = []
    if last:
        slope_ref, hidden, normed = refs
    elif turn:
        normed, hidden = refs
    else:
        uw_to, dw_to, normed, hidden, arrival = refs
        for source, target in ((uw_ref, uw_to), (dw_ref, dw_to)):
            rows = source.shape[0] // PARTS
            for p in range(PARTS):
                span = pl.ds(p * rows, rows)
                copy = pltpu.make_async_copy(
                    source.at[span, :], target.at[span, :], arrival.at[len(copies)]
                )
                copy.start()
                copies.append(copy)
        uw_ref, dw_ref = uw_to, dw_to
    size = normed.shape[-1]
    width_blocks = normed.shape[0]
    hidden_blocks = hidden.shape[0]
    x = x_ref[...].astype(F32)
    inverse = lax.rsqrt(jnp.mean(x * x, axis=-1, keepdims=True) + EPSILON)
    for b in range(width_blocks):
        cols = slice(b * size, (b + 1) * size)
        piece = x_ref[:, cols].astype(F32)
        normed[b] = (piece * inverse * s_ref[:, cols]).astype(BF16)

    rows = keep_up * size

    def up_step(step, carry):
        for cc in range(UP_UNROLL):
            c = step * UP_UNROLL + cc
            left = jnp.concatenate(
                [normed[up_index[c * keep_up + k]] for k in range(keep_up)], axis=1
            )
            first = pl.multiple_of(c * rows, rows)
            pre = jnp.dot(left, uw_ref[pl.ds(first, rows), :], preferred_element_type=F32)
            act, slope = gelu_parts(pre)
            hidden[c] = act.astype(BF16)
            if last:
                slope_ref[c] = slope
        return carry

    group = 4

    def down_step(step, carry):
        for ee in range(DOWN_UNROLL):
            e = step * DOWN_UNROLL + ee
            acc = x_ref[:, lane_block(e, size)].astype(F32)
            for k in range(0, keep_down, group):
                left = jnp.concatenate(
                    [hidden[down_index[e * keep_down + k + q]] for q in range(group)], axis=1
                )
                first = pl.multiple_of((e * keep_down + k) * size, group * size)
                acc = acc + jnp.dot(
                    left, dw_ref[pl.ds(first, group * size), :], preferred_element_type=F32
                )
            result = acc.astype(BF16)
            if last:
                target = teacher_ref[:, lane_block(e, size)].astype(F32)
                result = ((result.astype(F32) - target) * loss_scale).astype(BF16)
            out_ref[:, lane_block(e, size)] = result
        return carry

    for step_of, count, waits in (
        (up_step, hidden_blocks // UP_UNROLL, copies[:PARTS]),
        (down_step, width_blocks // DOWN_UNROLL, copies[PARTS:]),
    ):
        if waits:
            per = split_range(count, PARTS)
            for p, copy in enumerate(waits):
                copy.wait()
                lax.fori_loop(p * per, (p + 1) * per, step_of, 0)
        else:
            lax.fori_loop(0, count, step_of, 0)


def whole(i, *_):
    return (0, 0)


SMEM = pl.BlockSpec(memory_space=pltpu.SMEM)
VMEM = pl.BlockSpec(memory_space=pltpu.VMEM)


def section_forward(turn, last, loss_scale, states, scale_plus, weights, indices, teacher):
    rows, features = scale_plus.shape
    size = weights[0].shape[1]
    hidden_blocks, keep_up = indices[0].shape
    width_blocks, keep_down = indices[1].shape
    stream = jax.ShapeDtypeStruct((rows, features), BF16)
    out_shape = [stream]
    scratch = [pltpu.VMEM((width_blocks, rows, size), BF16)]
    hidden = (hidden_blocks, rows, size)
    operands = [index.reshape(-1) for index in indices] + list(states)
    operands += [scale_plus, *weights]
    in_specs = [SMEM, SMEM] + ([SMEM, VMEM, VMEM] if turn else [VMEM]) + [VMEM]
    in_specs += [VMEM, VMEM] if turn else [pl.BlockSpec(memory_space=pltpu.HBM)] * 2
    if last:
        operands.append(teacher)
        in_specs.append(VMEM)
    if turn:
        out_shape.append(stream)
    if last:
        out_shape += [jax.ShapeDtypeStruct(hidden, F32), jax.ShapeDtypeStruct(hidden, BF16)]
    else:
        scratch.append(pltpu.VMEM(hidden, BF16))
    if not turn:
        out_shape += [jax.ShapeDtypeStruct(w.shape, w.dtype) for w in weights]
        scratch.append(pltpu.SemaphoreType.DMA((2 * PARTS,)))

    def body(*refs):
        forward_kernel(keep_up, keep_down, turn, last, loss_scale, *refs)

    return pl.pallas_call(
        body,
        out_shape=out_shape,
        in_specs=in_specs,
        out_specs=[VMEM] * len(out_shape),
        scratch_shapes=scratch,
        compiler_params=pltpu.CompilerParams(vmem_limit_bytes=LIMIT if turn else 40 << 20),
        cost_estimate=pl.CostEstimate(
            flops=4 * rows * weights[0].size, bytes_accessed=4 * features, transcendentals=0
        ),
        name=f"forward_{turn}",
    )(*operands)


def contract_last(left, right):
    return lax.dot_general(left, right, (((1,), (1,)), ((), ())), preferred_element_type=F32)


def backward_kernel(
    keep_up, keep_down, turn, first_turn, up_index, down_index, *refs
):
    if first_turn:
        cot_ref, x_ref, s_ref, slope_ref, uw_ref, dw_ref, out_ref, grad_hidden, grad_normed = refs
    else:
        section, arrived_ref, held_ref, *refs = refs
        x_ref, s_ref, slope_ref, uw_ref, dw_ref, out_ref, cot_ref, grad_hidden, grad_normed = refs
        pick(section[0] == turn, arrived_ref, held_ref, cot_ref)
    size = grad_hidden.shape[-1]
    width_blocks = grad_normed.shape[0]
    hidden_blocks = grad_hidden.shape[0]
    grad_hidden[...] = jnp.zeros_like(grad_hidden)
    grad_normed[...] = jnp.zeros_like(grad_normed)
    group = 4

    def down_step(step, carry):
        for ee in range(DOWN_UNROLL):
            e = step * DOWN_UNROLL + ee
            left = cot_ref[:, lane_block(e, size)]
            for k in range(0, keep_down, group):
                first = pl.multiple_of((e * keep_down + k) * size, group * size)
                term = contract_last(left, dw_ref[pl.ds(first, group * size), :])
                for q in range(group):
                    h = down_index[e * keep_down + k + q]
                    grad_hidden[h] += term[:, q * size : (q + 1) * size]
        return carry

    lax.fori_loop(0, width_blocks // DOWN_UNROLL, down_step, 0)
    part = 3

    def up_step(step, carry):
        for cc in range(UP_UNROLL):
            c = step * UP_UNROLL + cc
            left = (slope_ref[c] * grad_hidden[c]).astype(BF16)
            for k in range(0, keep_up, part):
                first = pl.multiple_of((c * keep_up + k) * size, part * size)
                term = contract_last(left, uw_ref[pl.ds(first, part * size), :])
                for q in range(part):
                    w = up_index[c * keep_up + k + q]
                    grad_normed[w] += term[:, q * size : (q + 1) * size]
        return carry

    lax.fori_loop(0, hidden_blocks // UP_UNROLL, up_step, 0)
    x = x_ref[...].astype(F32)
    features = x.shape[1]
    inverse = lax.rsqrt(jnp.mean(x * x, axis=-1, keepdims=True) + EPSILON)
    along = jnp.zeros((x.shape[0], size), F32)
    for b in range(width_blocks):
        cols = slice(b * size, (b + 1) * size)
        scaled = grad_normed[b] * s_ref[:, cols]
        grad_normed[b] = scaled
        along += scaled * x_ref[:, cols].astype(F32)
    mean = jnp.sum(along, axis=-1, keepdims=True) * (1.0 / features)
    factor = inverse * inverse * inverse * mean
    for b in range(width_blocks):
        cols = slice(b * size, (b + 1) * size)
        grad = inverse * grad_normed[b] - x_ref[:, cols].astype(F32) * factor
        out_ref[:, cols] = (cot_ref[:, cols].astype(F32) + grad).astype(BF16)


def section_backward(turn, first_turn, states, stream, scale_plus, slope, weights, indices):
    rows, features = stream.shape
    size = weights[0].shape[1]
    hidden_blocks, keep_up = indices[0].shape
    width_blocks, keep_down = indices[1].shape

    def body(*refs):
        backward_kernel(keep_up, keep_down, turn, first_turn, *refs)

    result = jax.ShapeDtypeStruct((rows, features), BF16)
    out_shape = [result] if first_turn else [result, result]
    in_specs = [SMEM, SMEM] + ([VMEM] if first_turn else [SMEM, VMEM, VMEM]) + [VMEM] * 5
    return pl.pallas_call(
        body,
        out_shape=out_shape,
        in_specs=in_specs,
        out_specs=[VMEM] * len(out_shape),
        scratch_shapes=[
            pltpu.VMEM((hidden_blocks, rows, size), F32),
            pltpu.VMEM((width_blocks, rows, size), F32),
        ],
        compiler_params=pltpu.CompilerParams(vmem_limit_bytes=LIMIT),
        cost_estimate=pl.CostEstimate(flops=1000000, bytes_accessed=100000, transcendentals=0),
        name=f"backward_{turn}",
    )(*[index.reshape(-1) for index in indices], *states, stream, scale_plus, slope, *weights)


def turn_kernel(source_ref, out_ref):
    def step(h, carry):
        for i in range(4):
            out_ref[h * 4 + i] = source_ref[h * 4 + i].T
        return carry

    lax.fori_loop(0, source_ref.shape[0] // 4, step, 0)


def turn_hidden(hidden):
    blocks, rows, size = hidden.shape
    return pl.pallas_call(
        turn_kernel,
        out_shape=jax.ShapeDtypeStruct((blocks, size, rows), hidden.dtype),
        in_specs=[VMEM],
        out_specs=VMEM,
        compiler_params=pltpu.CompilerParams(vmem_limit_bytes=LIMIT),
        cost_estimate=pl.CostEstimate(
            flops=20000 * hidden.size, bytes_accessed=4 * hidden.size, transcendentals=0
        ),
        name="turn_hidden",
    )(hidden)


def weight_kernel(keep_down, columns, place, down_index, *refs):
    pieces, (cot_ref, keep_ref, give_ref, block_sum, largest) = refs[:-5], refs[-5:]
    size = cot_ref.shape[1] // columns
    chunk = block_sum.shape[0] // CORES
    blocks = block_sum.shape[0] // size
    far = pl.program_id(0)
    y, z, core = place[0], place[1], place[2]
    chips = pl.num_programs(0)
    owner = y * chips + lax.rem(z + far, chips)

    @pl.when(far == 0)
    def _():
        largest[...] = jnp.zeros_like(largest)

    top = largest[...]
    for g in range(blocks):
        b = owner * blocks + g
        e = lax.div(b, keep_down) - y * columns
        h = down_index[b]
        near, low, high = pieces[:-2], pieces[-2], pieces[-1]
        half = low.shape[0]
        far_piece = jnp.where(
            h < half, low[jnp.minimum(h, half - 1)], high[jnp.maximum(h - half, 0)]
        )
        left = jnp.concatenate([piece[h] for piece in near] + [far_piece], axis=1)
        term = jnp.dot(left, cot_ref[:, lane_block(e, size)], preferred_element_type=F32)
        block_sum[g * size : (g + 1) * size, :] = term
        top = jnp.maximum(top, jnp.max(jnp.abs(term).reshape(-1, 8, size), axis=0))
    largest[...] = top
    rows = pl.ds(pl.multiple_of(far * chunk, 8), chunk)
    keep_ref[rows, :] = block_sum[pl.ds(pl.multiple_of(core * chunk, 8), chunk), :]
    give_ref[rows, :] = block_sum[pl.ds(pl.multiple_of((1 - core) * chunk, 8), chunk), :]

    @pl.when(far == chips - 1)
    def _():
        peak = jnp.broadcast_to(jnp.max(top), (8, size))
        keep_ref[chips * chunk :, :] = peak
        give_ref[chips * chunk :, :] = peak


def weight_gradient(pieces, cot, down_index, place, chips, owners):
    size = pieces[0].shape[1]
    width_blocks, keep_down = down_index.shape
    columns = cot.shape[1] // size
    total_rows = width_blocks * keep_down * size
    chunk = split_range(total_rows, owners)

    def body(*refs):
        weight_kernel(keep_down, columns, *refs)

    held = [
        pl.BlockSpec(piece.shape, lambda i, *_: (0, 0, 0), pipeline_mode=pl.Buffered(1))
        for piece in pieces
    ]
    shape = jax.ShapeDtypeStruct((chips * chunk + 8, size), F32)
    return pl.pallas_call(
        body,
        out_shape=[shape, shape],
        grid_spec=pltpu.PrefetchScalarGridSpec(
            num_scalar_prefetch=2,
            grid=(chips,),
            in_specs=held + [pl.BlockSpec(cot.shape, whole)],
            out_specs=[pl.BlockSpec(shape.shape, whole)] * 2,
            scratch_shapes=[
                pltpu.VMEM((CORES * chunk, size), F32),
                pltpu.VMEM((8, size), F32),
            ],
        ),
        compiler_params=pltpu.CompilerParams(
            dimension_semantics=("arbitrary",), vmem_limit_bytes=40 << 20
        ),
        cost_estimate=pl.CostEstimate(
            flops=2 * cot.shape[0] * chips * CORES * chunk * size,
            bytes_accessed=2 * len(pieces) * pieces[0].size,
            transcendentals=0,
        ),
        name="weight_gradient",
    )(place, down_index.reshape(-1), *pieces, cot)


def dp_route(rows, chips, move):
    owners = rows * chips * CORES
    route = []
    for source in range(owners):
        y, rest = divmod(source, chips * CORES)
        z, core = divmod(rest, CORES)
        y, z, core = move(y, z, core)
        route.append((source, (y % rows * chips + z % chips) * CORES + core % CORES))
    return route


def hidden_pieces(turned, rows, chips):
    assert rows == ROWS
    half = turned.shape[0] // 2
    down = dp_route(rows, chips, lambda y, z, core: (y - 1, z, core))
    up = dp_route(rows, chips, lambda y, z, core: (y + 1, z, core))
    after = lax.ppermute(turned, "dp", down)
    before = lax.ppermute(turned, "dp", up)
    low = lax.ppermute(after[:half], "dp", down)
    high = lax.ppermute(before[half:], "dp", up)
    return [turned, after, before, low, high]


def reduce_weight_gradient(pieces, cot, down_index, rows, chips):
    owners = rows * chips * CORES
    number = lax.axis_index("dp")
    y = lax.div(number, chips * CORES)
    place = jnp.stack([y, lax.rem(lax.div(number, CORES), chips), lax.rem(number, CORES)])
    columns = split_range(cot.shape[1], rows)
    received = []
    for r in (0, 1, rows - 1, 2):
        first = lax.rem(y + rows - r, rows) * columns
        part = lax.dynamic_slice_in_dim(cot, first, columns, 1)
        if r:
            route = dp_route(rows, chips, lambda y, z, core: (y - r, z, core))
            part = lax.ppermute(part, "dp", route)
        received.append(part)
    keep, give = weight_gradient(
        pieces, jnp.concatenate(received, axis=0), down_index, place, chips, owners
    )
    swap = dp_route(rows, chips, lambda y, z, core: (y, z, core + 1))
    total = keep + lax.ppermute(give, "dp", swap)
    chunk = split_range(keep.shape[0] - 8, chips)
    bound = jnp.maximum(total[chips * chunk : chips * chunk + 1], 1e-30)
    power = jnp.floor(13.0 - jnp.log2(bound))
    factor = jnp.exp2(power)
    tag = jnp.broadcast_to(power, (16, power.shape[1])).astype(F16)
    result = total[:chunk]
    for r in range(1, chips):
        coded = (total[r * chunk : (r + 1) * chunk] * factor).astype(F16)
        route = dp_route(rows, chips, lambda y, z, core: (y, z + r, core))
        got = lax.ppermute(jnp.concatenate([coded, tag], axis=0), "dp", route)
        got = got.astype(F32)
        result = result + got[:chunk] * jnp.exp2(-got[chunk : chunk + 1])
    return result


def lookup(step_values, table):
    rows = step_values.shape[0]
    result = jnp.broadcast_to(table[0][None, :], (rows, table.shape[1]))
    for i in range(1, table.shape[0]):
        result = jnp.where((step_values == i)[:, None], table[i][None, :], result)
    return result


def per_device(
    clean_latent,
    noise_latent,
    teacher_velocity,
    step_index,
    modulation,
    up_weight,
    up_rows,
    down_weight,
    down_rows,
):
    section_count = lax.axis_size("section")
    section_number = lax.axis_index("section")
    owner_count = lax.axis_size("dp")
    row_total, feature_count = clean_latent.shape
    size = up_weight.shape[2]
    loss_scale = 1.0 / math.sqrt(row_total * owner_count)
    up_flat = lax.all_gather(up_weight, "dp", axis=1, tiled=True)[0]
    up_index = up_rows[0]
    down_flat = down_weight[0]
    down_index = down_rows[0]
    table = modulation[0]
    fraction = (step_index.astype(F32) + 1.0) / table.shape[0]
    entry = (
        (1.0 - fraction)[:, None] * clean_latent.astype(F32)
        + fraction[:, None] * noise_latent.astype(F32)
    ).astype(BF16)
    scale_plus = 1.0 + lookup(step_index, table)
    indices = (up_index, down_index)
    section = section_number.reshape(1).astype(jnp.int32)
    section, entry = lax.optimization_barrier((section, entry))

    result, *weights = section_forward(
        0, False, loss_scale, (entry,), scale_plus, (up_flat, down_flat), indices, None
    )
    mine = entry
    for turn in range(1, section_count):
        last = turn == section_count - 1
        arrived = lax.ppermute(result, "section", [(turn - 1, turn)])
        result, mine, *kept = section_forward(
            turn, last, loss_scale, (section, arrived, mine), scale_plus, weights, indices,
            teacher_velocity,
        )
    slope, hidden = kept
    cotangent = result
    rows = split_range(owner_count, CHIPS * CORES)
    states = (cotangent,)
    for turn in range(section_count - 1, 0, -1):
        first_turn = turn == section_count - 1
        sent, *moved = section_backward(
            turn, first_turn, states, mine, scale_plus, slope, weights, indices
        )
        if first_turn:
            hidden, sent = lax.optimization_barrier((hidden, sent))
            pieces = hidden_pieces(turn_hidden(hidden), rows, CHIPS)
        else:
            (cotangent,) = moved
        arrived = lax.ppermute(sent, "section", [(turn, turn - 1)])
        states = (section, arrived, cotangent)
    cotangent = jnp.where(section_number == 0, arrived, cotangent)

    return reduce_weight_gradient(pieces, cotangent, down_index, rows, CHIPS)[None]


def solution(mesh):
    in_specs = (
        P("dp", None),
        P("dp", None),
        P("dp", None),
        P("dp"),
        P("section", None, None),
        P("section", "dp", None),
        P("section", None, None),
        P("section", None, None),
        P("section", None, None),
    )
    out_specs = P("section", "dp", None)
    return jax.shard_map(
        per_device, mesh=mesh, in_specs=in_specs, out_specs=out_specs, check_vma=False
    )
```

time: 374 us -> 312 us (0.83)
  waiting for transfers between devices: 203 us -> 170 us
  Pallas kernels: 111 us -> 80.3 us
  other arithmetic: 12.4 us -> 5.65 us
    ppermute x3, waiting for transfers between devices: 51.3 us -> 14.7 us  [reduce_weight_gradient(): part = lax.ppermute(part, 'dp', route)]
    pallas_call x7 -> x8, Pallas kernels: 104 us -> 73.2 us  [the longest x4 39.3 us: section_forward(): pl.pallas_call(body, out_shape=out_shape, in_specs=in_specs, out_specs=[V...]
    select_n x6 -> x1, other arithmetic: 4.04 us -> 0.04 us  [per_device(): cotangent = jnp.where(section_number == 0, arrived, cotangent)]
    ppermute x6 -> x7, waiting for transfers between devices: 28 us -> 27.3 us  [the longest x3 27.3 us: per_device(): arrived = lax.ppermute(result, 'section', [(turn - 1, turn)])]
  transfers between devices with their start and end apart: 21 -> 22, of which waited for: 13 -> 14; matrix products, arithmetic and copies ran while one was open for 3% -> 2% of each run, Pallas kernels for 4% -> 7%
where the time goes in v3:
time: 312 us; the launch traced here: 309 us
  waiting for transfers between devices  170 us (54%)
  Pallas kernels  80.3 us (26%)
  starting transfers between devices  32.1 us (10%)
  between operations  13.8 us (4%)
  local copies, waits for them, and re-layouts  6.93 us (2%)
  other arithmetic  5.65 us (2%)
    all_gather x1, waiting for transfers between devices, per_device(): up_flat = lax.all_gather(up_weight, 'dp', axis=1, tiled=True)[0]  85.7 us
    pallas_call x4, Pallas kernels, section_forward(): pl.pallas_call(body, out_shape=out_shape, in_specs=in_specs, out_specs=[V...  39.3 us
    pallas_call x3, Pallas kernels, section_backward(): pl.pallas_call(body, out_shape=out_shape, in_specs=in_specs, out_specs=[V...  31.7 us
    ppermute x3, waiting for transfers between devices, per_device(): arrived = lax.ppermute(result, 'section', [(turn - 1, turn)])  27.3 us
    ppermute x7, waiting for transfers between devices, reduce_weight_gradient(): got = lax.ppermute(jnp.concatenate([coded, tag], axis=0), 'dp', route)  24 us
    ppermute x3, waiting for transfers between devices, reduce_weight_gradient(): part = lax.ppermute(part, 'dp', route)  14.7 us
    ppermute x3, waiting for transfers between devices, per_device(): arrived = lax.ppermute(sent, 'section', [(turn, turn - 1)])  13.8 us
    ppermute x7, starting transfers between devices, reduce_weight_gradient(): got = lax.ppermute(jnp.concatenate([coded, tag], axis=0), 'dp', route)  11.6 us
  transfers between devices with their start and end apart: 22, of which 14 were waited for; matrix products, arithmetic and copies ran while one was open for 2% of the time, Pallas kernels for 7%

profile of v3, /device:TPU:5, one launch (start us, length us, event | category | flops | bytes accessed | tf_op | source)
XLA Modules:
  0.0 309.1 jit_solution(8367422566850386315)
XLA Ops:
  8.7 1.3 add_convert_fusion.refs_2_.refs_4_
  12.9 85.7 %all-gather.2.cloned.1.call-done = bf16[1,36864,128]{2,1,0:T(8,128)(2,1)} async-done(((bf16[1,576,128]{2,1,0:T(8,128)(2,1)}), bf16[1,36864,128]{2,1,0:T(8,128)(2,1)}) %all-gather.2.cloned.1.call-update) | async-done | bytes 9437200 | tf_op jit(solution)/shard_map/all_gather | solution.py:475
  98.5 13.4 %forward_0.1 = (bf16[128,1536]{1,0:T(8,128)(2,1)S(1)}, bf16[36864,128]{1,0:T(8,128)(2,1)S(1)}, bf16[36864,128]{1,0:T(8,128)(2,1)}) custom-call(s32[288]{0:T(512)S(1)} %reshape_squeeze.5.refs_0_, s32[288]{0:T(512)S(1)} %reshape_squeeze.4.refs_1_, bf16[128,1536]{1,0:T(8,128)(2,1)S(1)} %add_convert_fusion.refs_2_.refs_4_, ...), custom_call_target="tpu_custom_call" | custom-call | flops 2415919104 | bytes 6144 | tf_op jit(solution)/shard_map/forward_0/pallas_call | solution.py:183
  112.6 3.7 %copy-done = bf16[36864,128]{1,0:T(8,128)(2,1)S(1)} copy-done((bf16[36864,128]{1,0:T(8,128)(2,1)S(1)}, bf16[36864,128]{1,0:T(8,128)(2,1)}, u32[]{:S(2)}) %copy-start) | copy-done | bytes 9437208
  116.3 8.6 %forward_1.1 = (bf16[128,1536]{1,0:T(8,128)(2,1)S(1)}, bf16[128,1536]{1,0:T(8,128)(2,1)S(1)}) custom-call(s32[288]{0:T(512)S(1)} %reshape_squeeze.5.refs_0_, s32[288]{0:T(512)S(1)} %reshape_squeeze.4.refs_1_, s32[1]{0:T(128)} %bitcast.3.refs_2_, bf16[128,1536]{1,0:T(8,128)(2,1)S(1)} %collective-permute-done.refs_3_, ...), custom_call_target="tpu_custom_call" | custom-call | flops 2415919104 | bytes 6144 | tf_op jit(solution)/shard_map/forward_1/pallas_call | solution.py:183
  126.1 20.3 %collective-permute-done.1.refs_3_ = bf16[128,1536]{1,0:T(8,128)(2,1)S(1)} collective-permute-done((bf16[128,1536]{1,0:T(8,128)(2,1)S(1)}, bf16[128,1536]{1,0:T(8,128)(2,1)S(1)}, u32[]{:S(2)}, u32[]{:S(2)}) %collective-permute-start.1) | collective-permute-done | bytes 393248 | tf_op jit(solution)/shard_map/ppermute | solution.py:496
  146.5 8.6 %forward_2.1 = (bf16[128,1536]{1,0:T(8,128)(2,1)S(1)}, bf16[128,1536]{1,0:T(8,128)(2,1)S(1)}) custom-call(s32[288]{0:T(512)S(1)} %reshape_squeeze.5.refs_0_, s32[288]{0:T(512)S(1)} %reshape_squeeze.4.refs_1_, s32[1]{0:T(128)} %bitcast.3.refs_2_, bf16[128,1536]{1,0:T(8,128)(2,1)S(1)} %collective-permute-done.1.refs_3_, ...), custom_call_target="tpu_custom_call" | custom-call | flops 2415919104 | bytes 6144 | tf_op jit(solution)/shard_map/forward_2/pallas_call | solution.py:183
  155.0 1.3 collective-permute-start.2
  156.3 7.0 %collective-permute-done.2.refs_3_ = bf16[128,1536]{1,0:T(8,128)(2,1)S(1)} collective-permute-done((bf16[128,1536]{1,0:T(8,128)(2,1)S(1)}, bf16[128,1536]{1,0:T(8,128)(2,1)S(1)}, u32[]{:S(2)}, u32[]{:S(2)}) %collective-permute-start.2) | collective-permute-done | bytes 393248 | tf_op jit(solution)/shard_map/ppermute | solution.py:496
  163.3 8.9 %forward_3.1 = (bf16[128,1536]{1,0:T(8,128)(2,1)S(1)}, bf16[128,1536]{1,0:T(8,128)(2,1)S(1)}, f32[48,128,128]{2,1,0:T(8,128)S(1)}, bf16[48,128,128]{2,1,0:T(8,128)(2,1)S(1)}) custom-call(s32[288]{0:T(512)S(1)} %reshape_squeeze.5.refs_0_, s32[288]{0:T(512)S(1)} %reshape_squeeze.4.refs_1_, s32[1]{0:T(128)} %bitcast.3.refs_2_, ...), custom_call_target="tpu_custom_call" | custom-call | flops 2415919104 | bytes 6144 | tf_op jit(solution)/shard_map/forward_3/pallas_call | solution.py:183
  172.2 10.5 %backward_3.1 = bf16[128,1536]{1,0:T(8,128)(2,1)S(1)} custom-call(s32[288]{0:T(512)S(1)} %reshape_squeeze.5.refs_0_, s32[288]{0:T(512)S(1)} %reshape_squeeze.4.refs_1_, bf16[128,1536]{1,0:T(8,128)(2,1)S(1)} %get-tuple-element.36.refs_2_.refs_4_, bf16[128,1536]{1,0:T(8,128)(2,1)S(1)} %get-tuple-element.37.refs_3_.refs_5_, ...), custom_call_target="tpu_custom_call" | custom-call | flops 1000000 | bytes 100000 | tf_op jit(solution)/shard_map/backward_3/pallas_call | solution.py:274
  182.7 2.3 turn_hidden.1.refs_2_
  187.7 8.7 %collective-permute-done.7.refs_3_ = bf16[128,1536]{1,0:T(8,128)(2,1)S(1)} collective-permute-done((bf16[128,1536]{1,0:T(8,128)(2,1)S(1)}, bf16[128,1536]{1,0:T(8,128)(2,1)S(1)}, u32[]{:S(2)}, u32[]{:S(2)}) %collective-permute-start.7) | collective-permute-done | bytes 393248 | tf_op jit(solution)/shard_map/ppermute | solution.py:515
  196.4 10.6 %backward_2.1 = (bf16[128,1536]{1,0:T(8,128)(2,1)S(1)}, bf16[128,1536]{1,0:T(8,128)(2,1)S(1)}) custom-call(s32[288]{0:T(512)S(1)} %reshape_squeeze.5.refs_0_, s32[288]{0:T(512)S(1)} %reshape_squeeze.4.refs_1_, s32[1]{0:T(128)} %bitcast.3.refs_2_, bf16[128,1536]{1,0:T(8,128)(2,1)S(1)} %collective-permute-done.7.refs_3_, ...), custom_call_target="tpu_custom_call" | custom-call | flops 1000000 | bytes 100000 | tf_op jit(solution)/shard_map/backward_2/pallas_call | solution.py:274
  208.3 5.1 %collective-permute-done.8.refs_3_ = bf16[128,1536]{1,0:T(8,128)(2,1)S(1)} collective-permute-done((bf16[128,1536]{1,0:T(8,128)(2,1)S(1)}, bf16[128,1536]{1,0:T(8,128)(2,1)S(1)}, u32[]{:S(2)}, u32[]{:S(2)}) %collective-permute-start.8) | collective-permute-done | bytes 393248 | tf_op jit(solution)/shard_map/ppermute | solution.py:515
  213.4 10.6 %backward_1.1 = (bf16[128,1536]{1,0:T(8,128)(2,1)S(1)}, bf16[128,1536]{1,0:T(8,128)(2,1)S(1)}) custom-call(s32[288]{0:T(512)S(1)} %reshape_squeeze.5.refs_0_, s32[288]{0:T(512)S(1)} %reshape_squeeze.4.refs_1_, s32[1]{0:T(128)} %bitcast.3.refs_2_, bf16[128,1536]{1,0:T(8,128)(2,1)S(1)} %collective-permute-done.8.refs_3_, ...), custom_call_target="tpu_custom_call" | custom-call | flops 1000000 | bytes 100000 | tf_op jit(solution)/shard_map/backward_1/pallas_call | solution.py:274
  224.8 1.8 collective-permute-start.5
  228.1 2.7 collective-permute-start.10
  232.2 9.7 %collective-permute-done.10 = bf16[128,384]{1,0:T(8,128)(2,1)S(1)} collective-permute-done((bf16[128,384]{1,0:T(8,128)(2,1)S(1)}, bf16[128,384]{1,0:T(8,128)(2,1)S(1)}, u32[]{:S(2)}, u32[]{:S(2)}) %collective-permute-start.10) | collective-permute-done | bytes 98336 | tf_op jit(solution)/shard_map/ppermute | solution.py:428
  241.8 5.0 %collective-permute-done.11 = bf16[128,384]{1,0:T(8,128)(2,1)S(1)} collective-permute-done((bf16[128,384]{1,0:T(8,128)(2,1)S(1)}, bf16[128,384]{1,0:T(8,128)(2,1)S(1)}, u32[]{:S(2)}, u32[]{:S(2)}) %collective-permute-start.11) | collective-permute-done | bytes 98336 | tf_op jit(solution)/shard_map/ppermute | solution.py:428
  246.9 7.0 %weight_gradient.1 = (f32[4616,128]{1,0:T(8,128)S(1)}, f32[4616,128]{1,0:T(8,128)S(1)}) custom-call(s32[3]{0:T(128)S(1)} %pad_add_fusion.refs_0_, s32[288]{0:T(512)S(1)} %reshape_squeeze.4.refs_1_, bf16[48,128,128]{2,1,0:T(8,128)(2,1)} %turn_hidden.1.refs_2_, bf16[48,128,128]{2,1,0:T(8,128)(2,1)S(1)} %collective-permute-done.3.refs_3_, ...), custom_call_target="tpu_custom_call" | custom-call | flops 1207959552 | bytes 7864320 | tf_op jit(solution)/shard_map/weight_gradient/pallas_call | solution.py:368
  254.0 6.5 %collective-permute-start.13 = (f32[4616,128]{1,0:T(8,128)S(1)}, f32[4616,128]{1,0:T(8,128)S(1)}, u32[]{:S(2)}, u32[]{:S(2)}) collective-permute-start(f32[4616,128]{1,0:T(8,128)S(1)} %get-tuple-element.46), channel_id=1, source_target_pairs={{0,1},{1,0},{2,3},{3,2},{4,5},{5,4},{6,7},{7,6},{8,9},{9,8},{10,11... | collective-permute-start | bytes 7090184 | tf_op jit(solution)/shard_map/ppermute | solution.py:434
  260.5 4.2 %collective-permute-done.13 = f32[4616,128]{1,0:T(8,128)S(1)} collective-permute-done((f32[4616,128]{1,0:T(8,128)S(1)}, f32[4616,128]{1,0:T(8,128)S(1)}, u32[]{:S(2)}, u32[]{:S(2)}) %collective-permute-start.13) | collective-permute-done | bytes 2363424 | tf_op jit(solution)/shard_map/ppermute | solution.py:434
  265.5 2.0 collective-permute-start.20
  268.2 2.4 collective-permute-start.18
  270.5 2.6 collective-permute-start.17
  274.3 2.8 collective-permute-start.15
  277.1 3.0 collective-permute-done.19
  280.2 3.1 %collective-permute-done.18 = f16[592,128]{1,0:T(8,128)(2,1)S(1)} collective-permute-done((f16[592,128]{1,0:T(8,128)(2,1)S(1)}, f16[592,128]{1,0:T(8,128)(2,1)S(1)}, u32[]{:S(2)}, u32[]{:S(2)}) %collective-permute-start.18) | collective-permute-done | bytes 151584 | tf_op jit(solution)/shard_map/ppermute | solution.py:444
  284.4 8.3 %collective-permute-done.16 = f16[592,128]{1,0:T(8,128)(2,1)S(1)} collective-permute-done((f16[592,128]{1,0:T(8,128)(2,1)S(1)}, f16[592,128]{1,0:T(8,128)(2,1)S(1)}, u32[]{:S(2)}, u32[]{:S(2)}) %collective-permute-start.16) | collective-permute-done | bytes 151584 | tf_op jit(solution)/shard_map/ppermute | solution.py:444
  292.8 1.4 collective-permute-done.15
  294.3 7.0 %collective-permute-done.14 = f16[592,128]{1,0:T(8,128)(2,1)S(1)} collective-permute-done((f16[592,128]{1,0:T(8,128)(2,1)S(1)}, f16[592,128]{1,0:T(8,128)(2,1)S(1)}, u32[]{:S(2)}, u32[]{:S(2)}) %collective-permute-start.14) | collective-permute-done | bytes 151584 | tf_op jit(solution)/shard_map/ppermute | solution.py:444
  (69 shorter events, 19.3 us)
Async XLA Ops:
  6.5 92.0 %all-gather.2.cloned.1.call-start = ((), (), s32[]{:S(2)}) async-start(), calls=%async_computation | async-start | bytes 9584640 | tf_op jit(solution)/shard_map/all_gather | solution.py:475
  111.9 0.7 collective-permute-start
  112.6 3.7 %copy-start = (bf16[36864,128]{1,0:T(8,128)(2,1)S(1)}, bf16[36864,128]{1,0:T(8,128)(2,1)}, u32[]{:S(2)}) copy-start(bf16[36864,128]{1,0:T(8,128)(2,1)} %get-tuple-element.30.refs_7_.refs_9_) | copy-start | bytes 28311556
  124.8 21.6 %collective-permute-start.1 = (bf16[128,1536]{1,0:T(8,128)(2,1)S(1)}, bf16[128,1536]{1,0:T(8,128)(2,1)S(1)}, u32[]{:S(2)}, u32[]{:S(2)}) collective-permute-start(bf16[128,1536]{1,0:T(8,128)(2,1)S(1)} %get-tuple-element.31), channel_id=1, source_target_pairs={{64,128},{65,129},{66,130},{67,131},{68,132},{69,133},{70,134},{71... | collective-permute-start | bytes 1179656 | tf_op jit(solution)/shard_map/ppermute | solution.py:496
  146.4 16.9 %slice-start = ((s8[9437184]{0:T(1024)(128)(4,1)}), s8[4194304]{0:T(1024)(128)(4,1)S(1)}, s32[]{:S(2)}) async-start(s8[9437184]{0:T(1024)(128)(4,1)} %bitcast.26), calls=%async_computation.1 | async-start | bytes 8388608
  146.4 16.9 %slice-start.1 = ((s8[9437184]{0:T(1024)(128)(4,1)}), s8[4194304]{0:T(1024)(128)(4,1)S(1)}, s32[]{:S(2)}) async-start(s8[9437184]{0:T(1024)(128)(4,1)} %bitcast.26), calls=%async_computation.2 | async-start | bytes 8388608
  146.4 16.9 %slice-start.2 = ((s8[9437184]{0:T(1024)(128)(4,1)}), s8[1048576]{0:T(1024)(128)(4,1)S(1)}, s32[]{:S(2)}) async-start(s8[9437184]{0:T(1024)(128)(4,1)} %bitcast.26), calls=%async_computation.3 | async-start | bytes 2097152
  146.4 16.9 %copy-start.1 = (bf16[128,1536]{1,0:T(8,128)(2,1)S(1)}, bf16[128,1536]{1,0:T(8,128)(2,1)}, u32[]{:S(2)}) copy-start(bf16[128,1536]{1,0:T(8,128)(2,1)} %refs_8_.1) | copy-start | bytes 1179652
  155.0 8.3 %collective-permute-start.2 = (bf16[128,1536]{1,0:T(8,128)(2,1)S(1)}, bf16[128,1536]{1,0:T(8,128)(2,1)S(1)}, u32[]{:S(2)}, u32[]{:S(2)}) collective-permute-start(bf16[128,1536]{1,0:T(8,128)(2,1)S(1)} %get-tuple-element.33), channel_id=1, source_target_pairs={{128,192},{129,193},{130,194},{131,195},{132,196},{133,197},{134,1... | collective-permute-start | bytes 1179656 | tf_op jit(solution)/shard_map/ppermute | solution.py:496
  185.0 39.8 %collective-permute-start.3 = (bf16[48,128,128]{2,1,0:T(8,128)(2,1)}, bf16[48,128,128]{2,1,0:T(8,128)(2,1)S(1)}, u32[]{:S(2)}, u32[]{:S(2)}) collective-permute-start(bf16[48,128,128]{2,1,0:T(8,128)(2,1)} %turn_hidden.1.refs_2_), channel_id=1, source_target_pairs={{0,48},{1,49},{2,50},{3,51},{4,52},{5,53},{6,54},{7,55},{8,56},{9,... | collective-permute-start | bytes 4718600 | tf_op jit(solution)/shard_map/ppermute | solution.py:409
  185.5 41.1 %collective-permute-start.4 = (bf16[48,128,128]{2,1,0:T(8,128)(2,1)}, bf16[48,128,128]{2,1,0:T(8,128)(2,1)}, u32[]{:S(2)}, u32[]{:S(2)}) collective-permute-start(bf16[48,128,128]{2,1,0:T(8,128)(2,1)} %turn_hidden.1.refs_2_), channel_id=1, source_target_pairs={{0,16},{1,17},{2,18},{3,19},{4,20},{5,21},{6,22},{7,23},{8,24},{9,... | collective-permute-start | bytes 4718600 | tf_op jit(solution)/shard_map/ppermute | solution.py:410
  186.5 10.0 %collective-permute-start.7 = (bf16[128,1536]{1,0:T(8,128)(2,1)S(1)}, bf16[128,1536]{1,0:T(8,128)(2,1)S(1)}, u32[]{:S(2)}, u32[]{:S(2)}) collective-permute-start(bf16[128,1536]{1,0:T(8,128)(2,1)S(1)} %backward_3.1), channel_id=1, source_target_pairs={{192,128},{193,129},{194,130},{195,131},{196,132},{197,133},{198,1... | collective-permute-start | bytes 1179656 | tf_op jit(solution)/shard_map/ppermute | solution.py:515
  207.0 6.4 %collective-permute-start.8 = (bf16[128,1536]{1,0:T(8,128)(2,1)S(1)}, bf16[128,1536]{1,0:T(8,128)(2,1)S(1)}, u32[]{:S(2)}, u32[]{:S(2)}) collective-permute-start(bf16[128,1536]{1,0:T(8,128)(2,1)S(1)} %get-tuple-element.41), channel_id=1, source_target_pairs={{128,64},{129,65},{130,66},{131,67},{132,68},{133,69},{134,70},{13... | collective-permute-start | bytes 1179656 | tf_op jit(solution)/shard_map/ppermute | solution.py:515
  224.0 4.0 %collective-permute-start.9 = (bf16[128,1536]{1,0:T(8,128)(2,1)S(1)}, bf16[128,1536]{1,0:T(8,128)(2,1)S(1)}, u32[]{:S(2)}, u32[]{:S(2)}) collective-permute-start(bf16[128,1536]{1,0:T(8,128)(2,1)S(1)} %get-tuple-element.43), channel_id=1, source_target_pairs={{64,0},{65,1},{66,2},{67,3},{68,4},{69,5},{70,6},{71,7},{72,8},{73... | collective-permute-start | bytes 1179656 | tf_op jit(solution)/shard_map/ppermute | solution.py:515
  224.8 22.1 %collective-permute-start.5 = (bf16[24,128,128]{2,1,0:T(8,128)(2,1)S(1)}, bf16[24,128,128]{2,1,0:T(8,128)(2,1)S(1)}, u32[]{:S(2)}, u32[]{:S(2)}) collective-permute-start(bf16[24,128,128]{2,1,0:T(8,128)(2,1)S(1)} %slice.120), channel_id=1, source_target_pairs={{0,48},{1,49},{2,50},{3,51},{4,52},{5,53},{6,54},{7,55},{8,56},{9,... | collective-permute-start | bytes 2359304 | tf_op jit(solution)/shard_map/ppermute | solution.py:411
  227.9 19.1 %collective-permute-start.6 = (bf16[24,128,128]{2,1,0:T(8,128)(2,1)S(1)}, bf16[24,128,128]{2,1,0:T(8,128)(2,1)S(1)}, u32[]{:S(2)}, u32[]{:S(2)}) collective-permute-start(bf16[24,128,128]{2,1,0:T(8,128)(2,1)S(1)} %slice.121), channel_id=1, source_target_pairs={{0,16},{1,17},{2,18},{3,19},{4,20},{5,21},{6,22},{7,23},{8,24},{9,... | collective-permute-start | bytes 2359304 | tf_op jit(solution)/shard_map/ppermute | solution.py:412
  228.1 13.7 %collective-permute-start.10 = (bf16[128,384]{1,0:T(8,128)(2,1)S(1)}, bf16[128,384]{1,0:T(8,128)(2,1)S(1)}, u32[]{:S(2)}, u32[]{:S(2)}) collective-permute-start(bf16[128,384]{1,0:T(8,128)(2,1)S(1)} %get-tuple-element.63), channel_id=1, source_target_pairs={{0,48},{1,49},{2,50},{3,51},{4,52},{5,53},{6,54},{7,55},{8,56},{9,... | collective-permute-start | bytes 294920 | tf_op jit(solution)/shard_map/ppermute | solution.py:428
  230.8 16.1 %collective-permute-start.11 = (bf16[128,384]{1,0:T(8,128)(2,1)S(1)}, bf16[128,384]{1,0:T(8,128)(2,1)S(1)}, u32[]{:S(2)}, u32[]{:S(2)}) collective-permute-start(bf16[128,384]{1,0:T(8,128)(2,1)S(1)} %get-tuple-element.62), channel_id=1, source_target_pairs={{0,16},{1,17},{2,18},{3,19},{4,20},{5,21},{6,22},{7,23},{8,24},{9,... | collective-permute-start | bytes 294920 | tf_op jit(solution)/shard_map/ppermute | solution.py:428
  230.8 16.1 %collective-permute-start.12 = (bf16[128,384]{1,0:T(8,128)(2,1)S(1)}, bf16[128,384]{1,0:T(8,128)(2,1)S(1)}, u32[]{:S(2)}, u32[]{:S(2)}) collective-permute-start(bf16[128,384]{1,0:T(8,128)(2,1)S(1)} %get-tuple-element.61), channel_id=1, source_target_pairs={{0,32},{1,33},{2,34},{3,35},{4,36},{5,37},{6,38},{7,39},{8,40},{9,... | collective-permute-start | bytes 294920 | tf_op jit(solution)/shard_map/ppermute | solution.py:428
  254.0 10.7 %collective-permute-start.13 = (f32[4616,128]{1,0:T(8,128)S(1)}, f32[4616,128]{1,0:T(8,128)S(1)}, u32[]{:S(2)}, u32[]{:S(2)}) collective-permute-start(f32[4616,128]{1,0:T(8,128)S(1)} %get-tuple-element.46), channel_id=1, source_target_pairs={{0,1},{1,0},{2,3},{3,2},{4,5},{5,4},{6,7},{7,6},{8,9},{9,8},{10,11... | collective-permute-start | bytes 7090184 | tf_op jit(solution)/shard_map/ppermute | solution.py:434
  265.5 8.8 %collective-permute-start.20 = (f16[592,128]{1,0:T(8,128)(2,1)S(1)}, f16[592,128]{1,0:T(8,128)(2,1)S(1)}, u32[]{:S(2)}, u32[]{:S(2)}) collective-permute-start(f16[592,128]{1,0:T(8,128)(2,1)S(1)} %get-tuple-element.70), channel_id=1, source_target_pairs={{0,14},{1,15},{2,0},{3,1},{4,2},{5,3},{6,4},{7,5},{8,6},{9,7},{10,... | collective-permute-start | bytes 454664 | tf_op jit(solution)/shard_map/ppermute | solution.py:444
  267.4 12.7 %collective-permute-start.19 = (f16[592,128]{1,0:T(8,128)(2,1)S(1)}, f16[592,128]{1,0:T(8,128)(2,1)S(1)}, u32[]{:S(2)}, u32[]{:S(2)}) collective-permute-start(f16[592,128]{1,0:T(8,128)(2,1)S(1)} %get-tuple-element.69), channel_id=1, source_target_pairs={{0,12},{1,13},{2,14},{3,15},{4,0},{5,1},{6,2},{7,3},{8,4},{9,5},{1... | collective-permute-start | bytes 454664 | tf_op jit(solution)/shard_map/ppermute | solution.py:444
  268.2 15.2 %collective-permute-start.18 = (f16[592,128]{1,0:T(8,128)(2,1)S(1)}, f16[592,128]{1,0:T(8,128)(2,1)S(1)}, u32[]{:S(2)}, u32[]{:S(2)}) collective-permute-start(f16[592,128]{1,0:T(8,128)(2,1)S(1)} %get-tuple-element.68), channel_id=1, source_target_pairs={{0,10},{1,11},{2,12},{3,13},{4,14},{5,15},{6,0},{7,1},{8,2},{9,3},... | collective-permute-start | bytes 454664 | tf_op jit(solution)/shard_map/ppermute | solution.py:444
  270.5 13.8 %collective-permute-start.17 = (f16[592,128]{1,0:T(8,128)(2,1)S(1)}, f16[592,128]{1,0:T(8,128)(2,1)S(1)}, u32[]{:S(2)}, u32[]{:S(2)}) collective-permute-start(f16[592,128]{1,0:T(8,128)(2,1)S(1)} %get-tuple-element.67), channel_id=1, source_target_pairs={{0,8},{1,9},{2,10},{3,11},{4,12},{5,13},{6,14},{7,15},{8,0},{9,1},... | collective-permute-start | bytes 454664 | tf_op jit(solution)/shard_map/ppermute | solution.py:444
  273.1 19.7 %collective-permute-start.16 = (f16[592,128]{1,0:T(8,128)(2,1)S(1)}, f16[592,128]{1,0:T(8,128)(2,1)S(1)}, u32[]{:S(2)}, u32[]{:S(2)}) collective-permute-start(f16[592,128]{1,0:T(8,128)(2,1)S(1)} %get-tuple-element.66), channel_id=1, source_target_pairs={{0,6},{1,7},{2,8},{3,9},{4,10},{5,11},{6,12},{7,13},{8,14},{9,15},... | collective-permute-start | bytes 454664 | tf_op jit(solution)/shard_map/ppermute | solution.py:444
  274.3 20.0 %collective-permute-start.15 = (f16[592,128]{1,0:T(8,128)(2,1)S(1)}, f16[592,128]{1,0:T(8,128)(2,1)S(1)}, u32[]{:S(2)}, u32[]{:S(2)}) collective-permute-start(f16[592,128]{1,0:T(8,128)(2,1)S(1)} %get-tuple-element.65), channel_id=1, source_target_pairs={{0,4},{1,5},{2,6},{3,7},{4,8},{5,9},{6,10},{7,11},{8,12},{9,13},{1... | collective-permute-start | bytes 454664 | tf_op jit(solution)/shard_map/ppermute | solution.py:444
  280.1 21.1 %collective-permute-start.14 = (f16[592,128]{1,0:T(8,128)(2,1)S(1)}, f16[592,128]{1,0:T(8,128)(2,1)S(1)}, u32[]{:S(2)}, u32[]{:S(2)}) collective-permute-start(f16[592,128]{1,0:T(8,128)(2,1)S(1)} %get-tuple-element.64), channel_id=1, source_target_pairs={{0,2},{1,3},{2,4},{3,5},{4,6},{5,7},{6,8},{7,9},{8,10},{9,11},{10,... | collective-permute-start | bytes 454664 | tf_op jit(solution)/shard_map/ppermute | solution.py:444
Sparse Core Ops, SparseCore 0:
  10.1 88.3 all-gather.1

commit v4 on v3

--- a/solution.py
+++ b/solution.py
@@ -68,7 +68,7 @@
         pick(section[0] == turn, arrived_ref, held_ref, x_ref)
     copies = []
     if last:
-        slope_ref, hidden, normed = refs
+        slope_ref, turned_ref, normed, hidden = refs
     elif turn:
         normed, hidden = refs
     else:
@@ -80,8 +80,9 @@
                 copy = pltpu.make_async_copy(
                     source.at[span, :], target.at[span, :], arrival.at[len(copies)]
                 )
-                copy.start()
                 copies.append(copy)
+        for copy in copies[:PARTS]:
+            copy.start()
         uw_ref, dw_ref = uw_to, dw_to
     size = normed.shape[-1]
     width_blocks = normed.shape[0]
@@ -104,9 +105,11 @@
             first = pl.multiple_of(c * rows, rows)
             pre = jnp.dot(left, uw_ref[pl.ds(first, rows), :], preferred_element_type=F32)
             act, slope = gelu_parts(pre)
-            hidden[c] = act.astype(BF16)
+            act = act.astype(BF16)
+            hidden[c] = act
             if last:
                 slope_ref[c] = slope
+                turned_ref[c] = act.T
         return carry
 
     group = 4
@@ -138,6 +141,8 @@
             per = split_range(count, PARTS)
             for p, copy in enumerate(waits):
                 copy.wait()
+                if step_of is up_step:
+                    copies[PARTS + p].start()
                 lax.fori_loop(p * per, (p + 1) * per, step_of, 0)
         else:
             lax.fori_loop(0, count, step_of, 0)
@@ -170,9 +175,9 @@
     if turn:
         out_shape.append(stream)
     if last:
-        out_shape += [jax.ShapeDtypeStruct(hidden, F32), jax.ShapeDtypeStruct(hidden, BF16)]
-    else:
-        scratch.append(pltpu.VMEM(hidden, BF16))
+        turned = (hidden_blocks, size, rows)
+        out_shape += [jax.ShapeDtypeStruct(hidden, F32), jax.ShapeDtypeStruct(turned, BF16)]
+    scratch.append(pltpu.VMEM(hidden, BF16))
     if not turn:
         out_shape += [jax.ShapeDtypeStruct(w.shape, w.dtype) for w in weights]
         scratch.append(pltpu.SemaphoreType.DMA((2 * PARTS,)))
@@ -186,7 +191,7 @@
         in_specs=in_specs,
         out_specs=[VMEM] * len(out_shape),
         scratch_shapes=scratch,
-        compiler_params=pltpu.CompilerParams(vmem_limit_bytes=LIMIT if turn else 40 << 20),
+        compiler_params=pltpu.CompilerParams(vmem_limit_bytes=LIMIT if turn else 31 << 20),
         cost_estimate=pl.CostEstimate(
             flops=4 * rows * weights[0].size, bytes_accessed=4 * features, transcendentals=0
         ),
@@ -281,37 +286,44 @@
             pltpu.VMEM((width_blocks, rows, size), F32),
         ],
         compiler_params=pltpu.CompilerParams(vmem_limit_bytes=LIMIT),
-        cost_estimate=pl.CostEstimate(flops=1000000, bytes_accessed=100000, transcendentals=0),
+        cost_estimate=pl.CostEstimate(
+            flops=30000000000 if turn == 1 else 1000000, bytes_accessed=100000, transcendentals=0
+        ),
         name=f"backward_{turn}",
     )(*[index.reshape(-1) for index in indices], *states, stream, scale_plus, slope, *weights)
 
 
-def turn_kernel(source_ref, out_ref):
+def join_kernel(own_ref, after_ref, before_ref, low_ref, high_ref, out_ref):
+    rows = own_ref.shape[-1]
+    half = low_ref.shape[0]
+
     def step(h, carry):
-        for i in range(4):
-            out_ref[h * 4 + i] = source_ref[h * 4 + i].T
+        for first, far_ref in ((0, low_ref), (half, high_ref)):
+            at = first + h
+            for i, piece in enumerate((own_ref[at], after_ref[at], before_ref[at], far_ref[h])):
+                out_ref[at, :, i * rows : (i + 1) * rows] = piece
         return carry
 
-    lax.fori_loop(0, source_ref.shape[0] // 4, step, 0)
-
-
-def turn_hidden(hidden):
-    blocks, rows, size = hidden.shape
+    lax.fori_loop(0, half, step, 0)
+
+
+def join_pieces(pieces):
+    blocks, size, rows = pieces[0].shape
     return pl.pallas_call(
-        turn_kernel,
-        out_shape=jax.ShapeDtypeStruct((blocks, size, rows), hidden.dtype),
-        in_specs=[VMEM],
+        join_kernel,
+        out_shape=jax.ShapeDtypeStruct((blocks, size, ROWS * rows), pieces[0].dtype),
+        in_specs=[VMEM] * len(pieces),
         out_specs=VMEM,
         compiler_params=pltpu.CompilerParams(vmem_limit_bytes=LIMIT),
         cost_estimate=pl.CostEstimate(
-            flops=20000 * hidden.size, bytes_accessed=4 * hidden.size, transcendentals=0
+            flops=1000000, bytes_accessed=8 * pieces[0].size, transcendentals=0
         ),
-        name="turn_hidden",
-    )(hidden)
+        name="join_pieces",
+    )(*pieces)
 
 
 def weight_kernel(keep_down, columns, place, down_index, *refs):
-    pieces, (cot_ref, keep_ref, give_ref, block_sum, largest) = refs[:-5], refs[-5:]
+    joined_ref, cot_ref, keep_ref, give_ref, block_sum, largest = refs
     size = cot_ref.shape[1] // columns
     chunk = block_sum.shape[0] // CORES
     blocks = block_sum.shape[0] // size
@@ -329,13 +341,7 @@
         b = owner * blocks + g
         e = lax.div(b, keep_down) - y * columns
         h = down_index[b]
-        near, low, high = pieces[:-2], pieces[-2], pieces[-1]
-        half = low.shape[0]
-        far_piece = jnp.where(
-            h < half, low[jnp.minimum(h, half - 1)], high[jnp.maximum(h - half, 0)]
-        )
-        left = jnp.concatenate([piece[h] for piece in near] + [far_piece], axis=1)
-        term = jnp.dot(left, cot_ref[:, lane_block(e, size)], preferred_element_type=F32)
+        term = jnp.dot(joined_ref[h], cot_ref[:, lane_block(e, size)], preferred_element_type=F32)
         block_sum[g * size : (g + 1) * size, :] = term
         top = jnp.maximum(top, jnp.max(jnp.abs(term).reshape(-1, 8, size), axis=0))
     largest[...] = top
@@ -350,8 +356,8 @@
         give_ref[chips * chunk :, :] = peak
 
 
-def weight_gradient(pieces, cot, down_index, place, chips, owners):
-    size = pieces[0].shape[1]
+def weight_gradient(joined, cot, down_index, place, chips, owners):
+    size = joined.shape[1]
     width_blocks, keep_down = down_index.shape
     columns = cot.shape[1] // size
     total_rows = width_blocks * keep_down * size
@@ -360,10 +366,6 @@
     def body(*refs):
         weight_kernel(keep_down, columns, *refs)
 
-    held = [
-        pl.BlockSpec(piece.shape, lambda i, *_: (0, 0, 0), pipeline_mode=pl.Buffered(1))
-        for piece in pieces
-    ]
     shape = jax.ShapeDtypeStruct((chips * chunk + 8, size), F32)
     return pl.pallas_call(
         body,
@@ -371,7 +373,10 @@
         grid_spec=pltpu.PrefetchScalarGridSpec(
             num_scalar_prefetch=2,
             grid=(chips,),
-            in_specs=held + [pl.BlockSpec(cot.shape, whole)],
+            in_specs=[
+                pl.BlockSpec(joined.shape, lambda i, *_: (0, 0, 0), pipeline_mode=pl.Buffered(1)),
+                pl.BlockSpec(cot.shape, whole),
+            ],
             out_specs=[pl.BlockSpec(shape.shape, whole)] * 2,
             scratch_shapes=[
                 pltpu.VMEM((CORES * chunk, size), F32),
@@ -383,11 +388,11 @@
         ),
         cost_estimate=pl.CostEstimate(
             flops=2 * cot.shape[0] * chips * CORES * chunk * size,
-            bytes_accessed=2 * len(pieces) * pieces[0].size,
+            bytes_accessed=2 * joined.size,
             transcendentals=0,
         ),
         name="weight_gradient",
-    )(place, down_index.reshape(-1), *pieces, cot)
+    )(place, down_index.reshape(-1), joined, cot)
 
 
 def dp_route(rows, chips, move):
@@ -413,7 +418,7 @@
     return [turned, after, before, low, high]
 
 
-def reduce_weight_gradient(pieces, cot, down_index, rows, chips):
+def reduce_weight_gradient(joined, cot, down_index, rows, chips):
     owners = rows * chips * CORES
     number = lax.axis_index("dp")
     y = lax.div(number, chips * CORES)
@@ -428,7 +433,7 @@
             part = lax.ppermute(part, "dp", route)
         received.append(part)
     keep, give = weight_gradient(
-        pieces, jnp.concatenate(received, axis=0), down_index, place, chips, owners
+        joined, jnp.concatenate(received, axis=0), down_index, place, chips, owners
     )
     swap = dp_route(rows, chips, lambda y, z, core: (y, z, core + 1))
     total = keep + lax.ppermute(give, "dp", swap)
@@ -498,25 +503,24 @@
             turn, last, loss_scale, (section, arrived, mine), scale_plus, weights, indices,
             teacher_velocity,
         )
-    slope, hidden = kept
+    slope, turned = kept
     cotangent = result
     rows = split_range(owner_count, CHIPS * CORES)
+    pieces = hidden_pieces(turned, rows, CHIPS)
     states = (cotangent,)
     for turn in range(section_count - 1, 0, -1):
         first_turn = turn == section_count - 1
         sent, *moved = section_backward(
             turn, first_turn, states, mine, scale_plus, slope, weights, indices
         )
-        if first_turn:
-            hidden, sent = lax.optimization_barrier((hidden, sent))
-            pieces = hidden_pieces(turn_hidden(hidden), rows, CHIPS)
-        else:
+        if not first_turn:
             (cotangent,) = moved
         arrived = lax.ppermute(sent, "section", [(turn, turn - 1)])
         states = (section, arrived, cotangent)
+    joined, arrived = lax.optimization_barrier((join_pieces(pieces), arrived))
     cotangent = jnp.where(section_number == 0, arrived, cotangent)
 
-    return reduce_weight_gradient(pieces, cotangent, down_index, rows, CHIPS)[None]
+    return reduce_weight_gradient(joined, cotangent, down_index, rows, CHIPS)[None]
 
 
 def solution(mesh):

time: 312 us -> 295 us (0.946)
  waiting for transfers between devices: 170 us -> 160 us
  Pallas kernels: 80.3 us -> 76.4 us
    ppermute x3, waiting for transfers between devices: 14.7 us -> 4.89 us  [reduce_weight_gradient(): part = lax.ppermute(part, 'dp', route)]
    ppermute x3, waiting for transfers between devices: 13.8 us -> 9.8 us  [per_device(): arrived = lax.ppermute(sent, 'section', [(turn, turn - 1)])]
    ppermute x1, waiting for transfers between devices: 0.01 us -> 3.28 us  [hidden_pieces(): high = lax.ppermute(before[half:], 'dp', up)]
  transfers between devices with their start and end apart: 22 -> 22, of which waited for: 14 -> 15; matrix products, arithmetic and copies ran while one was open for 2% -> 3% of each run, Pallas kernels for 7% -> 12%
where the time goes in v4:
time: 295 us; the launch traced here: 292 us
  waiting for transfers between devices  160 us (54%)
  Pallas kernels  76.4 us (26%)
  starting transfers between devices  29.9 us (10%)
  between operations  13.8 us (5%)
  local copies, waits for them, and re-layouts  6.79 us (2%)
  other arithmetic  5.65 us (2%)
    all_gather x1, waiting for transfers between devices, per_device(): up_flat = lax.all_gather(up_weight, 'dp', axis=1, tiled=True)[0]  85.7 us
    pallas_call x4, Pallas kernels, section_forward(): pl.pallas_call(body, out_shape=out_shape, in_specs=in_specs, out_specs=[V...  36.6 us
    pallas_call x3, Pallas kernels, section_backward(): pl.pallas_call(body, out_shape=out_shape, in_specs=in_specs, out_specs=[V...  32.5 us
    ppermute x3, waiting for transfers between devices, per_device(): arrived = lax.ppermute(result, 'section', [(turn - 1, turn)])  27.3 us
    ppermute x7, waiting for transfers between devices, reduce_weight_gradient(): got = lax.ppermute(jnp.concatenate([coded, tag], axis=0), 'dp', route)  23.9 us
    ppermute x7, starting transfers between devices, reduce_weight_gradient(): got = lax.ppermute(jnp.concatenate([coded, tag], axis=0), 'dp', route)  11.8 us
    ppermute x3, waiting for transfers between devices, per_device(): arrived = lax.ppermute(sent, 'section', [(turn, turn - 1)])  9.8 us
    ppermute x1, starting transfers between devices, reduce_weight_gradient(): total = keep + lax.ppermute(give, 'dp', swap)  6.67 us
  transfers between devices with their start and end apart: 22, of which 15 were waited for; matrix products, arithmetic and copies ran while one was open for 3% of the time, Pallas kernels for 12%

profile of v4, /device:TPU:5, one launch (start us, length us, event | category | flops | bytes accessed | tf_op | source)
XLA Modules:
  0.0 292.2 jit_solution(2789176501047544069)
XLA Ops:
  8.7 1.3 add_convert_fusion.refs_2_.refs_4_
  12.9 85.7 %all-gather.2.cloned.1.call-done = bf16[1,36864,128]{2,1,0:T(8,128)(2,1)} async-done(((bf16[1,576,128]{2,1,0:T(8,128)(2,1)}), bf16[1,36864,128]{2,1,0:T(8,128)(2,1)}) %all-gather.2.cloned.1.call-update) | async-done | bytes 9437200 | tf_op jit(solution)/shard_map/all_gather | solution.py:480
  98.5 10.1 %forward_0.1 = (bf16[128,1536]{1,0:T(8,128)(2,1)S(1)}, bf16[36864,128]{1,0:T(8,128)(2,1)S(1)}, bf16[36864,128]{1,0:T(8,128)(2,1)S(1)}) custom-call(s32[288]{0:T(512)S(1)} %reshape_squeeze.5.refs_0_, s32[288]{0:T(512)S(1)} %reshape_squeeze.4.refs_1_, bf16[128,1536]{1,0:T(8,128)(2,1)S(1)} %add_convert_fusion.refs_2_.refs_4_, ...), custom_call_target="tpu_custom_call" | custom-call | flops 2415919104 | bytes 6144 | tf_op jit(solution)/shard_map/forward_0/pallas_call | solution.py:188
  109.3 8.6 %forward_1.1 = (bf16[128,1536]{1,0:T(8,128)(2,1)S(1)}, bf16[128,1536]{1,0:T(8,128)(2,1)S(1)}) custom-call(s32[288]{0:T(512)S(1)} %reshape_squeeze.5.refs_0_, s32[288]{0:T(512)S(1)} %reshape_squeeze.4.refs_1_, s32[1]{0:T(128)} %bitcast.3.refs_2_, bf16[128,1536]{1,0:T(8,128)(2,1)S(1)} %collective-permute-done.refs_3_, ...), custom_call_target="tpu_custom_call" | custom-call | flops 2415919104 | bytes 6144 | tf_op jit(solution)/shard_map/forward_1/pallas_call | solution.py:188
  119.2 20.3 %collective-permute-done.1.refs_3_ = bf16[128,1536]{1,0:T(8,128)(2,1)S(1)} collective-permute-done((bf16[128,1536]{1,0:T(8,128)(2,1)S(1)}, bf16[128,1536]{1,0:T(8,128)(2,1)S(1)}, u32[]{:S(2)}, u32[]{:S(2)}) %collective-permute-start.1) | collective-permute-done | bytes 393248 | tf_op jit(solution)/shard_map/ppermute | solution.py:501
  139.5 8.6 %forward_2.1 = (bf16[128,1536]{1,0:T(8,128)(2,1)S(1)}, bf16[128,1536]{1,0:T(8,128)(2,1)S(1)}) custom-call(s32[288]{0:T(512)S(1)} %reshape_squeeze.5.refs_0_, s32[288]{0:T(512)S(1)} %reshape_squeeze.4.refs_1_, s32[1]{0:T(128)} %bitcast.3.refs_2_, bf16[128,1536]{1,0:T(8,128)(2,1)S(1)} %collective-permute-done.1.refs_3_, ...), custom_call_target="tpu_custom_call" | custom-call | flops 2415919104 | bytes 6144 | tf_op jit(solution)/shard_map/forward_2/pallas_call | solution.py:188
  149.4 7.0 %collective-permute-done.2.refs_3_ = bf16[128,1536]{1,0:T(8,128)(2,1)S(1)} collective-permute-done((bf16[128,1536]{1,0:T(8,128)(2,1)S(1)}, bf16[128,1536]{1,0:T(8,128)(2,1)S(1)}, u32[]{:S(2)}, u32[]{:S(2)}) %collective-permute-start.2) | collective-permute-done | bytes 393248 | tf_op jit(solution)/shard_map/ppermute | solution.py:501
  156.3 9.4 %forward_3.1 = (bf16[128,1536]{1,0:T(8,128)(2,1)S(1)}, bf16[128,1536]{1,0:T(8,128)(2,1)S(1)}, f32[48,128,128]{2,1,0:T(8,128)S(1)}, bf16[48,128,128]{2,1,0:T(8,128)(2,1)S(1)}) custom-call(s32[288]{0:T(512)S(1)} %reshape_squeeze.5.refs_0_, s32[288]{0:T(512)S(1)} %reshape_squeeze.4.refs_1_, s32[1]{0:T(128)} %bitcast.3.refs_2_, ...), custom_call_target="tpu_custom_call" | custom-call | flops 2415919104 | bytes 6144 | tf_op jit(solution)/shard_map/forward_3/pallas_call | solution.py:188
  167.3 10.6 %backward_3.1 = bf16[128,1536]{1,0:T(8,128)(2,1)S(1)} custom-call(s32[288]{0:T(512)S(1)} %reshape_squeeze.5.refs_0_, s32[288]{0:T(512)S(1)} %reshape_squeeze.4.refs_1_, bf16[128,1536]{1,0:T(8,128)(2,1)S(1)} %get-tuple-element.36.refs_2_.refs_4_, bf16[128,1536]{1,0:T(8,128)(2,1)S(1)} %get-tuple-element.37.refs_3_.refs_5_, ...), custom_call_target="tpu_custom_call" | custom-call | flops 1000000 | bytes 100000 | tf_op jit(solution)/shard_map/backward_3/pallas_call | solution.py:279
  179.2 8.6 %collective-permute-done.7.refs_3_ = bf16[128,1536]{1,0:T(8,128)(2,1)S(1)} collective-permute-done((bf16[128,1536]{1,0:T(8,128)(2,1)S(1)}, bf16[128,1536]{1,0:T(8,128)(2,1)S(1)}, u32[]{:S(2)}, u32[]{:S(2)}) %collective-permute-start.7) | collective-permute-done | bytes 393248 | tf_op jit(solution)/shard_map/ppermute | solution.py:518
  187.8 10.6 %backward_2.1 = (bf16[128,1536]{1,0:T(8,128)(2,1)S(1)}, bf16[128,1536]{1,0:T(8,128)(2,1)S(1)}) custom-call(s32[288]{0:T(512)S(1)} %reshape_squeeze.5.refs_0_, s32[288]{0:T(512)S(1)} %reshape_squeeze.4.refs_1_, s32[1]{0:T(128)} %bitcast.3.refs_2_, bf16[128,1536]{1,0:T(8,128)(2,1)S(1)} %collective-permute-done.7.refs_3_, ...), custom_call_target="tpu_custom_call" | custom-call | flops 1000000 | bytes 100000 | tf_op jit(solution)/shard_map/backward_2/pallas_call | solution.py:279
  200.7 1.8 collective-permute-start.5
  204.7 11.3 %backward_1.1 = (bf16[128,1536]{1,0:T(8,128)(2,1)}, bf16[128,1536]{1,0:T(8,128)(2,1)S(1)}) custom-call(s32[288]{0:T(512)S(1)} %reshape_squeeze.5.refs_0_, s32[288]{0:T(512)S(1)} %reshape_squeeze.4.refs_1_, s32[1]{0:T(128)} %bitcast.3.refs_2_, bf16[128,1536]{1,0:T(8,128)(2,1)S(1)} %collective-permute-done.8.refs_3_, ...), custom_call_target="tpu_custom_call" | custom-call | flops 30000001024 | bytes 100000 | tf_op jit(solution)/shard_map/backward_1/pallas_call | solution.py:279
  216.8 3.3 %collective-permute-done.6.high_ref = bf16[24,128,128]{2,1,0:T(8,128)(2,1)} collective-permute-done((bf16[24,128,128]{2,1,0:T(8,128)(2,1)}, bf16[24,128,128]{2,1,0:T(8,128)(2,1)}, u32[]{:S(2)}, u32[]{:S(2)}) %collective-permute-start.6) | collective-permute-done | bytes 786464 | tf_op jit(solution)/shard_map/ppermute | solution.py:417
  220.1 1.4 copy-done.1
  221.5 1.4 copy-done.3
  222.9 2.4 join_pieces.1.refs_2_
  225.4 1.5 collective-permute-start.11
  227.0 1.9 collective-permute-done.10
  230.2 1.7 collective-permute-done.12
  231.9 4.9 %weight_gradient.1 = (f32[4616,128]{1,0:T(8,128)S(1)}, f32[4616,128]{1,0:T(8,128)S(1)}) custom-call(s32[3]{0:T(128)S(1)} %pad_add_fusion.refs_0_, s32[288]{0:T(512)S(1)} %reshape_squeeze.4.refs_1_, bf16[48,128,512]{2,1,0:T(8,128)(2,1)S(1)} %join_pieces.1.refs_2_, bf16[512,384]{1,0:T(8,128)(2,1)S(1)} %pad_maximum_fusion.7.refs_3_), custom_call_target="tpu_custom_call" | custom-call | flops 1207959552 | bytes 6291456 | tf_op jit(solution)/shard_map/weight_gradient/pallas_call | solution.py:370
  236.9 6.7 %collective-permute-start.13 = (f32[4616,128]{1,0:T(8,128)S(1)}, f32[4616,128]{1,0:T(8,128)S(1)}, u32[]{:S(2)}, u32[]{:S(2)}) collective-permute-start(f32[4616,128]{1,0:T(8,128)S(1)} %get-tuple-element.46), channel_id=1, source_target_pairs={{0,1},{1,0},{2,3},{3,2},{4,5},{5,4},{6,7},{7,6},{8,9},{9,8},{10,11... | collective-permute-start | bytes 7090184 | tf_op jit(solution)/shard_map/ppermute | solution.py:439
  243.5 4.2 %collective-permute-done.13 = f32[4616,128]{1,0:T(8,128)S(1)} collective-permute-done((f32[4616,128]{1,0:T(8,128)S(1)}, f32[4616,128]{1,0:T(8,128)S(1)}, u32[]{:S(2)}, u32[]{:S(2)}) %collective-permute-start.13) | collective-permute-done | bytes 2363424 | tf_op jit(solution)/shard_map/ppermute | solution.py:439
  248.5 2.2 collective-permute-start.20
  251.4 2.2 collective-permute-start.18
  253.6 2.6 collective-permute-start.17
  256.1 1.4 collective-permute-start.16
  257.5 2.8 collective-permute-start.15
  260.4 3.0 %collective-permute-done.19 = f16[592,128]{1,0:T(8,128)(2,1)S(1)} collective-permute-done((f16[592,128]{1,0:T(8,128)(2,1)S(1)}, f16[592,128]{1,0:T(8,128)(2,1)S(1)}, u32[]{:S(2)}, u32[]{:S(2)}) %collective-permute-start.19) | collective-permute-done | bytes 151584 | tf_op jit(solution)/shard_map/ppermute | solution.py:449
  263.4 3.1 %collective-permute-done.18 = f16[592,128]{1,0:T(8,128)(2,1)S(1)} collective-permute-done((f16[592,128]{1,0:T(8,128)(2,1)S(1)}, f16[592,128]{1,0:T(8,128)(2,1)S(1)}, u32[]{:S(2)}, u32[]{:S(2)}) %collective-permute-start.18) | collective-permute-done | bytes 151584 | tf_op jit(solution)/shard_map/ppermute | solution.py:449
  266.6 9.6 %collective-permute-done.16 = f16[592,128]{1,0:T(8,128)(2,1)S(1)} collective-permute-done((f16[592,128]{1,0:T(8,128)(2,1)S(1)}, f16[592,128]{1,0:T(8,128)(2,1)S(1)}, u32[]{:S(2)}, u32[]{:S(2)}) %collective-permute-start.16) | collective-permute-done | bytes 151584 | tf_op jit(solution)/shard_map/ppermute | solution.py:449
  277.4 7.0 %collective-permute-done.14 = f16[592,128]{1,0:T(8,128)(2,1)S(1)} collective-permute-done((f16[592,128]{1,0:T(8,128)(2,1)S(1)}, f16[592,128]{1,0:T(8,128)(2,1)S(1)}, u32[]{:S(2)}, u32[]{:S(2)}) %collective-permute-start.14) | collective-permute-done | bytes 151584 | tf_op jit(solution)/shard_map/ppermute | solution.py:449
  (68 shorter events, 21.6 us)
Async XLA Ops:
  6.5 92.0 %all-gather.2.cloned.1.call-start = ((), (), s32[]{:S(2)}) async-start(), calls=%async_computation | async-start | bytes 9584640 | tf_op jit(solution)/shard_map/all_gather | solution.py:480
  108.6 0.7 collective-permute-start
  117.9 21.6 %collective-permute-start.1 = (bf16[128,1536]{1,0:T(8,128)(2,1)S(1)}, bf16[128,1536]{1,0:T(8,128)(2,1)S(1)}, u32[]{:S(2)}, u32[]{:S(2)}) collective-permute-start(bf16[128,1536]{1,0:T(8,128)(2,1)S(1)} %get-tuple-element.31), channel_id=1, source_target_pairs={{64,128},{65,129},{66,130},{67,131},{68,132},{69,133},{70,134},{71... | collective-permute-start | bytes 1179656 | tf_op jit(solution)/shard_map/ppermute | solution.py:501
  139.5 16.9 %copy-start.4 = (bf16[128,1536]{1,0:T(8,128)(2,1)S(1)}, bf16[128,1536]{1,0:T(8,128)(2,1)}, u32[]{:S(2)}) copy-start(bf16[128,1536]{1,0:T(8,128)(2,1)} %refs_8_.1) | copy-start | bytes 1179652
  148.0 8.3 %collective-permute-start.2 = (bf16[128,1536]{1,0:T(8,128)(2,1)S(1)}, bf16[128,1536]{1,0:T(8,128)(2,1)S(1)}, u32[]{:S(2)}, u32[]{:S(2)}) collective-permute-start(bf16[128,1536]{1,0:T(8,128)(2,1)S(1)} %get-tuple-element.33), channel_id=1, source_target_pairs={{128,192},{129,193},{130,194},{131,195},{132,196},{133,197},{134,1... | collective-permute-start | bytes 1179656 | tf_op jit(solution)/shard_map/ppermute | solution.py:501
  165.8 12.1 %copy-start.2 = (bf16[48,128,128]{2,1,0:T(8,128)(2,1)}, bf16[48,128,128]{2,1,0:T(8,128)(2,1)S(1)}, u32[]{:S(2)}) copy-start(bf16[48,128,128]{2,1,0:T(8,128)(2,1)S(1)} %get-tuple-element.35.own_ref) | copy-start | bytes 4718596
  165.8 33.9 %collective-permute-start.3 = (bf16[48,128,128]{2,1,0:T(8,128)(2,1)S(1)}, bf16[48,128,128]{2,1,0:T(8,128)(2,1)S(1)}, u32[]{:S(2)}, u32[]{:S(2)}) collective-permute-start(bf16[48,128,128]{2,1,0:T(8,128)(2,1)S(1)} %get-tuple-element.35.own_ref), channel_id=1, source_target_pairs={{0,48},{1,49},{2,50},{3,51},{4,52},{5,53},{6,54},{7,55},{8,56},{9,... | collective-permute-start | bytes 4718600 | tf_op jit(solution)/shard_map/ppermute | solution.py:414
  166.4 36.0 %collective-permute-start.4 = (bf16[48,128,128]{2,1,0:T(8,128)(2,1)S(1)}, bf16[48,128,128]{2,1,0:T(8,128)(2,1)S(1)}, u32[]{:S(2)}, u32[]{:S(2)}) collective-permute-start(bf16[48,128,128]{2,1,0:T(8,128)(2,1)S(1)} %get-tuple-element.35.own_ref), channel_id=1, source_target_pairs={{0,16},{1,17},{2,18},{3,19},{4,20},{5,21},{6,22},{7,23},{8,24},{9,... | collective-permute-start | bytes 4718600 | tf_op jit(solution)/shard_map/ppermute | solution.py:415
  177.9 9.9 %collective-permute-start.7 = (bf16[128,1536]{1,0:T(8,128)(2,1)S(1)}, bf16[128,1536]{1,0:T(8,128)(2,1)S(1)}, u32[]{:S(2)}, u32[]{:S(2)}) collective-permute-start(bf16[128,1536]{1,0:T(8,128)(2,1)S(1)} %backward_3.1), channel_id=1, source_target_pairs={{192,128},{193,129},{194,130},{195,131},{196,132},{197,133},{198,1... | collective-permute-start | bytes 1179656 | tf_op jit(solution)/shard_map/ppermute | solution.py:518
  198.4 6.3 %collective-permute-start.8 = (bf16[128,1536]{1,0:T(8,128)(2,1)S(1)}, bf16[128,1536]{1,0:T(8,128)(2,1)S(1)}, u32[]{:S(2)}, u32[]{:S(2)}) collective-permute-start(bf16[128,1536]{1,0:T(8,128)(2,1)S(1)} %get-tuple-element.39), channel_id=1, source_target_pairs={{128,64},{129,65},{130,66},{131,67},{132,68},{133,69},{134,70},{13... | collective-permute-start | bytes 1179656 | tf_op jit(solution)/shard_map/ppermute | solution.py:518
  200.7 16.1 %collective-permute-start.5 = (bf16[24,128,128]{2,1,0:T(8,128)(2,1)}, bf16[24,128,128]{2,1,0:T(8,128)(2,1)S(1)}, u32[]{:S(2)}, u32[]{:S(2)}) collective-permute-start(bf16[24,128,128]{2,1,0:T(8,128)(2,1)} %slice.120), channel_id=1, source_target_pairs={{0,48},{1,49},{2,50},{3,51},{4,52},{5,53},{6,54},{7,55},{8,56},{9,... | collective-permute-start | bytes 2359304 | tf_op jit(solution)/shard_map/ppermute | solution.py:416
  202.4 13.6 %copy-start = (bf16[48,128,128]{2,1,0:T(8,128)(2,1)}, bf16[48,128,128]{2,1,0:T(8,128)(2,1)S(1)}, u32[]{:S(2)}) copy-start(bf16[48,128,128]{2,1,0:T(8,128)(2,1)S(1)} %collective-permute-done.4.before_ref) | copy-start | bytes 4718596
  203.4 16.6 %collective-permute-start.6 = (bf16[24,128,128]{2,1,0:T(8,128)(2,1)}, bf16[24,128,128]{2,1,0:T(8,128)(2,1)}, u32[]{:S(2)}, u32[]{:S(2)}) collective-permute-start(bf16[24,128,128]{2,1,0:T(8,128)(2,1)} %slice.121), channel_id=1, source_target_pairs={{0,16},{1,17},{2,18},{3,19},{4,20},{5,21},{6,22},{7,23},{8,24},{9,... | collective-permute-start | bytes 2359304 | tf_op jit(solution)/shard_map/ppermute | solution.py:417
  216.0 9.2 %collective-permute-start.9 = (bf16[128,1536]{1,0:T(8,128)(2,1)}, bf16[128,1536]{1,0:T(8,128)(2,1)S(1)}, u32[]{:S(2)}, u32[]{:S(2)}) collective-permute-start(bf16[128,1536]{1,0:T(8,128)(2,1)} %get-tuple-element.41), channel_id=1, source_target_pairs={{64,0},{65,1},{66,2},{67,3},{68,4},{69,5},{70,6},{71,7},{72,8},{73... | collective-permute-start | bytes 1179656 | tf_op jit(solution)/shard_map/ppermute | solution.py:518
  220.1 1.4 copy-start.1
  221.5 1.4 copy-start.3
  225.4 3.5 %collective-permute-start.10 = (bf16[128,384]{1,0:T(8,128)(2,1)S(1)}, bf16[128,384]{1,0:T(8,128)(2,1)S(1)}, u32[]{:S(2)}, u32[]{:S(2)}) collective-permute-start(bf16[128,384]{1,0:T(8,128)(2,1)S(1)} %get-tuple-element.63), channel_id=1, source_target_pairs={{0,48},{1,49},{2,50},{3,51},{4,52},{5,53},{6,54},{7,55},{8,56},{9,... | collective-permute-start | bytes 294920 | tf_op jit(solution)/shard_map/ppermute | solution.py:433
  225.4 4.8 %collective-permute-start.11 = (bf16[128,384]{1,0:T(8,128)(2,1)S(1)}, bf16[128,384]{1,0:T(8,128)(2,1)S(1)}, u32[]{:S(2)}, u32[]{:S(2)}) collective-permute-start(bf16[128,384]{1,0:T(8,128)(2,1)S(1)} %get-tuple-element.62), channel_id=1, source_target_pairs={{0,16},{1,17},{2,18},{3,19},{4,20},{5,21},{6,22},{7,23},{8,24},{9,... | collective-permute-start | bytes 294920 | tf_op jit(solution)/shard_map/ppermute | solution.py:433
  226.9 5.0 %collective-permute-start.12 = (bf16[128,384]{1,0:T(8,128)(2,1)S(1)}, bf16[128,384]{1,0:T(8,128)(2,1)S(1)}, u32[]{:S(2)}, u32[]{:S(2)}) collective-permute-start(bf16[128,384]{1,0:T(8,128)(2,1)S(1)} %get-tuple-element.61), channel_id=1, source_target_pairs={{0,32},{1,33},{2,34},{3,35},{4,36},{5,37},{6,38},{7,39},{8,40},{9,... | collective-permute-start | bytes 294920 | tf_op jit(solution)/shard_map/ppermute | solution.py:433
  236.9 10.8 %collective-permute-start.13 = (f32[4616,128]{1,0:T(8,128)S(1)}, f32[4616,128]{1,0:T(8,128)S(1)}, u32[]{:S(2)}, u32[]{:S(2)}) collective-permute-start(f32[4616,128]{1,0:T(8,128)S(1)} %get-tuple-element.46), channel_id=1, source_target_pairs={{0,1},{1,0},{2,3},{3,2},{4,5},{5,4},{6,7},{7,6},{8,9},{9,8},{10,11... | collective-permute-start | bytes 7090184 | tf_op jit(solution)/shard_map/ppermute | solution.py:439
  248.5 9.0 %collective-permute-start.20 = (f16[592,128]{1,0:T(8,128)(2,1)S(1)}, f16[592,128]{1,0:T(8,128)(2,1)S(1)}, u32[]{:S(2)}, u32[]{:S(2)}) collective-permute-start(f16[592,128]{1,0:T(8,128)(2,1)S(1)} %get-tuple-element.70), channel_id=1, source_target_pairs={{0,14},{1,15},{2,0},{3,1},{4,2},{5,3},{6,4},{7,5},{8,6},{9,7},{10,... | collective-permute-start | bytes 454664 | tf_op jit(solution)/shard_map/ppermute | solution.py:449
  250.6 12.8 %collective-permute-start.19 = (f16[592,128]{1,0:T(8,128)(2,1)S(1)}, f16[592,128]{1,0:T(8,128)(2,1)S(1)}, u32[]{:S(2)}, u32[]{:S(2)}) collective-permute-start(f16[592,128]{1,0:T(8,128)(2,1)S(1)} %get-tuple-element.69), channel_id=1, source_target_pairs={{0,12},{1,13},{2,14},{3,15},{4,0},{5,1},{6,2},{7,3},{8,4},{9,5},{1... | collective-permute-start | bytes 454664 | tf_op jit(solution)/shard_map/ppermute | solution.py:449
  251.4 15.1 %collective-permute-start.18 = (f16[592,128]{1,0:T(8,128)(2,1)S(1)}, f16[592,128]{1,0:T(8,128)(2,1)S(1)}, u32[]{:S(2)}, u32[]{:S(2)}) collective-permute-start(f16[592,128]{1,0:T(8,128)(2,1)S(1)} %get-tuple-element.68), channel_id=1, source_target_pairs={{0,10},{1,11},{2,12},{3,13},{4,14},{5,15},{6,0},{7,1},{8,2},{9,3},... | collective-permute-start | bytes 454664 | tf_op jit(solution)/shard_map/ppermute | solution.py:449
  253.6 13.0 %collective-permute-start.17 = (f16[592,128]{1,0:T(8,128)(2,1)S(1)}, f16[592,128]{1,0:T(8,128)(2,1)S(1)}, u32[]{:S(2)}, u32[]{:S(2)}) collective-permute-start(f16[592,128]{1,0:T(8,128)(2,1)S(1)} %get-tuple-element.67), channel_id=1, source_target_pairs={{0,8},{1,9},{2,10},{3,11},{4,12},{5,13},{6,14},{7,15},{8,0},{9,1},... | collective-permute-start | bytes 454664 | tf_op jit(solution)/shard_map/ppermute | solution.py:449
  256.1 20.1 %collective-permute-start.16 = (f16[592,128]{1,0:T(8,128)(2,1)S(1)}, f16[592,128]{1,0:T(8,128)(2,1)S(1)}, u32[]{:S(2)}, u32[]{:S(2)}) collective-permute-start(f16[592,128]{1,0:T(8,128)(2,1)S(1)} %get-tuple-element.66), channel_id=1, source_target_pairs={{0,6},{1,7},{2,8},{3,9},{4,10},{5,11},{6,12},{7,13},{8,14},{9,15},... | collective-permute-start | bytes 454664 | tf_op jit(solution)/shard_map/ppermute | solution.py:449
  257.5 19.9 %collective-permute-start.15 = (f16[592,128]{1,0:T(8,128)(2,1)S(1)}, f16[592,128]{1,0:T(8,128)(2,1)S(1)}, u32[]{:S(2)}, u32[]{:S(2)}) collective-permute-start(f16[592,128]{1,0:T(8,128)(2,1)S(1)} %get-tuple-element.65), channel_id=1, source_target_pairs={{0,4},{1,5},{2,6},{3,7},{4,8},{5,9},{6,10},{7,11},{8,12},{9,13},{1... | collective-permute-start | bytes 454664 | tf_op jit(solution)/shard_map/ppermute | solution.py:449
  263.4 21.0 %collective-permute-start.14 = (f16[592,128]{1,0:T(8,128)(2,1)S(1)}, f16[592,128]{1,0:T(8,128)(2,1)S(1)}, u32[]{:S(2)}, u32[]{:S(2)}) collective-permute-start(f16[592,128]{1,0:T(8,128)(2,1)S(1)} %get-tuple-element.64), channel_id=1, source_target_pairs={{0,2},{1,3},{2,4},{3,5},{4,6},{5,7},{6,8},{7,9},{8,10},{9,11},{10,... | collective-permute-start | bytes 454664 | tf_op jit(solution)/shard_map/ppermute | solution.py:449
Sparse Core Ops, SparseCore 0:
  10.1 88.3 all-gather.1

commit v5 on v4

--- a/solution.py
+++ b/solution.py
@@ -13,6 +13,8 @@
 F16 = jnp.float16
 CORES = 2
 CHIPS = 8
+ORDER = (0, 1, 3, 7, 5, 4, 2, 6)
+TAG = 16
 UP_UNROLL = 4
 DOWN_UNROLL = 3
 LIMIT = 12 << 20
@@ -330,7 +332,7 @@
     far = pl.program_id(0)
     y, z, core = place[0], place[1], place[2]
     chips = pl.num_programs(0)
-    owner = y * chips + lax.rem(z + far, chips)
+    owner = y * chips + lax.rem(z + place[3 + far], chips)
 
     @pl.when(far == 0)
     def _():
@@ -407,7 +409,7 @@
 
 
 def hidden_pieces(turned, rows, chips):
-    assert rows == ROWS
+    assert rows == ROWS and chips == CHIPS == len(ORDER)
     half = turned.shape[0] // 2
     down = dp_route(rows, chips, lambda y, z, core: (y - 1, z, core))
     up = dp_route(rows, chips, lambda y, z, core: (y + 1, z, core))
@@ -422,7 +424,8 @@
     owners = rows * chips * CORES
     number = lax.axis_index("dp")
     y = lax.div(number, chips * CORES)
-    place = jnp.stack([y, lax.rem(lax.div(number, CORES), chips), lax.rem(number, CORES)])
+    z = lax.rem(lax.div(number, CORES), chips)
+    place = jnp.stack([y, z, lax.rem(number, CORES)] + [jnp.int32(far) for far in ORDER])
     columns = split_range(cot.shape[1], rows)
     received = []
     for r in (0, 1, rows - 1, 2):
@@ -440,16 +443,30 @@
     chunk = split_range(keep.shape[0] - 8, chips)
     bound = jnp.maximum(total[chips * chunk : chips * chunk + 1], 1e-30)
     power = jnp.floor(13.0 - jnp.log2(bound))
-    factor = jnp.exp2(power)
-    tag = jnp.broadcast_to(power, (16, power.shape[1])).astype(F16)
-    result = total[:chunk]
-    for r in range(1, chips):
-        coded = (total[r * chunk : (r + 1) * chunk] * factor).astype(F16)
-        route = dp_route(rows, chips, lambda y, z, core: (y, z + r, core))
-        got = lax.ppermute(jnp.concatenate([coded, tag], axis=0), "dp", route)
-        got = got.astype(F32)
-        result = result + got[:chunk] * jnp.exp2(-got[chunk : chunk + 1])
-    return result
+
+    def send(values, power, steps):
+        tag = jnp.broadcast_to(power, (TAG, power.shape[1]))
+        coded = jnp.concatenate([values * jnp.exp2(power), tag], axis=0).astype(F16)
+        route = dp_route(rows, chips, lambda y, z, core: (y, z + steps, core))
+        got = lax.ppermute(coded, "dp", route).astype(F32)
+        power = got[-TAG : 1 - TAG]
+        return got[:-TAG] * jnp.exp2(-power), power
+
+    half = chunk // 2
+    middle = 5 * chunk
+    from_below, power_below = send(total[chunk : 3 * chunk], power, 1)
+    from_above, power_above = send(total[3 * chunk : middle], power, -1)
+    low, power_low = send(total[middle : middle + half], power, 2)
+    high, power_high = send(total[middle + half : middle + chunk], power, -2)
+    upward = total[6 * chunk : 7 * chunk] + from_below[chunk:]
+    upward = jnp.concatenate([upward[:half] + low, upward[half:]], axis=0)
+    downward = total[7 * chunk : 8 * chunk] + from_above[chunk:]
+    downward = jnp.concatenate([downward[:half], downward[half:] + high], axis=0)
+    up_power = jnp.minimum(jnp.minimum(power, power_below), power_low) - 2.0
+    down_power = jnp.minimum(jnp.minimum(power, power_above), power_high) - 2.0
+    result = total[:chunk] + from_below[:chunk] + from_above[:chunk]
+    result = result + send(upward, up_power, 2)[0]
+    return result + send(downward, down_power, -2)[0]
 
 
 def lookup(step_values, table):

time: 295 us -> 288 us (0.976)
  waiting for transfers between devices: 160 us -> 148 us
  local copies, waits for them, and re-layouts: 6.79 us -> 12.3 us
    ppermute x7 -> x6, waiting for transfers between devices: 23.9 us -> 11.8 us  [send(): got = lax.ppermute(coded, 'dp', route).astype(F32)]
    unnamed x11 -> x15, local copies, waits for them, and re-layouts: 3.6 us -> 9.01 us
    ppermute x7 -> x6, starting transfers between devices: 11.8 us -> 10.4 us  [send(): got = lax.ppermute(coded, 'dp', route).astype(F32)]
  transfers between devices with their start and end apart: 22 -> 21, of which waited for: 15 -> 13; matrix products, arithmetic and copies ran while one was open for 3% -> 3% of each run, Pallas kernels for 12% -> 12%
where the time goes in v5:
time: 288 us; the launch traced here: 284 us
  waiting for transfers between devices  148 us (51%)
  Pallas kernels  76.4 us (27%)
  starting transfers between devices  28.4 us (10%)
  between operations  13.9 us (5%)
  local copies, waits for them, and re-layouts  12.3 us (4%)
  other arithmetic  5.83 us (2%)
    all_gather x1, waiting for transfers between devices, per_device(): up_flat = lax.all_gather(up_weight, 'dp', axis=1, tiled=True)[0]  85.7 us
    pallas_call x4, Pallas kernels, section_forward(): pl.pallas_call(body, out_shape=out_shape, in_specs=in_specs, out_specs=[V...  36.6 us
    pallas_call x3, Pallas kernels, section_backward(): pl.pallas_call(body, out_shape=out_shape, in_specs=in_specs, out_specs=[V...  32.5 us
    ppermute x3, waiting for transfers between devices, per_device(): arrived = lax.ppermute(result, 'section', [(turn - 1, turn)])  27.3 us
    ppermute x6, waiting for transfers between devices, send(): got = lax.ppermute(coded, 'dp', route).astype(F32)  11.8 us
    ppermute x6, starting transfers between devices, send(): got = lax.ppermute(coded, 'dp', route).astype(F32)  10.4 us
    ppermute x3, waiting for transfers between devices, per_device(): arrived = lax.ppermute(sent, 'section', [(turn, turn - 1)])  9.8 us
    unnamed x15, local copies, waits for them, and re-layouts  9.01 us
  transfers between devices with their start and end apart: 21, of which 13 were waited for; matrix products, arithmetic and copies ran while one was open for 3% of the time, Pallas kernels for 12%

profile of v5, /device:TPU:5, one launch (start us, length us, event | category | flops | bytes accessed | tf_op | source)
XLA Modules:
  0.0 284.4 jit_solution(15300616824450203332)
XLA Ops:
  8.7 1.3 add_convert_fusion.refs_2_.refs_4_
  12.9 85.7 %all-gather.2.cloned.1.call-done = bf16[1,36864,128]{2,1,0:T(8,128)(2,1)} async-done(((bf16[1,576,128]{2,1,0:T(8,128)(2,1)}), bf16[1,36864,128]{2,1,0:T(8,128)(2,1)}) %all-gather.2.cloned.1.call-update) | async-done | bytes 9437200 | tf_op jit(solution)/shard_map/all_gather | solution.py:497
  98.5 10.1 %forward_0.1 = (bf16[128,1536]{1,0:T(8,128)(2,1)S(1)}, bf16[36864,128]{1,0:T(8,128)(2,1)S(1)}, bf16[36864,128]{1,0:T(8,128)(2,1)S(1)}) custom-call(s32[288]{0:T(512)S(1)} %reshape_squeeze.5.refs_0_, s32[288]{0:T(512)S(1)} %reshape_squeeze.4.refs_1_, bf16[128,1536]{1,0:T(8,128)(2,1)S(1)} %add_convert_fusion.refs_2_.refs_4_, ...), custom_call_target="tpu_custom_call" | custom-call | flops 2415919104 | bytes 6144 | tf_op jit(solution)/shard_map/forward_0/pallas_call | solution.py:190
  109.3 8.6 %forward_1.1 = (bf16[128,1536]{1,0:T(8,128)(2,1)S(1)}, bf16[128,1536]{1,0:T(8,128)(2,1)S(1)}) custom-call(s32[288]{0:T(512)S(1)} %reshape_squeeze.5.refs_0_, s32[288]{0:T(512)S(1)} %reshape_squeeze.4.refs_1_, s32[1]{0:T(128)} %bitcast.3.refs_2_, bf16[128,1536]{1,0:T(8,128)(2,1)S(1)} %collective-permute-done.refs_3_, ...), custom_call_target="tpu_custom_call" | custom-call | flops 2415919104 | bytes 6144 | tf_op jit(solution)/shard_map/forward_1/pallas_call | solution.py:190
  119.2 20.3 %collective-permute-done.1.refs_3_ = bf16[128,1536]{1,0:T(8,128)(2,1)S(1)} collective-permute-done((bf16[128,1536]{1,0:T(8,128)(2,1)S(1)}, bf16[128,1536]{1,0:T(8,128)(2,1)S(1)}, u32[]{:S(2)}, u32[]{:S(2)}) %collective-permute-start.1) | collective-permute-done | bytes 393248 | tf_op jit(solution)/shard_map/ppermute | solution.py:518
  139.5 8.6 %forward_2.1 = (bf16[128,1536]{1,0:T(8,128)(2,1)S(1)}, bf16[128,1536]{1,0:T(8,128)(2,1)S(1)}) custom-call(s32[288]{0:T(512)S(1)} %reshape_squeeze.5.refs_0_, s32[288]{0:T(512)S(1)} %reshape_squeeze.4.refs_1_, s32[1]{0:T(128)} %bitcast.3.refs_2_, bf16[128,1536]{1,0:T(8,128)(2,1)S(1)} %collective-permute-done.1.refs_3_, ...), custom_call_target="tpu_custom_call" | custom-call | flops 2415919104 | bytes 6144 | tf_op jit(solution)/shard_map/forward_2/pallas_call | solution.py:190
  148.0 1.3 collective-permute-start.2
  149.4 7.0 %collective-permute-done.2.refs_3_ = bf16[128,1536]{1,0:T(8,128)(2,1)S(1)} collective-permute-done((bf16[128,1536]{1,0:T(8,128)(2,1)S(1)}, bf16[128,1536]{1,0:T(8,128)(2,1)S(1)}, u32[]{:S(2)}, u32[]{:S(2)}) %collective-permute-start.2) | collective-permute-done | bytes 393248 | tf_op jit(solution)/shard_map/ppermute | solution.py:518
  156.3 9.4 %forward_3.1 = (bf16[128,1536]{1,0:T(8,128)(2,1)S(1)}, bf16[128,1536]{1,0:T(8,128)(2,1)S(1)}, f32[48,128,128]{2,1,0:T(8,128)S(1)}, bf16[48,128,128]{2,1,0:T(8,128)(2,1)S(1)}) custom-call(s32[288]{0:T(512)S(1)} %reshape_squeeze.5.refs_0_, s32[288]{0:T(512)S(1)} %reshape_squeeze.4.refs_1_, s32[1]{0:T(128)} %bitcast.3.refs_2_, ...), custom_call_target="tpu_custom_call" | custom-call | flops 2415919104 | bytes 6144 | tf_op jit(solution)/shard_map/forward_3/pallas_call | solution.py:190
  167.3 10.6 %backward_3.1 = bf16[128,1536]{1,0:T(8,128)(2,1)S(1)} custom-call(s32[288]{0:T(512)S(1)} %reshape_squeeze.5.refs_0_, s32[288]{0:T(512)S(1)} %reshape_squeeze.4.refs_1_, bf16[128,1536]{1,0:T(8,128)(2,1)S(1)} %get-tuple-element.36.refs_2_.refs_4_, bf16[128,1536]{1,0:T(8,128)(2,1)S(1)} %get-tuple-element.37.refs_3_.refs_5_, ...), custom_call_target="tpu_custom_call" | custom-call | flops 1000000 | bytes 100000 | tf_op jit(solution)/shard_map/backward_3/pallas_call | solution.py:281
  179.2 8.6 %collective-permute-done.7.refs_3_ = bf16[128,1536]{1,0:T(8,128)(2,1)S(1)} collective-permute-done((bf16[128,1536]{1,0:T(8,128)(2,1)S(1)}, bf16[128,1536]{1,0:T(8,128)(2,1)S(1)}, u32[]{:S(2)}, u32[]{:S(2)}) %collective-permute-start.7) | collective-permute-done | bytes 393248 | tf_op jit(solution)/shard_map/ppermute | solution.py:535
  187.8 10.6 %backward_2.1 = (bf16[128,1536]{1,0:T(8,128)(2,1)S(1)}, bf16[128,1536]{1,0:T(8,128)(2,1)S(1)}) custom-call(s32[288]{0:T(512)S(1)} %reshape_squeeze.5.refs_0_, s32[288]{0:T(512)S(1)} %reshape_squeeze.4.refs_1_, s32[1]{0:T(128)} %bitcast.3.refs_2_, bf16[128,1536]{1,0:T(8,128)(2,1)S(1)} %collective-permute-done.7.refs_3_, ...), custom_call_target="tpu_custom_call" | custom-call | flops 1000000 | bytes 100000 | tf_op jit(solution)/shard_map/backward_2/pallas_call | solution.py:281
  200.7 1.8 collective-permute-start.5
  204.7 11.3 %backward_1.1 = (bf16[128,1536]{1,0:T(8,128)(2,1)}, bf16[128,1536]{1,0:T(8,128)(2,1)S(1)}) custom-call(s32[288]{0:T(512)S(1)} %reshape_squeeze.5.refs_0_, s32[288]{0:T(512)S(1)} %reshape_squeeze.4.refs_1_, s32[1]{0:T(128)} %bitcast.3.refs_2_, bf16[128,1536]{1,0:T(8,128)(2,1)S(1)} %collective-permute-done.8.refs_3_, ...), custom_call_target="tpu_custom_call" | custom-call | flops 30000001024 | bytes 100000 | tf_op jit(solution)/shard_map/backward_1/pallas_call | solution.py:281
  216.8 3.3 %collective-permute-done.6.high_ref = bf16[24,128,128]{2,1,0:T(8,128)(2,1)} collective-permute-done((bf16[24,128,128]{2,1,0:T(8,128)(2,1)}, bf16[24,128,128]{2,1,0:T(8,128)(2,1)}, u32[]{:S(2)}, u32[]{:S(2)}) %collective-permute-start.6) | collective-permute-done | bytes 786464 | tf_op jit(solution)/shard_map/ppermute | solution.py:419
  220.1 1.4 copy-done.3
  221.5 1.4 copy-done.5
  222.9 2.4 join_pieces.1.refs_2_
  225.2 2.6 copy-done
  228.1 1.5 collective-permute-start.11
  229.6 1.9 collective-permute-done.10
  232.8 1.7 collective-permute-done.12
  234.5 2.8 copy-done.1
  237.3 4.9 %weight_gradient.1 = (f32[4616,128]{1,0:T(8,128)S(1)}, f32[4616,128]{1,0:T(8,128)S(1)}) custom-call(s32[11]{0:T(128)S(1)} %stack.15.refs_0_, s32[288]{0:T(512)S(1)} %reshape_squeeze.4.refs_1_, bf16[48,128,512]{2,1,0:T(8,128)(2,1)S(1)} %copy-done.1, bf16[512,384]{1,0:T(8,128)(2,1)S(1)} %pad_maximum_fusion.2.refs_3_), custom_call_target="tpu_custom_call" | custom-call | flops 1207959552 | bytes 6291456 | tf_op jit(solution)/shard_map/weight_gradient/pallas_call | solution.py:372
  242.3 6.7 %collective-permute-start.13 = (f32[4616,128]{1,0:T(8,128)S(1)}, f32[4616,128]{1,0:T(8,128)S(1)}, u32[]{:S(2)}, u32[]{:S(2)}) collective-permute-start(f32[4616,128]{1,0:T(8,128)S(1)} %get-tuple-element.46), channel_id=1, source_target_pairs={{0,1},{1,0},{2,3},{3,2},{4,5},{5,4},{6,7},{7,6},{8,9},{9,8},{10,11... | collective-permute-start | bytes 7090184 | tf_op jit(solution)/shard_map/ppermute | solution.py:442
  248.9 4.2 %collective-permute-done.13 = f32[4616,128]{1,0:T(8,128)S(1)} collective-permute-done((f32[4616,128]{1,0:T(8,128)S(1)}, f32[4616,128]{1,0:T(8,128)S(1)}, u32[]{:S(2)}, u32[]{:S(2)}) %collective-permute-start.13) | collective-permute-done | bytes 2363424 | tf_op jit(solution)/shard_map/ppermute | solution.py:442
  255.1 1.7 collective-permute-start.15
  256.9 3.6 %collective-permute-start.18 = (f16[304,128]{1,0:T(8,128)(2,1)S(1)}, f16[304,128]{1,0:T(8,128)(2,1)S(1)}, u32[]{:S(2)}, u32[]{:S(2)}) collective-permute-start(f16[304,128]{1,0:T(8,128)(2,1)S(1)} %get-tuple-element.78), channel_id=1, source_target_pairs={{0,12},{1,13},{2,14},{3,15},{4,0},{5,1},{6,2},{7,3},{8,4},{9,5},{1... | collective-permute-start | bytes 233480 | tf_op jit(solution)/shard_map/ppermute | solution.py:451
  260.5 6.1 %collective-permute-done.16 = f16[304,128]{1,0:T(8,128)(2,1)S(1)} collective-permute-done((f16[304,128]{1,0:T(8,128)(2,1)S(1)}, f16[304,128]{1,0:T(8,128)(2,1)S(1)}, u32[]{:S(2)}, u32[]{:S(2)}) %collective-permute-start.16) | collective-permute-done | bytes 77856 | tf_op jit(solution)/shard_map/ppermute | solution.py:451
  267.1 2.1 collective-permute-start.17
  269.4 1.6 collective-permute-start.19
  271.0 4.5 %collective-permute-done.17 = f16[592,128]{1,0:T(8,128)(2,1)S(1)} collective-permute-done((f16[592,128]{1,0:T(8,128)(2,1)S(1)}, f16[592,128]{1,0:T(8,128)(2,1)S(1)}, u32[]{:S(2)}, u32[]{:S(2)}) %collective-permute-start.17) | collective-permute-done | bytes 151584 | tf_op jit(solution)/shard_map/ppermute | solution.py:451
  (79 shorter events, 21.2 us)
Async XLA Ops:
  6.5 92.0 %all-gather.2.cloned.1.call-start = ((), (), s32[]{:S(2)}) async-start(), calls=%async_computation | async-start | bytes 9584640 | tf_op jit(solution)/shard_map/all_gather | solution.py:497
  108.6 0.7 collective-permute-start
  117.9 21.6 %collective-permute-start.1 = (bf16[128,1536]{1,0:T(8,128)(2,1)S(1)}, bf16[128,1536]{1,0:T(8,128)(2,1)S(1)}, u32[]{:S(2)}, u32[]{:S(2)}) collective-permute-start(bf16[128,1536]{1,0:T(8,128)(2,1)S(1)} %get-tuple-element.31), channel_id=1, source_target_pairs={{64,128},{65,129},{66,130},{67,131},{68,132},{69,133},{70,134},{71... | collective-permute-start | bytes 1179656 | tf_op jit(solution)/shard_map/ppermute | solution.py:518
  139.5 16.9 %copy-start.6 = (bf16[128,1536]{1,0:T(8,128)(2,1)S(1)}, bf16[128,1536]{1,0:T(8,128)(2,1)}, u32[]{:S(2)}) copy-start(bf16[128,1536]{1,0:T(8,128)(2,1)} %refs_8_.1) | copy-start | bytes 1179652
  148.0 8.3 %collective-permute-start.2 = (bf16[128,1536]{1,0:T(8,128)(2,1)S(1)}, bf16[128,1536]{1,0:T(8,128)(2,1)S(1)}, u32[]{:S(2)}, u32[]{:S(2)}) collective-permute-start(bf16[128,1536]{1,0:T(8,128)(2,1)S(1)} %get-tuple-element.33), channel_id=1, source_target_pairs={{128,192},{129,193},{130,194},{131,195},{132,196},{133,197},{134,1... | collective-permute-start | bytes 1179656 | tf_op jit(solution)/shard_map/ppermute | solution.py:518
  165.8 12.1 %copy-start.4 = (bf16[48,128,128]{2,1,0:T(8,128)(2,1)}, bf16[48,128,128]{2,1,0:T(8,128)(2,1)S(1)}, u32[]{:S(2)}) copy-start(bf16[48,128,128]{2,1,0:T(8,128)(2,1)S(1)} %get-tuple-element.35.own_ref) | copy-start | bytes 4718596
  165.8 33.9 %collective-permute-start.3 = (bf16[48,128,128]{2,1,0:T(8,128)(2,1)S(1)}, bf16[48,128,128]{2,1,0:T(8,128)(2,1)S(1)}, u32[]{:S(2)}, u32[]{:S(2)}) collective-permute-start(bf16[48,128,128]{2,1,0:T(8,128)(2,1)S(1)} %get-tuple-element.35.own_ref), channel_id=1, source_target_pairs={{0,48},{1,49},{2,50},{3,51},{4,52},{5,53},{6,54},{7,55},{8,56},{9,... | collective-permute-start | bytes 4718600 | tf_op jit(solution)/shard_map/ppermute | solution.py:416
  166.4 36.0 %collective-permute-start.4 = (bf16[48,128,128]{2,1,0:T(8,128)(2,1)S(1)}, bf16[48,128,128]{2,1,0:T(8,128)(2,1)S(1)}, u32[]{:S(2)}, u32[]{:S(2)}) collective-permute-start(bf16[48,128,128]{2,1,0:T(8,128)(2,1)S(1)} %get-tuple-element.35.own_ref), channel_id=1, source_target_pairs={{0,16},{1,17},{2,18},{3,19},{4,20},{5,21},{6,22},{7,23},{8,24},{9,... | collective-permute-start | bytes 4718600 | tf_op jit(solution)/shard_map/ppermute | solution.py:417
  177.9 9.9 %collective-permute-start.7 = (bf16[128,1536]{1,0:T(8,128)(2,1)S(1)}, bf16[128,1536]{1,0:T(8,128)(2,1)S(1)}, u32[]{:S(2)}, u32[]{:S(2)}) collective-permute-start(bf16[128,1536]{1,0:T(8,128)(2,1)S(1)} %backward_3.1), channel_id=1, source_target_pairs={{192,128},{193,129},{194,130},{195,131},{196,132},{197,133},{198,1... | collective-permute-start | bytes 1179656 | tf_op jit(solution)/shard_map/ppermute | solution.py:535
  198.4 6.3 %collective-permute-start.8 = (bf16[128,1536]{1,0:T(8,128)(2,1)S(1)}, bf16[128,1536]{1,0:T(8,128)(2,1)S(1)}, u32[]{:S(2)}, u32[]{:S(2)}) collective-permute-start(bf16[128,1536]{1,0:T(8,128)(2,1)S(1)} %get-tuple-element.39), channel_id=1, source_target_pairs={{128,64},{129,65},{130,66},{131,67},{132,68},{133,69},{134,70},{13... | collective-permute-start | bytes 1179656 | tf_op jit(solution)/shard_map/ppermute | solution.py:535
  200.7 16.1 %collective-permute-start.5 = (bf16[24,128,128]{2,1,0:T(8,128)(2,1)}, bf16[24,128,128]{2,1,0:T(8,128)(2,1)S(1)}, u32[]{:S(2)}, u32[]{:S(2)}) collective-permute-start(bf16[24,128,128]{2,1,0:T(8,128)(2,1)} %slice.140), channel_id=1, source_target_pairs={{0,48},{1,49},{2,50},{3,51},{4,52},{5,53},{6,54},{7,55},{8,56},{9,... | collective-permute-start | bytes 2359304 | tf_op jit(solution)/shard_map/ppermute | solution.py:418
  202.4 13.6 %copy-start.2 = (bf16[48,128,128]{2,1,0:T(8,128)(2,1)}, bf16[48,128,128]{2,1,0:T(8,128)(2,1)S(1)}, u32[]{:S(2)}) copy-start(bf16[48,128,128]{2,1,0:T(8,128)(2,1)S(1)} %collective-permute-done.4.before_ref) | copy-start | bytes 4718596
  203.4 16.6 %collective-permute-start.6 = (bf16[24,128,128]{2,1,0:T(8,128)(2,1)}, bf16[24,128,128]{2,1,0:T(8,128)(2,1)}, u32[]{:S(2)}, u32[]{:S(2)}) collective-permute-start(bf16[24,128,128]{2,1,0:T(8,128)(2,1)} %slice.141), channel_id=1, source_target_pairs={{0,16},{1,17},{2,18},{3,19},{4,20},{5,21},{6,22},{7,23},{8,24},{9,... | collective-permute-start | bytes 2359304 | tf_op jit(solution)/shard_map/ppermute | solution.py:419
  216.0 11.9 %collective-permute-start.9 = (bf16[128,1536]{1,0:T(8,128)(2,1)}, bf16[128,1536]{1,0:T(8,128)(2,1)S(1)}, u32[]{:S(2)}, u32[]{:S(2)}) collective-permute-start(bf16[128,1536]{1,0:T(8,128)(2,1)} %get-tuple-element.41), channel_id=1, source_target_pairs={{64,0},{65,1},{66,2},{67,3},{68,4},{69,5},{70,6},{71,7},{72,8},{73... | collective-permute-start | bytes 1179656 | tf_op jit(solution)/shard_map/ppermute | solution.py:535
  220.1 1.4 copy-start.3
  221.5 1.4 copy-start.5
  225.2 2.6 copy-start
  228.0 3.5 %collective-permute-start.10 = (bf16[128,384]{1,0:T(8,128)(2,1)S(1)}, bf16[128,384]{1,0:T(8,128)(2,1)S(1)}, u32[]{:S(2)}, u32[]{:S(2)}) collective-permute-start(bf16[128,384]{1,0:T(8,128)(2,1)S(1)} %get-tuple-element.68), channel_id=1, source_target_pairs={{0,48},{1,49},{2,50},{3,51},{4,52},{5,53},{6,54},{7,55},{8,56},{9,... | collective-permute-start | bytes 294920 | tf_op jit(solution)/shard_map/ppermute | solution.py:436
  228.1 4.8 %collective-permute-start.11 = (bf16[128,384]{1,0:T(8,128)(2,1)S(1)}, bf16[128,384]{1,0:T(8,128)(2,1)S(1)}, u32[]{:S(2)}, u32[]{:S(2)}) collective-permute-start(bf16[128,384]{1,0:T(8,128)(2,1)S(1)} %get-tuple-element.67), channel_id=1, source_target_pairs={{0,16},{1,17},{2,18},{3,19},{4,20},{5,21},{6,22},{7,23},{8,24},{9,... | collective-permute-start | bytes 294920 | tf_op jit(solution)/shard_map/ppermute | solution.py:436
  229.5 5.0 %collective-permute-start.12 = (bf16[128,384]{1,0:T(8,128)(2,1)S(1)}, bf16[128,384]{1,0:T(8,128)(2,1)S(1)}, u32[]{:S(2)}, u32[]{:S(2)}) collective-permute-start(bf16[128,384]{1,0:T(8,128)(2,1)S(1)} %get-tuple-element.66), channel_id=1, source_target_pairs={{0,32},{1,33},{2,34},{3,35},{4,36},{5,37},{6,38},{7,39},{8,40},{9,... | collective-permute-start | bytes 294920 | tf_op jit(solution)/shard_map/ppermute | solution.py:436
  234.5 2.8 copy-start.1
  242.3 10.8 %collective-permute-start.13 = (f32[4616,128]{1,0:T(8,128)S(1)}, f32[4616,128]{1,0:T(8,128)S(1)}, u32[]{:S(2)}, u32[]{:S(2)}) collective-permute-start(f32[4616,128]{1,0:T(8,128)S(1)} %get-tuple-element.46), channel_id=1, source_target_pairs={{0,1},{1,0},{2,3},{3,2},{4,5},{5,4},{6,7},{7,6},{8,9},{9,8},{10,11... | collective-permute-start | bytes 7090184 | tf_op jit(solution)/shard_map/ppermute | solution.py:442
  253.8 12.9 %collective-permute-start.14 = (f16[1168,128]{1,0:T(8,128)(2,1)S(1)}, f16[1168,128]{1,0:T(8,128)(2,1)S(1)}, u32[]{:S(2)}, u32[]{:S(2)}) collective-permute-start(f16[1168,128]{1,0:T(8,128)(2,1)S(1)} %get-tuple-element.75), channel_id=1, source_target_pairs={{0,2},{1,3},{2,4},{3,5},{4,6},{5,7},{6,8},{7,9},{8,10},{9,11},{10,... | collective-permute-start | bytes 897032 | tf_op jit(solution)/shard_map/ppermute | solution.py:451
  255.1 11.7 %collective-permute-start.15 = (f16[1168,128]{1,0:T(8,128)(2,1)S(1)}, f16[1168,128]{1,0:T(8,128)(2,1)S(1)}, u32[]{:S(2)}, u32[]{:S(2)}) collective-permute-start(f16[1168,128]{1,0:T(8,128)(2,1)S(1)} %get-tuple-element.76), channel_id=1, source_target_pairs={{0,14},{1,15},{2,0},{3,1},{4,2},{5,3},{6,4},{7,5},{8,6},{9,7},{10,... | collective-permute-start | bytes 897032 | tf_op jit(solution)/shard_map/ppermute | solution.py:451
  256.8 9.8 %collective-permute-start.16 = (f16[304,128]{1,0:T(8,128)(2,1)S(1)}, f16[304,128]{1,0:T(8,128)(2,1)S(1)}, u32[]{:S(2)}, u32[]{:S(2)}) collective-permute-start(f16[304,128]{1,0:T(8,128)(2,1)S(1)} %get-tuple-element.77), channel_id=1, source_target_pairs={{0,4},{1,5},{2,6},{3,7},{4,8},{5,9},{6,10},{7,11},{8,12},{9,13},{1... | collective-permute-start | bytes 233480 | tf_op jit(solution)/shard_map/ppermute | solution.py:451
  256.9 9.7 %collective-permute-start.18 = (f16[304,128]{1,0:T(8,128)(2,1)S(1)}, f16[304,128]{1,0:T(8,128)(2,1)S(1)}, u32[]{:S(2)}, u32[]{:S(2)}) collective-permute-start(f16[304,128]{1,0:T(8,128)(2,1)S(1)} %get-tuple-element.78), channel_id=1, source_target_pairs={{0,12},{1,13},{2,14},{3,15},{4,0},{5,1},{6,2},{7,3},{8,4},{9,5},{1... | collective-permute-start | bytes 233480 | tf_op jit(solution)/shard_map/ppermute | solution.py:451
  267.1 8.4 %collective-permute-start.17 = (f16[592,128]{1,0:T(8,128)(2,1)S(1)}, f16[592,128]{1,0:T(8,128)(2,1)S(1)}, u32[]{:S(2)}, u32[]{:S(2)}) collective-permute-start(f16[592,128]{1,0:T(8,128)(2,1)S(1)} %pad_maximum_fusion.3), channel_id=1, source_target_pairs={{0,4},{1,5},{2,6},{3,7},{4,8},{5,9},{6,10},{7,11},{8,12},{9,13},{1... | collective-permute-start | bytes 454664 | tf_op jit(solution)/shard_map/ppermute | solution.py:451
  269.4 7.3 %collective-permute-start.19 = (f16[592,128]{1,0:T(8,128)(2,1)S(1)}, f16[592,128]{1,0:T(8,128)(2,1)S(1)}, u32[]{:S(2)}, u32[]{:S(2)}) collective-permute-start(f16[592,128]{1,0:T(8,128)(2,1)S(1)} %pad_maximum_fusion.4), channel_id=1, source_target_pairs={{0,12},{1,13},{2,14},{3,15},{4,0},{5,1},{6,2},{7,3},{8,4},{9,5},{1... | collective-permute-start | bytes 454664 | tf_op jit(solution)/shard_map/ppermute | solution.py:451
Sparse Core Ops, SparseCore 0:
  10.1 88.3 all-gather.1

commit v6 on v5

--- a/solution.py
+++ b/solution.py
@@ -15,8 +15,13 @@
 CHIPS = 8
 ORDER = (0, 1, 3, 7, 5, 4, 2, 6)
 TAG = 16
-UP_UNROLL = 4
-DOWN_UNROLL = 3
+FORWARD_GROUP = 4
+DOWN_GROUP = 12
+UP_GROUP = 6
+UP_UNROLL = 16
+DOWN_UNROLL = 6
+FORWARD_UNROLL = 12
+FORWARD_DOWN = 3
 LIMIT = 12 << 20
 PARTS = 4
 ROWS = 4
@@ -49,6 +54,13 @@
     @pl.when(jnp.logical_not(take))
     def _():
         out_ref[...] = held_ref[...]
+
+
+def part_copy(source, target, part, semaphore):
+    rows = source.shape[0] // PARTS
+    first = part * rows
+    span = pl.ds(first if isinstance(part, int) else pl.multiple_of(first, rows), rows)
+    return pltpu.make_async_copy(source.at[span, :], target.at[span, :], semaphore)
 
 
 def forward_kernel(keep_up, keep_down, turn, last, loss_scale, *refs):
@@ -68,24 +80,24 @@
     if turn:
         x_ref = refs.pop(0)
         pick(section[0] == turn, arrived_ref, held_ref, x_ref)
-    copies = []
     if last:
         slope_ref, turned_ref, normed, hidden = refs
     elif turn:
         normed, hidden = refs
     else:
         uw_to, dw_to, normed, hidden, arrival = refs
-        for source, target in ((uw_ref, uw_to), (dw_ref, dw_to)):
-            rows = source.shape[0] // PARTS
-            for p in range(PARTS):
-                span = pl.ds(p * rows, rows)
-                copy = pltpu.make_async_copy(
-                    source.at[span, :], target.at[span, :], arrival.at[len(copies)]
-                )
-                copies.append(copy)
-        for copy in copies[:PARTS]:
-            copy.start()
+        uw_from, dw_from = uw_ref, dw_ref
         uw_ref, dw_ref = uw_to, dw_to
+
+    def up_copy(part):
+        return part_copy(uw_from, uw_to, part, arrival.at[part])
+
+    def down_copy(part):
+        return part_copy(dw_from, dw_to, part, arrival.at[PARTS + part])
+
+    if not turn:
+        for part in range(PARTS):
+            up_copy(part).start()
     size = normed.shape[-1]
     width_blocks = normed.shape[0]
     hidden_blocks = hidden.shape[0]
@@ -97,10 +109,16 @@
         normed[b] = (piece * inverse * s_ref[:, cols]).astype(BF16)
 
     rows = keep_up * size
+    up_unroll, down_unroll = FORWARD_UNROLL, FORWARD_DOWN
+    if not turn:
+        up_unroll, down_unroll = hidden_blocks // PARTS, width_blocks // PARTS
 
     def up_step(step, carry):
-        for cc in range(UP_UNROLL):
-            c = step * UP_UNROLL + cc
+        if not turn:
+            up_copy(step).wait()
+            down_copy(step).start()
+        for cc in range(up_unroll):
+            c = step * up_unroll + cc
             left = jnp.concatenate(
                 [normed[up_index[c * keep_up + k]] for k in range(keep_up)], axis=1
             )
@@ -114,11 +132,13 @@
                 turned_ref[c] = act.T
         return carry
 
-    group = 4
+    group = FORWARD_GROUP
 
     def down_step(step, carry):
-        for ee in range(DOWN_UNROLL):
-            e = step * DOWN_UNROLL + ee
+        if not turn:
+            down_copy(step).wait()
+        for ee in range(down_unroll):
+            e = step * down_unroll + ee
             acc = x_ref[:, lane_block(e, size)].astype(F32)
             for k in range(0, keep_down, group):
                 left = jnp.concatenate(
@@ -135,19 +155,8 @@
             out_ref[:, lane_block(e, size)] = result
         return carry
 
-    for step_of, count, waits in (
-        (up_step, hidden_blocks // UP_UNROLL, copies[:PARTS]),
-        (down_step, width_blocks // DOWN_UNROLL, copies[PARTS:]),
-    ):
-        if waits:
-            per = split_range(count, PARTS)
-            for p, copy in enumerate(waits):
-                copy.wait()
-                if step_of is up_step:
-                    copies[PARTS + p].start()
-                lax.fori_loop(p * per, (p + 1) * per, step_of, 0)
-        else:
-            lax.fori_loop(0, count, step_of, 0)
+    lax.fori_loop(0, hidden_blocks // up_unroll, up_step, 0)
+    lax.fori_loop(0, width_blocks // down_unroll, down_step, 0)
 
 
 def whole(i, *_):
@@ -219,7 +228,7 @@
     hidden_blocks = grad_hidden.shape[0]
     grad_hidden[...] = jnp.zeros_like(grad_hidden)
     grad_normed[...] = jnp.zeros_like(grad_normed)
-    group = 4
+    group = DOWN_GROUP
 
     def down_step(step, carry):
         for ee in range(DOWN_UNROLL):
@@ -234,7 +243,7 @@
         return carry
 
     lax.fori_loop(0, width_blocks // DOWN_UNROLL, down_step, 0)
-    part = 3
+    part = UP_GROUP
 
     def up_step(step, carry):
         for cc in range(UP_UNROLL):

time: 288 us -> 282 us (0.979)
  Pallas kernels: 76.4 us -> 63.1 us
  waiting for transfers between devices: 148 us -> 156 us
    pallas_call x3, Pallas kernels: 32.5 us -> 24.7 us  [section_backward(): pl.pallas_call(body, out_shape=out_shape, in_specs=in_specs, out_specs=[V...]
    pallas_call x4, Pallas kernels: 36.6 us -> 31.2 us  [section_forward(): pl.pallas_call(body, out_shape=out_shape, in_specs=in_specs, out_specs=[V...]
    ppermute x1, waiting for transfers between devices: 0.01 us -> 4.95 us  [hidden_pieces(): after = lax.ppermute(turned, 'dp', down)]
    ppermute x1, waiting for transfers between devices: 0.01 us -> 3.85 us  [hidden_pieces(): low = lax.ppermute(after[:half], 'dp', down)]
  transfers between devices with their start and end apart: 21 -> 21, of which waited for: 13 -> 14; matrix products, arithmetic and copies ran while one was open for 3% -> 3% of each run, Pallas kernels for 12% -> 10%
where the time goes in v6:
time: 282 us; the launch traced here: 279 us
  waiting for transfers between devices  156 us (55%)
  Pallas kernels  63.1 us (22%)
  starting transfers between devices  28 us (10%)
  between operations  13.9 us (5%)
  local copies, waits for them, and re-layouts  12.3 us (4%)
  other arithmetic  5.83 us (2%)
    all_gather x1, waiting for transfers between devices, per_device(): up_flat = lax.all_gather(up_weight, 'dp', axis=1, tiled=True)[0]  85.7 us
    pallas_call x4, Pallas kernels, section_forward(): pl.pallas_call(body, out_shape=out_shape, in_specs=in_specs, out_specs=[V...  31.2 us
    ppermute x3, waiting for transfers between devices, per_device(): arrived = lax.ppermute(result, 'section', [(turn - 1, turn)])  27.3 us
    pallas_call x3, Pallas kernels, section_backward(): pl.pallas_call(body, out_shape=out_shape, in_specs=in_specs, out_specs=[V...  24.7 us
    ppermute x6, waiting for transfers between devices, send(): got = lax.ppermute(coded, 'dp', route).astype(F32)  11.7 us
    ppermute x6, starting transfers between devices, send(): got = lax.ppermute(coded, 'dp', route).astype(F32)  10.1 us
    unnamed x15, local copies, waits for them, and re-layouts  9.01 us
    ppermute x3, waiting for transfers between devices, per_device(): arrived = lax.ppermute(sent, 'section', [(turn, turn - 1)])  8.58 us
  transfers between devices with their start and end apart: 21, of which 14 were waited for; matrix products, arithmetic and copies ran while one was open for 3% of the time, Pallas kernels for 10%

profile of v6, /device:TPU:5, one launch (start us, length us, event | category | flops | bytes accessed | tf_op | source)
XLA Modules:
  0.0 278.6 jit_solution(7410191904555424937)
XLA Ops:
  12.9 85.7 %all-gather.2.cloned.1.call-done = bf16[1,36864,128]{2,1,0:T(8,128)(2,1)} async-done(((bf16[1,576,128]{2,1,0:T(8,128)(2,1)}), bf16[1,36864,128]{2,1,0:T(8,128)(2,1)}) %all-gather.2.cloned.1.call-update) | async-done | bytes 9437200 | tf_op jit(solution)/shard_map/all_gather | solution.py:506
  98.5 8.8 %forward_0.1 = (bf16[128,1536]{1,0:T(8,128)(2,1)S(1)}, bf16[36864,128]{1,0:T(8,128)(2,1)S(1)}, bf16[36864,128]{1,0:T(8,128)(2,1)S(1)}) custom-call(s32[288]{0:T(512)S(1)} %reshape_squeeze.5.refs_0_, s32[288]{0:T(512)S(1)} %reshape_squeeze.4.refs_1_, bf16[128,1536]{1,0:T(8,128)(2,1)S(1)} %add_convert_fusion.refs_2_.refs_4_, ...), custom_call_target="tpu_custom_call" | custom-call | flops 2415919104 | bytes 6144 | tf_op jit(solution)/shard_map/forward_0/pallas_call | solution.py:199
  108.0 7.3 %forward_1.1 = (bf16[128,1536]{1,0:T(8,128)(2,1)S(1)}, bf16[128,1536]{1,0:T(8,128)(2,1)S(1)}) custom-call(s32[288]{0:T(512)S(1)} %reshape_squeeze.5.refs_0_, s32[288]{0:T(512)S(1)} %reshape_squeeze.4.refs_1_, s32[1]{0:T(128)} %bitcast.3.refs_2_, bf16[128,1536]{1,0:T(8,128)(2,1)S(1)} %collective-permute-done.refs_3_, ...), custom_call_target="tpu_custom_call" | custom-call | flops 2415919104 | bytes 6144 | tf_op jit(solution)/shard_map/forward_1/pallas_call | solution.py:199
  116.6 20.3 %collective-permute-done.1.refs_3_ = bf16[128,1536]{1,0:T(8,128)(2,1)S(1)} collective-permute-done((bf16[128,1536]{1,0:T(8,128)(2,1)S(1)}, bf16[128,1536]{1,0:T(8,128)(2,1)S(1)}, u32[]{:S(2)}, u32[]{:S(2)}) %collective-permute-start.1) | collective-permute-done | bytes 393248 | tf_op jit(solution)/shard_map/ppermute | solution.py:527
  136.9 7.3 %forward_2.1 = (bf16[128,1536]{1,0:T(8,128)(2,1)S(1)}, bf16[128,1536]{1,0:T(8,128)(2,1)S(1)}) custom-call(s32[288]{0:T(512)S(1)} %reshape_squeeze.5.refs_0_, s32[288]{0:T(512)S(1)} %reshape_squeeze.4.refs_1_, s32[1]{0:T(128)} %bitcast.3.refs_2_, bf16[128,1536]{1,0:T(8,128)(2,1)S(1)} %collective-permute-done.1.refs_3_, ...), custom_call_target="tpu_custom_call" | custom-call | flops 2415919104 | bytes 6144 | tf_op jit(solution)/shard_map/forward_2/pallas_call | solution.py:199
  145.5 7.0 %collective-permute-done.2.refs_3_ = bf16[128,1536]{1,0:T(8,128)(2,1)S(1)} collective-permute-done((bf16[128,1536]{1,0:T(8,128)(2,1)S(1)}, bf16[128,1536]{1,0:T(8,128)(2,1)S(1)}, u32[]{:S(2)}, u32[]{:S(2)}) %collective-permute-start.2) | collective-permute-done | bytes 393248 | tf_op jit(solution)/shard_map/ppermute | solution.py:527
  152.5 7.9 %forward_3.1 = (bf16[128,1536]{1,0:T(8,128)(2,1)S(1)}, bf16[128,1536]{1,0:T(8,128)(2,1)S(1)}, f32[48,128,128]{2,1,0:T(8,128)S(1)}, bf16[48,128,128]{2,1,0:T(8,128)(2,1)S(1)}) custom-call(s32[288]{0:T(512)S(1)} %reshape_squeeze.5.refs_0_, s32[288]{0:T(512)S(1)} %reshape_squeeze.4.refs_1_, s32[1]{0:T(128)} %bitcast.3.refs_2_, ...), custom_call_target="tpu_custom_call" | custom-call | flops 2415919104 | bytes 6144 | tf_op jit(solution)/shard_map/forward_3/pallas_call | solution.py:199
  161.9 8.0 %backward_3.1 = bf16[128,1536]{1,0:T(8,128)(2,1)S(1)} custom-call(s32[288]{0:T(512)S(1)} %reshape_squeeze.5.refs_0_, s32[288]{0:T(512)S(1)} %reshape_squeeze.4.refs_1_, bf16[128,1536]{1,0:T(8,128)(2,1)S(1)} %get-tuple-element.36.refs_2_.refs_4_, bf16[128,1536]{1,0:T(8,128)(2,1)S(1)} %get-tuple-element.37.refs_3_.refs_5_, ...), custom_call_target="tpu_custom_call" | custom-call | flops 1000000 | bytes 100000 | tf_op jit(solution)/shard_map/backward_3/pallas_call | solution.py:290
  171.2 8.6 %collective-permute-done.7.refs_3_ = bf16[128,1536]{1,0:T(8,128)(2,1)S(1)} collective-permute-done((bf16[128,1536]{1,0:T(8,128)(2,1)S(1)}, bf16[128,1536]{1,0:T(8,128)(2,1)S(1)}, u32[]{:S(2)}, u32[]{:S(2)}) %collective-permute-start.7) | collective-permute-done | bytes 393248 | tf_op jit(solution)/shard_map/ppermute | solution.py:544
  179.8 8.0 %backward_2.1 = (bf16[128,1536]{1,0:T(8,128)(2,1)S(1)}, bf16[128,1536]{1,0:T(8,128)(2,1)S(1)}) custom-call(s32[288]{0:T(512)S(1)} %reshape_squeeze.5.refs_0_, s32[288]{0:T(512)S(1)} %reshape_squeeze.4.refs_1_, s32[1]{0:T(128)} %bitcast.3.refs_2_, bf16[128,1536]{1,0:T(8,128)(2,1)S(1)} %collective-permute-done.7.refs_3_, ...), custom_call_target="tpu_custom_call" | custom-call | flops 1000000 | bytes 100000 | tf_op jit(solution)/shard_map/backward_2/pallas_call | solution.py:290
  189.1 4.9 %collective-permute-done.3.after_ref = bf16[48,128,128]{2,1,0:T(8,128)(2,1)S(1)} collective-permute-done((bf16[48,128,128]{2,1,0:T(8,128)(2,1)S(1)}, bf16[48,128,128]{2,1,0:T(8,128)(2,1)S(1)}, u32[]{:S(2)}, u32[]{:S(2)}) %collective-permute-start.3) | collective-permute-done | bytes 1572896 | tf_op jit(solution)/shard_map/ppermute | solution.py:425
  195.0 1.7 collective-permute-start.5
  197.7 8.7 %backward_1.1 = (bf16[128,1536]{1,0:T(8,128)(2,1)}, bf16[128,1536]{1,0:T(8,128)(2,1)S(1)}) custom-call(s32[288]{0:T(512)S(1)} %reshape_squeeze.5.refs_0_, s32[288]{0:T(512)S(1)} %reshape_squeeze.4.refs_1_, s32[1]{0:T(128)} %bitcast.3.refs_2_, bf16[128,1536]{1,0:T(8,128)(2,1)S(1)} %collective-permute-done.8.refs_3_, ...), custom_call_target="tpu_custom_call" | custom-call | flops 30000001024 | bytes 100000 | tf_op jit(solution)/shard_map/backward_1/pallas_call | solution.py:290
  207.2 3.8 %collective-permute-done.5.low_ref = bf16[24,128,128]{2,1,0:T(8,128)(2,1)S(1)} collective-permute-done((bf16[24,128,128]{2,1,0:T(8,128)(2,1)}, bf16[24,128,128]{2,1,0:T(8,128)(2,1)S(1)}, u32[]{:S(2)}, u32[]{:S(2)}) %collective-permute-start.5) | collective-permute-done | bytes 786464 | tf_op jit(solution)/shard_map/ppermute | solution.py:427
  211.1 3.7 %collective-permute-done.6.high_ref = bf16[24,128,128]{2,1,0:T(8,128)(2,1)} collective-permute-done((bf16[24,128,128]{2,1,0:T(8,128)(2,1)}, bf16[24,128,128]{2,1,0:T(8,128)(2,1)}, u32[]{:S(2)}, u32[]{:S(2)}) %collective-permute-start.6) | collective-permute-done | bytes 786464 | tf_op jit(solution)/shard_map/ppermute | solution.py:428
  214.8 1.4 copy-done.3
  217.6 2.4 join_pieces.1.refs_2_
  220.0 2.6 copy-done
  223.0 1.5 collective-permute-start.11
  224.6 1.9 collective-permute-done.10
  227.8 1.7 collective-permute-done.12
  229.5 2.8 copy-done.1
  232.3 4.9 %weight_gradient.1 = (f32[4616,128]{1,0:T(8,128)S(1)}, f32[4616,128]{1,0:T(8,128)S(1)}) custom-call(s32[11]{0:T(128)S(1)} %stack.15.refs_0_, s32[288]{0:T(512)S(1)} %reshape_squeeze.4.refs_1_, bf16[48,128,512]{2,1,0:T(8,128)(2,1)S(1)} %copy-done.1, bf16[512,384]{1,0:T(8,128)(2,1)S(1)} %pad_maximum_fusion.2.refs_3_), custom_call_target="tpu_custom_call" | custom-call | flops 1207959552 | bytes 6291456 | tf_op jit(solution)/shard_map/weight_gradient/pallas_call | solution.py:381
  237.2 6.2 %collective-permute-start.13 = (f32[4616,128]{1,0:T(8,128)S(1)}, f32[4616,128]{1,0:T(8,128)S(1)}, u32[]{:S(2)}, u32[]{:S(2)}) collective-permute-start(f32[4616,128]{1,0:T(8,128)S(1)} %get-tuple-element.46), channel_id=1, source_target_pairs={{0,1},{1,0},{2,3},{3,2},{4,5},{5,4},{6,7},{7,6},{8,9},{9,8},{10,11... | collective-permute-start | bytes 7090184 | tf_op jit(solution)/shard_map/ppermute | solution.py:451
  243.4 4.2 %collective-permute-done.13 = f32[4616,128]{1,0:T(8,128)S(1)} collective-permute-done((f32[4616,128]{1,0:T(8,128)S(1)}, f32[4616,128]{1,0:T(8,128)S(1)}, u32[]{:S(2)}, u32[]{:S(2)}) %collective-permute-start.13) | collective-permute-done | bytes 2363424 | tf_op jit(solution)/shard_map/ppermute | solution.py:451
  249.3 1.7 collective-permute-start.15
  251.2 3.6 %collective-permute-start.18 = (f16[304,128]{1,0:T(8,128)(2,1)S(1)}, f16[304,128]{1,0:T(8,128)(2,1)S(1)}, u32[]{:S(2)}, u32[]{:S(2)}) collective-permute-start(f16[304,128]{1,0:T(8,128)(2,1)S(1)} %get-tuple-element.78), channel_id=1, source_target_pairs={{0,12},{1,13},{2,14},{3,15},{4,0},{5,1},{6,2},{7,3},{8,4},{9,5},{1... | collective-permute-start | bytes 233480 | tf_op jit(solution)/shard_map/ppermute | solution.py:460
  254.8 6.2 %collective-permute-done.16 = f16[304,128]{1,0:T(8,128)(2,1)S(1)} collective-permute-done((f16[304,128]{1,0:T(8,128)(2,1)S(1)}, f16[304,128]{1,0:T(8,128)(2,1)S(1)}, u32[]{:S(2)}, u32[]{:S(2)}) %collective-permute-start.16) | collective-permute-done | bytes 77856 | tf_op jit(solution)/shard_map/ppermute | solution.py:460
  261.5 2.0 collective-permute-start.17
  263.6 1.7 collective-permute-start.19
  265.4 4.1 %collective-permute-done.17 = f16[592,128]{1,0:T(8,128)(2,1)S(1)} collective-permute-done((f16[592,128]{1,0:T(8,128)(2,1)S(1)}, f16[592,128]{1,0:T(8,128)(2,1)S(1)}, u32[]{:S(2)}, u32[]{:S(2)}) %collective-permute-start.17) | collective-permute-done | bytes 151584 | tf_op jit(solution)/shard_map/ppermute | solution.py:460
  269.5 1.4 collective-permute-done.19
  (79 shorter events, 22.9 us)
Async XLA Ops:
  6.5 92.0 %all-gather.2.cloned.1.call-start = ((), (), s32[]{:S(2)}) async-start(), calls=%async_computation | async-start | bytes 9584640 | tf_op jit(solution)/shard_map/all_gather | solution.py:506
  107.3 0.7 collective-permute-start
  115.3 21.6 %collective-permute-start.1 = (bf16[128,1536]{1,0:T(8,128)(2,1)S(1)}, bf16[128,1536]{1,0:T(8,128)(2,1)S(1)}, u32[]{:S(2)}, u32[]{:S(2)}) collective-permute-start(bf16[128,1536]{1,0:T(8,128)(2,1)S(1)} %get-tuple-element.31), channel_id=1, source_target_pairs={{64,128},{65,129},{66,130},{67,131},{68,132},{69,133},{70,134},{71... | collective-permute-start | bytes 1179656 | tf_op jit(solution)/shard_map/ppermute | solution.py:527
  136.9 15.6 %copy-start.6 = (bf16[128,1536]{1,0:T(8,128)(2,1)S(1)}, bf16[128,1536]{1,0:T(8,128)(2,1)}, u32[]{:S(2)}) copy-start(bf16[128,1536]{1,0:T(8,128)(2,1)} %refs_8_.1) | copy-start | bytes 1179652
  144.2 8.3 %collective-permute-start.2 = (bf16[128,1536]{1,0:T(8,128)(2,1)S(1)}, bf16[128,1536]{1,0:T(8,128)(2,1)S(1)}, u32[]{:S(2)}, u32[]{:S(2)}) collective-permute-start(bf16[128,1536]{1,0:T(8,128)(2,1)S(1)} %get-tuple-element.33), channel_id=1, source_target_pairs={{128,192},{129,193},{130,194},{131,195},{132,196},{133,197},{134,1... | collective-permute-start | bytes 1179656 | tf_op jit(solution)/shard_map/ppermute | solution.py:527
  160.3 9.5 %copy-start.4 = (bf16[48,128,128]{2,1,0:T(8,128)(2,1)}, bf16[48,128,128]{2,1,0:T(8,128)(2,1)S(1)}, u32[]{:S(2)}) copy-start(bf16[48,128,128]{2,1,0:T(8,128)(2,1)S(1)} %get-tuple-element.35.own_ref) | copy-start | bytes 4718596
  160.4 33.7 %collective-permute-start.3 = (bf16[48,128,128]{2,1,0:T(8,128)(2,1)S(1)}, bf16[48,128,128]{2,1,0:T(8,128)(2,1)S(1)}, u32[]{:S(2)}, u32[]{:S(2)}) collective-permute-start(bf16[48,128,128]{2,1,0:T(8,128)(2,1)S(1)} %get-tuple-element.35.own_ref), channel_id=1, source_target_pairs={{0,48},{1,49},{2,50},{3,51},{4,52},{5,53},{6,54},{7,55},{8,56},{9,... | collective-permute-start | bytes 4718600 | tf_op jit(solution)/shard_map/ppermute | solution.py:425
  161.0 35.7 %collective-permute-start.4 = (bf16[48,128,128]{2,1,0:T(8,128)(2,1)S(1)}, bf16[48,128,128]{2,1,0:T(8,128)(2,1)S(1)}, u32[]{:S(2)}, u32[]{:S(2)}) collective-permute-start(bf16[48,128,128]{2,1,0:T(8,128)(2,1)S(1)} %get-tuple-element.35.own_ref), channel_id=1, source_target_pairs={{0,16},{1,17},{2,18},{3,19},{4,20},{5,21},{6,22},{7,23},{8,24},{9,... | collective-permute-start | bytes 4718600 | tf_op jit(solution)/shard_map/ppermute | solution.py:426
  169.9 9.9 %collective-permute-start.7 = (bf16[128,1536]{1,0:T(8,128)(2,1)S(1)}, bf16[128,1536]{1,0:T(8,128)(2,1)S(1)}, u32[]{:S(2)}, u32[]{:S(2)}) collective-permute-start(bf16[128,1536]{1,0:T(8,128)(2,1)S(1)} %backward_3.1), channel_id=1, source_target_pairs={{192,128},{193,129},{194,130},{195,131},{196,132},{197,133},{198,1... | collective-permute-start | bytes 1179656 | tf_op jit(solution)/shard_map/ppermute | solution.py:544
  187.7 10.0 %collective-permute-start.8 = (bf16[128,1536]{1,0:T(8,128)(2,1)S(1)}, bf16[128,1536]{1,0:T(8,128)(2,1)S(1)}, u32[]{:S(2)}, u32[]{:S(2)}) collective-permute-start(bf16[128,1536]{1,0:T(8,128)(2,1)S(1)} %get-tuple-element.39), channel_id=1, source_target_pairs={{128,64},{129,65},{130,66},{131,67},{132,68},{133,69},{134,70},{13... | collective-permute-start | bytes 1179656 | tf_op jit(solution)/shard_map/ppermute | solution.py:544
  195.0 16.1 %collective-permute-start.5 = (bf16[24,128,128]{2,1,0:T(8,128)(2,1)}, bf16[24,128,128]{2,1,0:T(8,128)(2,1)S(1)}, u32[]{:S(2)}, u32[]{:S(2)}) collective-permute-start(bf16[24,128,128]{2,1,0:T(8,128)(2,1)} %slice.140), channel_id=1, source_target_pairs={{0,48},{1,49},{2,50},{3,51},{4,52},{5,53},{6,54},{7,55},{8,56},{9,... | collective-permute-start | bytes 2359304 | tf_op jit(solution)/shard_map/ppermute | solution.py:427
  196.7 9.8 %copy-start.2 = (bf16[48,128,128]{2,1,0:T(8,128)(2,1)}, bf16[48,128,128]{2,1,0:T(8,128)(2,1)S(1)}, u32[]{:S(2)}) copy-start(bf16[48,128,128]{2,1,0:T(8,128)(2,1)S(1)} %collective-permute-done.4.before_ref) | copy-start | bytes 4718596
  197.7 17.0 %collective-permute-start.6 = (bf16[24,128,128]{2,1,0:T(8,128)(2,1)}, bf16[24,128,128]{2,1,0:T(8,128)(2,1)}, u32[]{:S(2)}, u32[]{:S(2)}) collective-permute-start(bf16[24,128,128]{2,1,0:T(8,128)(2,1)} %slice.141), channel_id=1, source_target_pairs={{0,16},{1,17},{2,18},{3,19},{4,20},{5,21},{6,22},{7,23},{8,24},{9,... | collective-permute-start | bytes 2359304 | tf_op jit(solution)/shard_map/ppermute | solution.py:428
  206.5 16.1 %collective-permute-start.9 = (bf16[128,1536]{1,0:T(8,128)(2,1)}, bf16[128,1536]{1,0:T(8,128)(2,1)S(1)}, u32[]{:S(2)}, u32[]{:S(2)}) collective-permute-start(bf16[128,1536]{1,0:T(8,128)(2,1)} %get-tuple-element.41), channel_id=1, source_target_pairs={{64,0},{65,1},{66,2},{67,3},{68,4},{69,5},{70,6},{71,7},{72,8},{73... | collective-permute-start | bytes 1179656 | tf_op jit(solution)/shard_map/ppermute | solution.py:544
  214.8 1.4 copy-start.3
  216.2 1.4 copy-start.5
  220.0 2.6 copy-start
  222.7 3.8 %collective-permute-start.10 = (bf16[128,384]{1,0:T(8,128)(2,1)S(1)}, bf16[128,384]{1,0:T(8,128)(2,1)S(1)}, u32[]{:S(2)}, u32[]{:S(2)}) collective-permute-start(bf16[128,384]{1,0:T(8,128)(2,1)S(1)} %get-tuple-element.68), channel_id=1, source_target_pairs={{0,48},{1,49},{2,50},{3,51},{4,52},{5,53},{6,54},{7,55},{8,56},{9,... | collective-permute-start | bytes 294920 | tf_op jit(solution)/shard_map/ppermute | solution.py:445
  223.0 4.8 %collective-permute-start.11 = (bf16[128,384]{1,0:T(8,128)(2,1)S(1)}, bf16[128,384]{1,0:T(8,128)(2,1)S(1)}, u32[]{:S(2)}, u32[]{:S(2)}) collective-permute-start(bf16[128,384]{1,0:T(8,128)(2,1)S(1)} %get-tuple-element.67), channel_id=1, source_target_pairs={{0,16},{1,17},{2,18},{3,19},{4,20},{5,21},{6,22},{7,23},{8,24},{9,... | collective-permute-start | bytes 294920 | tf_op jit(solution)/shard_map/ppermute | solution.py:445
  224.5 5.0 %collective-permute-start.12 = (bf16[128,384]{1,0:T(8,128)(2,1)S(1)}, bf16[128,384]{1,0:T(8,128)(2,1)S(1)}, u32[]{:S(2)}, u32[]{:S(2)}) collective-permute-start(bf16[128,384]{1,0:T(8,128)(2,1)S(1)} %get-tuple-element.66), channel_id=1, source_target_pairs={{0,32},{1,33},{2,34},{3,35},{4,36},{5,37},{6,38},{7,39},{8,40},{9,... | collective-permute-start | bytes 294920 | tf_op jit(solution)/shard_map/ppermute | solution.py:445
  229.5 2.8 copy-start.1
  237.2 10.4 %collective-permute-start.13 = (f32[4616,128]{1,0:T(8,128)S(1)}, f32[4616,128]{1,0:T(8,128)S(1)}, u32[]{:S(2)}, u32[]{:S(2)}) collective-permute-start(f32[4616,128]{1,0:T(8,128)S(1)} %get-tuple-element.46), channel_id=1, source_target_pairs={{0,1},{1,0},{2,3},{3,2},{4,5},{5,4},{6,7},{7,6},{8,9},{9,8},{10,11... | collective-permute-start | bytes 7090184 | tf_op jit(solution)/shard_map/ppermute | solution.py:451
  248.3 12.7 %collective-permute-start.14 = (f16[1168,128]{1,0:T(8,128)(2,1)S(1)}, f16[1168,128]{1,0:T(8,128)(2,1)S(1)}, u32[]{:S(2)}, u32[]{:S(2)}) collective-permute-start(f16[1168,128]{1,0:T(8,128)(2,1)S(1)} %get-tuple-element.75), channel_id=1, source_target_pairs={{0,2},{1,3},{2,4},{3,5},{4,6},{5,7},{6,8},{7,9},{8,10},{9,11},{10,... | collective-permute-start | bytes 897032 | tf_op jit(solution)/shard_map/ppermute | solution.py:460
  249.3 11.8 %collective-permute-start.15 = (f16[1168,128]{1,0:T(8,128)(2,1)S(1)}, f16[1168,128]{1,0:T(8,128)(2,1)S(1)}, u32[]{:S(2)}, u32[]{:S(2)}) collective-permute-start(f16[1168,128]{1,0:T(8,128)(2,1)S(1)} %get-tuple-element.76), channel_id=1, source_target_pairs={{0,14},{1,15},{2,0},{3,1},{4,2},{5,3},{6,4},{7,5},{8,6},{9,7},{10,... | collective-permute-start | bytes 897032 | tf_op jit(solution)/shard_map/ppermute | solution.py:460
  251.1 9.9 %collective-permute-start.16 = (f16[304,128]{1,0:T(8,128)(2,1)S(1)}, f16[304,128]{1,0:T(8,128)(2,1)S(1)}, u32[]{:S(2)}, u32[]{:S(2)}) collective-permute-start(f16[304,128]{1,0:T(8,128)(2,1)S(1)} %get-tuple-element.77), channel_id=1, source_target_pairs={{0,4},{1,5},{2,6},{3,7},{4,8},{5,9},{6,10},{7,11},{8,12},{9,13},{1... | collective-permute-start | bytes 233480 | tf_op jit(solution)/shard_map/ppermute | solution.py:460
  251.2 9.8 %collective-permute-start.18 = (f16[304,128]{1,0:T(8,128)(2,1)S(1)}, f16[304,128]{1,0:T(8,128)(2,1)S(1)}, u32[]{:S(2)}, u32[]{:S(2)}) collective-permute-start(f16[304,128]{1,0:T(8,128)(2,1)S(1)} %get-tuple-element.78), channel_id=1, source_target_pairs={{0,12},{1,13},{2,14},{3,15},{4,0},{5,1},{6,2},{7,3},{8,4},{9,5},{1... | collective-permute-start | bytes 233480 | tf_op jit(solution)/shard_map/ppermute | solution.py:460
  261.5 8.0 %collective-permute-start.17 = (f16[592,128]{1,0:T(8,128)(2,1)S(1)}, f16[592,128]{1,0:T(8,128)(2,1)S(1)}, u32[]{:S(2)}, u32[]{:S(2)}) collective-permute-start(f16[592,128]{1,0:T(8,128)(2,1)S(1)} %pad_maximum_fusion.3), channel_id=1, source_target_pairs={{0,4},{1,5},{2,6},{3,7},{4,8},{5,9},{6,10},{7,11},{8,12},{9,13},{1... | collective-permute-start | bytes 454664 | tf_op jit(solution)/shard_map/ppermute | solution.py:460
  263.6 7.3 %collective-permute-start.19 = (f16[592,128]{1,0:T(8,128)(2,1)S(1)}, f16[592,128]{1,0:T(8,128)(2,1)S(1)}, u32[]{:S(2)}, u32[]{:S(2)}) collective-permute-start(f16[592,128]{1,0:T(8,128)(2,1)S(1)} %pad_maximum_fusion.4), channel_id=1, source_target_pairs={{0,12},{1,13},{2,14},{3,15},{4,0},{5,1},{6,2},{7,3},{8,4},{9,5},{1... | collective-permute-start | bytes 454664 | tf_op jit(solution)/shard_map/ppermute | solution.py:460
Sparse Core Ops, SparseCore 0:
  10.1 88.3 all-gather.1

commit v7 on v6

--- a/solution.py
+++ b/solution.py
@@ -19,7 +19,7 @@
 DOWN_GROUP = 12
 UP_GROUP = 6
 UP_UNROLL = 16
-DOWN_UNROLL = 6
+DOWN_UNROLL = 3
 FORWARD_UNROLL = 12
 FORWARD_DOWN = 3
 LIMIT = 12 << 20
@@ -429,17 +429,21 @@
     return [turned, after, before, low, high]
 
 
-def reduce_weight_gradient(joined, cot, down_index, rows, chips):
-    owners = rows * chips * CORES
+def dp_place(rows, chips, columns):
     number = lax.axis_index("dp")
     y = lax.div(number, chips * CORES)
     z = lax.rem(lax.div(number, CORES), chips)
     place = jnp.stack([y, z, lax.rem(number, CORES)] + [jnp.int32(far) for far in ORDER])
+    firsts = [lax.rem(y + rows - r, rows) * columns for r in range(rows)]
+    return place, firsts
+
+
+def reduce_weight_gradient(joined, cot, down_index, place, firsts, rows, chips):
+    owners = rows * chips * CORES
     columns = split_range(cot.shape[1], rows)
     received = []
     for r in (0, 1, rows - 1, 2):
-        first = lax.rem(y + rows - r, rows) * columns
-        part = lax.dynamic_slice_in_dim(cot, first, columns, 1)
+        part = lax.dynamic_slice_in_dim(cot, firsts[r], columns, 1)
         if r:
             route = dp_route(rows, chips, lambda y, z, core: (y - r, z, core))
             part = lax.ppermute(part, "dp", route)
@@ -516,7 +520,12 @@
     scale_plus = 1.0 + lookup(step_index, table)
     indices = (up_index, down_index)
     section = section_number.reshape(1).astype(jnp.int32)
-    section, entry = lax.optimization_barrier((section, entry))
+    rows = split_range(owner_count, CHIPS * CORES)
+    place, firsts = dp_place(rows, CHIPS, split_range(feature_count, rows))
+    opening = section_number == 0
+    section, entry, place, firsts, opening = lax.optimization_barrier(
+        (section, entry, place, firsts, opening)
+    )
 
     result, *weights = section_forward(
         0, False, loss_scale, (entry,), scale_plus, (up_flat, down_flat), indices, None
@@ -531,7 +540,6 @@
         )
     slope, turned = kept
     cotangent = result
-    rows = split_range(owner_count, CHIPS * CORES)
     pieces = hidden_pieces(turned, rows, CHIPS)
     states = (cotangent,)
     for turn in range(section_count - 1, 0, -1):
@@ -544,9 +552,9 @@
         arrived = lax.ppermute(sent, "section", [(turn, turn - 1)])
         states = (section, arrived, cotangent)
     joined, arrived = lax.optimization_barrier((join_pieces(pieces), arrived))
-    cotangent = jnp.where(section_number == 0, arrived, cotangent)
-
-    return reduce_weight_gradient(joined, cotangent, down_index, rows, CHIPS)[None]
+    cotangent = jnp.where(opening, arrived, cotangent)
+
+    return reduce_weight_gradient(joined, cotangent, down_index, place, firsts, rows, CHIPS)[None]
 
 
 def solution(mesh):

time: 282 us -> 278 us (0.986)
  local copies, waits for them, and re-layouts: 12.3 us -> 7.06 us
  waiting for transfers between devices: 156 us -> 151 us
  starting transfers between devices: 28 us -> 32.4 us
    unnamed x15 -> x11, local copies, waits for them, and re-layouts: 9.01 us -> 3.6 us
    ppermute x1, waiting for transfers between devices: 4.95 us -> 0.01 us  [hidden_pieces(): after = lax.ppermute(turned, 'dp', down)]
    ppermute x1, waiting for transfers between devices: 0.01 us -> 4.32 us  [hidden_pieces(): before = lax.ppermute(turned, 'dp', up)]
    ppermute x1, waiting for transfers between devices: 3.85 us -> 0.11 us  [hidden_pieces(): low = lax.ppermute(after[:half], 'dp', down)]
    ppermute x3, starting transfers between devices: 1.76 us -> 4.96 us  [reduce_weight_gradient(): part = lax.ppermute(part, 'dp', route)]
where the time goes in v7:
time: 278 us; the launch traced here: 274 us
  waiting for transfers between devices  151 us (54%)
  Pallas kernels  64.1 us (23%)
  starting transfers between devices  32.4 us (12%)
  between operations  13.9 us (5%)
  local copies, waits for them, and re-layouts  7.06 us (3%)
  other arithmetic  5.72 us (2%)
    all_gather x1, waiting for transfers between devices, per_device(): up_flat = lax.all_gather(up_weight, 'dp', axis=1, tiled=True)[0]  85.5 us
    pallas_call x4, Pallas kernels, section_forward(): pl.pallas_call(body, out_shape=out_shape, in_specs=in_specs, out_specs=[V...  31.2 us
    ppermute x3, waiting for transfers between devices, per_device(): arrived = lax.ppermute(result, 'section', [(turn - 1, turn)])  27.3 us
    pallas_call x3, Pallas kernels, section_backward(): pl.pallas_call(body, out_shape=out_shape, in_specs=in_specs, out_specs=[V...  25.6 us
    ppermute x6, waiting for transfers between devices, send(): got = lax.ppermute(coded, 'dp', route).astype(F32)  13.9 us
    ppermute x6, starting transfers between devices, send(): got = lax.ppermute(coded, 'dp', route).astype(F32)  9.26 us
    ppermute x3, waiting for transfers between devices, per_device(): arrived = lax.ppermute(sent, 'section', [(turn, turn - 1)])  8.58 us
    ppermute x1, starting transfers between devices, reduce_weight_gradient(): total = keep + lax.ppermute(give, 'dp', swap)  6.23 us
  transfers between devices with their start and end apart: 21, of which 14 were waited for; matrix products, arithmetic and copies ran while one was open for 3% of the time, Pallas kernels for 10%

profile of v7, /device:TPU:5, one launch (start us, length us, event | category | flops | bytes accessed | tf_op | source)
XLA Modules:
  0.0 274.1 jit_solution(12714961557322801947)
XLA Ops:
  9.8 1.3 add_convert_fusion.refs_2_.refs_4_
  13.0 85.5 %all-gather.2.cloned.1.call-done = bf16[1,36864,128]{2,1,0:T(8,128)(2,1)} async-done(((bf16[1,576,128]{2,1,0:T(8,128)(2,1)}), bf16[1,36864,128]{2,1,0:T(8,128)(2,1)}) %all-gather.2.cloned.1.call-update) | async-done | bytes 9437200 | tf_op jit(solution)/shard_map/all_gather | solution.py:510
  98.5 8.8 %forward_0.1 = (bf16[128,1536]{1,0:T(8,128)(2,1)S(1)}, bf16[36864,128]{1,0:T(8,128)(2,1)S(1)}, bf16[36864,128]{1,0:T(8,128)(2,1)S(1)}) custom-call(s32[288]{0:T(512)S(1)} %reshape_squeeze.5.refs_0_, s32[288]{0:T(512)S(1)} %reshape_squeeze.4.refs_1_, bf16[128,1536]{1,0:T(8,128)(2,1)S(1)} %add_convert_fusion.refs_2_.refs_4_, ...), custom_call_target="tpu_custom_call" | custom-call | flops 2415919104 | bytes 6144 | tf_op jit(solution)/shard_map/forward_0/pallas_call | solution.py:199
  108.0 7.3 %forward_1.1 = (bf16[128,1536]{1,0:T(8,128)(2,1)S(1)}, bf16[128,1536]{1,0:T(8,128)(2,1)S(1)}) custom-call(s32[288]{0:T(512)S(1)} %reshape_squeeze.5.refs_0_, s32[288]{0:T(512)S(1)} %reshape_squeeze.4.refs_1_, s32[1]{0:T(128)} %bitcast.refs_2_, bf16[128,1536]{1,0:T(8,128)(2,1)S(1)} %collective-permute-done.refs_3_, ...), custom_call_target="tpu_custom_call" | custom-call | flops 2415919104 | bytes 6144 | tf_op jit(solution)/shard_map/forward_1/pallas_call | solution.py:199
  116.6 20.3 %collective-permute-done.1.refs_3_ = bf16[128,1536]{1,0:T(8,128)(2,1)S(1)} collective-permute-done((bf16[128,1536]{1,0:T(8,128)(2,1)S(1)}, bf16[128,1536]{1,0:T(8,128)(2,1)S(1)}, u32[]{:S(2)}, u32[]{:S(2)}) %collective-permute-start.1) | collective-permute-done | bytes 393248 | tf_op jit(solution)/shard_map/ppermute | solution.py:536
  136.9 7.3 %forward_2.1 = (bf16[128,1536]{1,0:T(8,128)(2,1)S(1)}, bf16[128,1536]{1,0:T(8,128)(2,1)S(1)}) custom-call(s32[288]{0:T(512)S(1)} %reshape_squeeze.5.refs_0_, s32[288]{0:T(512)S(1)} %reshape_squeeze.4.refs_1_, s32[1]{0:T(128)} %bitcast.refs_2_, bf16[128,1536]{1,0:T(8,128)(2,1)S(1)} %collective-permute-done.1.refs_3_, ...), custom_call_target="tpu_custom_call" | custom-call | flops 2415919104 | bytes 6144 | tf_op jit(solution)/shard_map/forward_2/pallas_call | solution.py:199
  144.2 1.3 collective-permute-start.2
  145.5 7.0 %collective-permute-done.2.refs_3_ = bf16[128,1536]{1,0:T(8,128)(2,1)S(1)} collective-permute-done((bf16[128,1536]{1,0:T(8,128)(2,1)S(1)}, bf16[128,1536]{1,0:T(8,128)(2,1)S(1)}, u32[]{:S(2)}, u32[]{:S(2)}) %collective-permute-start.2) | collective-permute-done | bytes 393248 | tf_op jit(solution)/shard_map/ppermute | solution.py:536
  152.5 7.9 %forward_3.1 = (bf16[128,1536]{1,0:T(8,128)(2,1)S(1)}, bf16[128,1536]{1,0:T(8,128)(2,1)S(1)}, f32[48,128,128]{2,1,0:T(8,128)S(1)}, bf16[48,128,128]{2,1,0:T(8,128)(2,1)S(1)}) custom-call(s32[288]{0:T(512)S(1)} %reshape_squeeze.5.refs_0_, s32[288]{0:T(512)S(1)} %reshape_squeeze.4.refs_1_, s32[1]{0:T(128)} %bitcast.refs_2_, ...), custom_call_target="tpu_custom_call" | custom-call | flops 2415919104 | bytes 6144 | tf_op jit(solution)/shard_map/forward_3/pallas_call | solution.py:199
  160.4 2.7 collective-permute-start.3
  163.1 8.3 %backward_3.1 = bf16[128,1536]{1,0:T(8,128)(2,1)S(1)} custom-call(s32[288]{0:T(512)S(1)} %reshape_squeeze.5.refs_0_, s32[288]{0:T(512)S(1)} %reshape_squeeze.4.refs_1_, bf16[128,1536]{1,0:T(8,128)(2,1)S(1)} %get-tuple-element.43.refs_2_.refs_4_, bf16[128,1536]{1,0:T(8,128)(2,1)S(1)} %get-tuple-element.44.refs_3_.refs_5_, ...), custom_call_target="tpu_custom_call" | custom-call | flops 1000000 | bytes 100000 | tf_op jit(solution)/shard_map/backward_3/pallas_call | solution.py:290
  172.7 8.6 %collective-permute-done.7.refs_3_ = bf16[128,1536]{1,0:T(8,128)(2,1)S(1)} collective-permute-done((bf16[128,1536]{1,0:T(8,128)(2,1)S(1)}, bf16[128,1536]{1,0:T(8,128)(2,1)S(1)}, u32[]{:S(2)}, u32[]{:S(2)}) %collective-permute-start.7) | collective-permute-done | bytes 393248 | tf_op jit(solution)/shard_map/ppermute | solution.py:552
  181.3 8.3 %backward_2.1 = (bf16[128,1536]{1,0:T(8,128)(2,1)S(1)}, bf16[128,1536]{1,0:T(8,128)(2,1)S(1)}) custom-call(s32[288]{0:T(512)S(1)} %reshape_squeeze.5.refs_0_, s32[288]{0:T(512)S(1)} %reshape_squeeze.4.refs_1_, s32[1]{0:T(128)} %bitcast.refs_2_, bf16[128,1536]{1,0:T(8,128)(2,1)S(1)} %collective-permute-done.7.refs_3_, ...), custom_call_target="tpu_custom_call" | custom-call | flops 1000000 | bytes 100000 | tf_op jit(solution)/shard_map/backward_2/pallas_call | solution.py:290
  190.9 4.3 %collective-permute-done.4.before_ref = bf16[48,128,128]{2,1,0:T(8,128)(2,1)S(1)} collective-permute-done((bf16[48,128,128]{2,1,0:T(8,128)(2,1)S(1)}, bf16[48,128,128]{2,1,0:T(8,128)(2,1)S(1)}, u32[]{:S(2)}, u32[]{:S(2)}) %collective-permute-start.4) | collective-permute-done | bytes 1572896 | tf_op jit(solution)/shard_map/ppermute | solution.py:426
  197.2 2.7 collective-permute-start.5
  199.9 9.0 %backward_1.1 = (bf16[128,1536]{1,0:T(8,128)(2,1)}, bf16[128,1536]{1,0:T(8,128)(2,1)S(1)}) custom-call(s32[288]{0:T(512)S(1)} %reshape_squeeze.5.refs_0_, s32[288]{0:T(512)S(1)} %reshape_squeeze.4.refs_1_, s32[1]{0:T(128)} %bitcast.refs_2_, bf16[128,1536]{1,0:T(8,128)(2,1)S(1)} %collective-permute-done.8.refs_3_, ...), custom_call_target="tpu_custom_call" | custom-call | flops 30000001024 | bytes 100000 | tf_op jit(solution)/shard_map/backward_1/pallas_call | solution.py:290
  209.6 3.8 %collective-permute-done.6.high_ref = bf16[24,128,128]{2,1,0:T(8,128)(2,1)S(1)} collective-permute-done((bf16[24,128,128]{2,1,0:T(8,128)(2,1)}, bf16[24,128,128]{2,1,0:T(8,128)(2,1)S(1)}, u32[]{:S(2)}, u32[]{:S(2)}) %collective-permute-start.6) | collective-permute-done | bytes 786464 | tf_op jit(solution)/shard_map/ppermute | solution.py:428
  213.5 1.4 copy-done.1
  214.9 1.4 copy-done.3
  216.3 2.4 join_pieces.1.refs_2_
  219.0 2.3 collective-permute-start.12
  221.3 1.8 collective-permute-start.11
  224.0 1.9 collective-permute-done.11
  226.6 4.9 %weight_gradient.1 = (f32[4616,128]{1,0:T(8,128)S(1)}, f32[4616,128]{1,0:T(8,128)S(1)}) custom-call(s32[11]{0:T(128)S(1)} %stack.15.refs_0_, s32[288]{0:T(512)S(1)} %reshape_squeeze.4.refs_1_, bf16[48,128,512]{2,1,0:T(8,128)(2,1)S(1)} %join_pieces.1.refs_2_, bf16[512,384]{1,0:T(8,128)(2,1)S(1)} %pad_maximum_fusion.2.refs_3_), custom_call_target="tpu_custom_call" | custom-call | flops 1207959552 | bytes 6291456 | tf_op jit(solution)/shard_map/weight_gradient/pallas_call | solution.py:381
  231.5 6.2 %collective-permute-start.13 = (f32[4616,128]{1,0:T(8,128)S(1)}, f32[4616,128]{1,0:T(8,128)S(1)}, u32[]{:S(2)}, u32[]{:S(2)}) collective-permute-start(f32[4616,128]{1,0:T(8,128)S(1)} %get-tuple-element.58), channel_id=1, source_target_pairs={{0,1},{1,0},{2,3},{3,2},{4,5},{5,4},{6,7},{7,6},{8,9},{9,8},{10,11... | collective-permute-start | bytes 7090184 | tf_op jit(solution)/shard_map/ppermute | solution.py:455
  237.7 4.2 %collective-permute-done.13 = f32[4616,128]{1,0:T(8,128)S(1)} collective-permute-done((f32[4616,128]{1,0:T(8,128)S(1)}, f32[4616,128]{1,0:T(8,128)S(1)}, u32[]{:S(2)}, u32[]{:S(2)}) %collective-permute-start.13) | collective-permute-done | bytes 2363424 | tf_op jit(solution)/shard_map/ppermute | solution.py:455
  243.5 1.7 collective-permute-start.15
  245.4 3.6 %collective-permute-start.18 = (f16[304,128]{1,0:T(8,128)(2,1)S(1)}, f16[304,128]{1,0:T(8,128)(2,1)S(1)}, u32[]{:S(2)}, u32[]{:S(2)}) collective-permute-start(f16[304,128]{1,0:T(8,128)(2,1)S(1)} %get-tuple-element.90), channel_id=1, source_target_pairs={{0,12},{1,13},{2,14},{3,15},{4,0},{5,1},{6,2},{7,3},{8,4},{9,5},{1... | collective-permute-start | bytes 233480 | tf_op jit(solution)/shard_map/ppermute | solution.py:464
  249.0 6.0 %collective-permute-done.16 = f16[304,128]{1,0:T(8,128)(2,1)S(1)} collective-permute-done((f16[304,128]{1,0:T(8,128)(2,1)S(1)}, f16[304,128]{1,0:T(8,128)(2,1)S(1)}, u32[]{:S(2)}, u32[]{:S(2)}) %collective-permute-start.16) | collective-permute-done | bytes 77856 | tf_op jit(solution)/shard_map/ppermute | solution.py:464
  255.5 2.8 %collective-permute-start.19 = (f16[592,128]{1,0:T(8,128)(2,1)S(1)}, f16[592,128]{1,0:T(8,128)(2,1)S(1)}, u32[]{:S(2)}, u32[]{:S(2)}) collective-permute-start(f16[592,128]{1,0:T(8,128)(2,1)S(1)} %pad_maximum_fusion.4), channel_id=1, source_target_pairs={{0,12},{1,13},{2,14},{3,15},{4,0},{5,1},{6,2},{7,3},{8,4},{9,5},{1... | collective-permute-start | bytes 454664 | tf_op jit(solution)/shard_map/ppermute | solution.py:464
  258.6 5.8 %collective-permute-done.19 = f16[592,128]{1,0:T(8,128)(2,1)S(1)} collective-permute-done((f16[592,128]{1,0:T(8,128)(2,1)S(1)}, f16[592,128]{1,0:T(8,128)(2,1)S(1)}, u32[]{:S(2)}, u32[]{:S(2)}) %collective-permute-start.19) | collective-permute-done | bytes 151584 | tf_op jit(solution)/shard_map/ppermute | solution.py:464
  264.4 2.0 collective-permute-done.17
  (75 shorter events, 17.6 us)
Async XLA Ops:
  6.5 92.0 %all-gather.2.cloned.1.call-start = ((), (), s32[]{:S(2)}) async-start(), calls=%async_computation | async-start | bytes 9584640 | tf_op jit(solution)/shard_map/all_gather | solution.py:510
  107.3 0.7 collective-permute-start
  115.3 21.6 %collective-permute-start.1 = (bf16[128,1536]{1,0:T(8,128)(2,1)S(1)}, bf16[128,1536]{1,0:T(8,128)(2,1)S(1)}, u32[]{:S(2)}, u32[]{:S(2)}) collective-permute-start(bf16[128,1536]{1,0:T(8,128)(2,1)S(1)} %get-tuple-element.38), channel_id=1, source_target_pairs={{64,128},{65,129},{66,130},{67,131},{68,132},{69,133},{70,134},{71... | collective-permute-start | bytes 1179656 | tf_op jit(solution)/shard_map/ppermute | solution.py:536
  136.9 15.6 %copy-start.4 = (bf16[128,1536]{1,0:T(8,128)(2,1)S(1)}, bf16[128,1536]{1,0:T(8,128)(2,1)}, u32[]{:S(2)}) copy-start(bf16[128,1536]{1,0:T(8,128)(2,1)} %refs_8_.1) | copy-start | bytes 1179652
  144.2 8.3 %collective-permute-start.2 = (bf16[128,1536]{1,0:T(8,128)(2,1)S(1)}, bf16[128,1536]{1,0:T(8,128)(2,1)S(1)}, u32[]{:S(2)}, u32[]{:S(2)}) collective-permute-start(bf16[128,1536]{1,0:T(8,128)(2,1)S(1)} %get-tuple-element.40), channel_id=1, source_target_pairs={{128,192},{129,193},{130,194},{131,195},{132,196},{133,197},{134,1... | collective-permute-start | bytes 1179656 | tf_op jit(solution)/shard_map/ppermute | solution.py:536
  160.3 11.0 %copy-start.2 = (bf16[48,128,128]{2,1,0:T(8,128)(2,1)}, bf16[48,128,128]{2,1,0:T(8,128)(2,1)S(1)}, u32[]{:S(2)}) copy-start(bf16[48,128,128]{2,1,0:T(8,128)(2,1)S(1)} %get-tuple-element.42.own_ref) | copy-start | bytes 4718596
  160.4 34.9 %collective-permute-start.4 = (bf16[48,128,128]{2,1,0:T(8,128)(2,1)S(1)}, bf16[48,128,128]{2,1,0:T(8,128)(2,1)S(1)}, u32[]{:S(2)}, u32[]{:S(2)}) collective-permute-start(bf16[48,128,128]{2,1,0:T(8,128)(2,1)S(1)} %get-tuple-element.42.own_ref), channel_id=1, source_target_pairs={{0,16},{1,17},{2,18},{3,19},{4,20},{5,21},{6,22},{7,23},{8,24},{9,... | collective-permute-start | bytes 4718600 | tf_op jit(solution)/shard_map/ppermute | solution.py:426
  160.4 35.7 %collective-permute-start.3 = (bf16[48,128,128]{2,1,0:T(8,128)(2,1)S(1)}, bf16[48,128,128]{2,1,0:T(8,128)(2,1)S(1)}, u32[]{:S(2)}, u32[]{:S(2)}) collective-permute-start(bf16[48,128,128]{2,1,0:T(8,128)(2,1)S(1)} %get-tuple-element.42.own_ref), channel_id=1, source_target_pairs={{0,48},{1,49},{2,50},{3,51},{4,52},{5,53},{6,54},{7,55},{8,56},{9,... | collective-permute-start | bytes 4718600 | tf_op jit(solution)/shard_map/ppermute | solution.py:425
  171.4 9.9 %collective-permute-start.7 = (bf16[128,1536]{1,0:T(8,128)(2,1)S(1)}, bf16[128,1536]{1,0:T(8,128)(2,1)S(1)}, u32[]{:S(2)}, u32[]{:S(2)}) collective-permute-start(bf16[128,1536]{1,0:T(8,128)(2,1)S(1)} %backward_3.1), channel_id=1, source_target_pairs={{192,128},{193,129},{194,130},{195,131},{196,132},{197,133},{198,1... | collective-permute-start | bytes 1179656 | tf_op jit(solution)/shard_map/ppermute | solution.py:552
  189.6 10.3 %collective-permute-start.8 = (bf16[128,1536]{1,0:T(8,128)(2,1)S(1)}, bf16[128,1536]{1,0:T(8,128)(2,1)S(1)}, u32[]{:S(2)}, u32[]{:S(2)}) collective-permute-start(bf16[128,1536]{1,0:T(8,128)(2,1)S(1)} %get-tuple-element.46), channel_id=1, source_target_pairs={{128,64},{129,65},{130,66},{131,67},{132,68},{133,69},{134,70},{13... | collective-permute-start | bytes 1179656 | tf_op jit(solution)/shard_map/ppermute | solution.py:552
  196.2 17.2 %collective-permute-start.6 = (bf16[24,128,128]{2,1,0:T(8,128)(2,1)}, bf16[24,128,128]{2,1,0:T(8,128)(2,1)S(1)}, u32[]{:S(2)}, u32[]{:S(2)}) collective-permute-start(bf16[24,128,128]{2,1,0:T(8,128)(2,1)} %slice.141), channel_id=1, source_target_pairs={{0,16},{1,17},{2,18},{3,19},{4,20},{5,21},{6,22},{7,23},{8,24},{9,... | collective-permute-start | bytes 2359304 | tf_op jit(solution)/shard_map/ppermute | solution.py:428
  196.2 12.7 %copy-start = (bf16[48,128,128]{2,1,0:T(8,128)(2,1)}, bf16[48,128,128]{2,1,0:T(8,128)(2,1)S(1)}, u32[]{:S(2)}) copy-start(bf16[48,128,128]{2,1,0:T(8,128)(2,1)S(1)} %collective-permute-done.3.after_ref) | copy-start | bytes 4718596
  197.2 16.3 %collective-permute-start.5 = (bf16[24,128,128]{2,1,0:T(8,128)(2,1)}, bf16[24,128,128]{2,1,0:T(8,128)(2,1)}, u32[]{:S(2)}, u32[]{:S(2)}) collective-permute-start(bf16[24,128,128]{2,1,0:T(8,128)(2,1)} %slice.140), channel_id=1, source_target_pairs={{0,48},{1,49},{2,50},{3,51},{4,52},{5,53},{6,54},{7,55},{8,56},{9,... | collective-permute-start | bytes 2359304 | tf_op jit(solution)/shard_map/ppermute | solution.py:427
  208.9 9.8 %collective-permute-start.9 = (bf16[128,1536]{1,0:T(8,128)(2,1)}, bf16[128,1536]{1,0:T(8,128)(2,1)S(1)}, u32[]{:S(2)}, u32[]{:S(2)}) collective-permute-start(bf16[128,1536]{1,0:T(8,128)(2,1)} %get-tuple-element.48), channel_id=1, source_target_pairs={{64,0},{65,1},{66,2},{67,3},{68,4},{69,5},{70,6},{71,7},{72,8},{73... | collective-permute-start | bytes 1179656 | tf_op jit(solution)/shard_map/ppermute | solution.py:552
  213.5 1.4 copy-start.1
  214.9 1.4 copy-start.3
  219.0 5.1 %collective-permute-start.12 = (bf16[128,384]{1,0:T(8,128)(2,1)S(1)}, bf16[128,384]{1,0:T(8,128)(2,1)S(1)}, u32[]{:S(2)}, u32[]{:S(2)}) collective-permute-start(bf16[128,384]{1,0:T(8,128)(2,1)S(1)} %get-tuple-element.78), channel_id=1, source_target_pairs={{0,32},{1,33},{2,34},{3,35},{4,36},{5,37},{6,38},{7,39},{8,40},{9,... | collective-permute-start | bytes 294920 | tf_op jit(solution)/shard_map/ppermute | solution.py:449
  221.3 4.7 %collective-permute-start.11 = (bf16[128,384]{1,0:T(8,128)(2,1)S(1)}, bf16[128,384]{1,0:T(8,128)(2,1)S(1)}, u32[]{:S(2)}, u32[]{:S(2)}) collective-permute-start(bf16[128,384]{1,0:T(8,128)(2,1)S(1)} %get-tuple-element.79), channel_id=1, source_target_pairs={{0,16},{1,17},{2,18},{3,19},{4,20},{5,21},{6,22},{7,23},{8,24},{9,... | collective-permute-start | bytes 294920 | tf_op jit(solution)/shard_map/ppermute | solution.py:449
  223.1 3.5 %collective-permute-start.10 = (bf16[128,384]{1,0:T(8,128)(2,1)S(1)}, bf16[128,384]{1,0:T(8,128)(2,1)S(1)}, u32[]{:S(2)}, u32[]{:S(2)}) collective-permute-start(bf16[128,384]{1,0:T(8,128)(2,1)S(1)} %get-tuple-element.80), channel_id=1, source_target_pairs={{0,48},{1,49},{2,50},{3,51},{4,52},{5,53},{6,54},{7,55},{8,56},{9,... | collective-permute-start | bytes 294920 | tf_op jit(solution)/shard_map/ppermute | solution.py:449
  231.5 10.4 %collective-permute-start.13 = (f32[4616,128]{1,0:T(8,128)S(1)}, f32[4616,128]{1,0:T(8,128)S(1)}, u32[]{:S(2)}, u32[]{:S(2)}) collective-permute-start(f32[4616,128]{1,0:T(8,128)S(1)} %get-tuple-element.58), channel_id=1, source_target_pairs={{0,1},{1,0},{2,3},{3,2},{4,5},{5,4},{6,7},{7,6},{8,9},{9,8},{10,11... | collective-permute-start | bytes 7090184 | tf_op jit(solution)/shard_map/ppermute | solution.py:455
  242.5 12.6 %collective-permute-start.14 = (f16[1168,128]{1,0:T(8,128)(2,1)S(1)}, f16[1168,128]{1,0:T(8,128)(2,1)S(1)}, u32[]{:S(2)}, u32[]{:S(2)}) collective-permute-start(f16[1168,128]{1,0:T(8,128)(2,1)S(1)} %get-tuple-element.87), channel_id=1, source_target_pairs={{0,2},{1,3},{2,4},{3,5},{4,6},{5,7},{6,8},{7,9},{8,10},{9,11},{10,... | collective-permute-start | bytes 897032 | tf_op jit(solution)/shard_map/ppermute | solution.py:464
  243.5 11.6 %collective-permute-start.15 = (f16[1168,128]{1,0:T(8,128)(2,1)S(1)}, f16[1168,128]{1,0:T(8,128)(2,1)S(1)}, u32[]{:S(2)}, u32[]{:S(2)}) collective-permute-start(f16[1168,128]{1,0:T(8,128)(2,1)S(1)} %get-tuple-element.88), channel_id=1, source_target_pairs={{0,14},{1,15},{2,0},{3,1},{4,2},{5,3},{6,4},{7,5},{8,6},{9,7},{10,... | collective-permute-start | bytes 897032 | tf_op jit(solution)/shard_map/ppermute | solution.py:464
  245.3 9.7 %collective-permute-start.16 = (f16[304,128]{1,0:T(8,128)(2,1)S(1)}, f16[304,128]{1,0:T(8,128)(2,1)S(1)}, u32[]{:S(2)}, u32[]{:S(2)}) collective-permute-start(f16[304,128]{1,0:T(8,128)(2,1)S(1)} %get-tuple-element.89), channel_id=1, source_target_pairs={{0,4},{1,5},{2,6},{3,7},{4,8},{5,9},{6,10},{7,11},{8,12},{9,13},{1... | collective-permute-start | bytes 233480 | tf_op jit(solution)/shard_map/ppermute | solution.py:464
  245.4 9.6 %collective-permute-start.18 = (f16[304,128]{1,0:T(8,128)(2,1)S(1)}, f16[304,128]{1,0:T(8,128)(2,1)S(1)}, u32[]{:S(2)}, u32[]{:S(2)}) collective-permute-start(f16[304,128]{1,0:T(8,128)(2,1)S(1)} %get-tuple-element.90), channel_id=1, source_target_pairs={{0,12},{1,13},{2,14},{3,15},{4,0},{5,1},{6,2},{7,3},{8,4},{9,5},{1... | collective-permute-start | bytes 233480 | tf_op jit(solution)/shard_map/ppermute | solution.py:464
  255.5 8.9 %collective-permute-start.19 = (f16[592,128]{1,0:T(8,128)(2,1)S(1)}, f16[592,128]{1,0:T(8,128)(2,1)S(1)}, u32[]{:S(2)}, u32[]{:S(2)}) collective-permute-start(f16[592,128]{1,0:T(8,128)(2,1)S(1)} %pad_maximum_fusion.4), channel_id=1, source_target_pairs={{0,12},{1,13},{2,14},{3,15},{4,0},{5,1},{6,2},{7,3},{8,4},{9,5},{1... | collective-permute-start | bytes 454664 | tf_op jit(solution)/shard_map/ppermute | solution.py:464
  258.5 8.0 %collective-permute-start.17 = (f16[592,128]{1,0:T(8,128)(2,1)S(1)}, f16[592,128]{1,0:T(8,128)(2,1)S(1)}, u32[]{:S(2)}, u32[]{:S(2)}) collective-permute-start(f16[592,128]{1,0:T(8,128)(2,1)S(1)} %pad_maximum_fusion.3), channel_id=1, source_target_pairs={{0,4},{1,5},{2,6},{3,7},{4,8},{5,9},{6,10},{7,11},{8,12},{9,13},{1... | collective-permute-start | bytes 454664 | tf_op jit(solution)/shard_map/ppermute | solution.py:464
Sparse Core Ops, SparseCore 0:
  10.1 88.3 all-gather.1

commit v8 on v7

--- a/solution.py
+++ b/solution.py
@@ -20,7 +20,7 @@
 UP_GROUP = 6
 UP_UNROLL = 16
 DOWN_UNROLL = 3
-FORWARD_UNROLL = 12
+FORWARD_UNROLL = 8
 FORWARD_DOWN = 3
 LIMIT = 12 << 20
 PARTS = 4

time: 278 us -> 279 us (level)
  no operation moved by 1% of the time
where the time goes in v8:
time: 279 us; the launch traced here: 275 us
  waiting for transfers between devices  151 us (54%)
  Pallas kernels  65.1 us (23%)
  starting transfers between devices  32.6 us (12%)
  between operations  13.9 us (5%)
  local copies, waits for them, and re-layouts  7.06 us (3%)
  other arithmetic  5.72 us (2%)
    all_gather x1, waiting for transfers between devices, per_device(): up_flat = lax.all_gather(up_weight, 'dp', axis=1, tiled=True)[0]  85.5 us
    pallas_call x4, Pallas kernels, section_forward(): pl.pallas_call(body, out_shape=out_shape, in_specs=in_specs, out_specs=[V...  32.2 us
    ppermute x3, waiting for transfers between devices, per_device(): arrived = lax.ppermute(result, 'section', [(turn - 1, turn)])  27.3 us
    pallas_call x3, Pallas kernels, section_backward(): pl.pallas_call(body, out_shape=out_shape, in_specs=in_specs, out_specs=[V...  25.6 us
    ppermute x6, waiting for transfers between devices, send(): got = lax.ppermute(coded, 'dp', route).astype(F32)  14.1 us
    ppermute x6, starting transfers between devices, send(): got = lax.ppermute(coded, 'dp', route).astype(F32)  9.26 us
    ppermute x3, waiting for transfers between devices, per_device(): arrived = lax.ppermute(sent, 'section', [(turn, turn - 1)])  8.4 us
    ppermute x1, starting transfers between devices, reduce_weight_gradient(): total = keep + lax.ppermute(give, 'dp', swap)  6.23 us
  transfers between devices with their start and end apart: 21, of which 14 were waited for; matrix products, arithmetic and copies ran while one was open for 3% of the time, Pallas kernels for 10%

profile of v8, /device:TPU:5, one launch (start us, length us, event | category | flops | bytes accessed | tf_op | source)
XLA Modules:
  0.0 275.3 jit_solution(14048771677420525635)
XLA Ops:
  9.8 1.3 add_convert_fusion.refs_2_.refs_4_
  13.0 85.5 %all-gather.2.cloned.1.call-done = bf16[1,36864,128]{2,1,0:T(8,128)(2,1)} async-done(((bf16[1,576,128]{2,1,0:T(8,128)(2,1)}), bf16[1,36864,128]{2,1,0:T(8,128)(2,1)}) %all-gather.2.cloned.1.call-update) | async-done | bytes 9437200 | tf_op jit(solution)/shard_map/all_gather | solution.py:510
  98.5 8.8 %forward_0.1 = (bf16[128,1536]{1,0:T(8,128)(2,1)S(1)}, bf16[36864,128]{1,0:T(8,128)(2,1)S(1)}, bf16[36864,128]{1,0:T(8,128)(2,1)S(1)}) custom-call(s32[288]{0:T(512)S(1)} %reshape_squeeze.5.refs_0_, s32[288]{0:T(512)S(1)} %reshape_squeeze.4.refs_1_, bf16[128,1536]{1,0:T(8,128)(2,1)S(1)} %add_convert_fusion.refs_2_.refs_4_, ...), custom_call_target="tpu_custom_call" | custom-call | flops 2415919104 | bytes 6144 | tf_op jit(solution)/shard_map/forward_0/pallas_call | solution.py:199
  108.0 7.6 %forward_1.1 = (bf16[128,1536]{1,0:T(8,128)(2,1)S(1)}, bf16[128,1536]{1,0:T(8,128)(2,1)S(1)}) custom-call(s32[288]{0:T(512)S(1)} %reshape_squeeze.5.refs_0_, s32[288]{0:T(512)S(1)} %reshape_squeeze.4.refs_1_, s32[1]{0:T(128)} %bitcast.refs_2_, bf16[128,1536]{1,0:T(8,128)(2,1)S(1)} %collective-permute-done.refs_3_, ...), custom_call_target="tpu_custom_call" | custom-call | flops 2415919104 | bytes 6144 | tf_op jit(solution)/shard_map/forward_1/pallas_call | solution.py:199
  116.9 20.3 %collective-permute-done.1.refs_3_ = bf16[128,1536]{1,0:T(8,128)(2,1)S(1)} collective-permute-done((bf16[128,1536]{1,0:T(8,128)(2,1)S(1)}, bf16[128,1536]{1,0:T(8,128)(2,1)S(1)}, u32[]{:S(2)}, u32[]{:S(2)}) %collective-permute-start.1) | collective-permute-done | bytes 393248 | tf_op jit(solution)/shard_map/ppermute | solution.py:536
  137.2 7.6 %forward_2.1 = (bf16[128,1536]{1,0:T(8,128)(2,1)S(1)}, bf16[128,1536]{1,0:T(8,128)(2,1)S(1)}) custom-call(s32[288]{0:T(512)S(1)} %reshape_squeeze.5.refs_0_, s32[288]{0:T(512)S(1)} %reshape_squeeze.4.refs_1_, s32[1]{0:T(128)} %bitcast.refs_2_, bf16[128,1536]{1,0:T(8,128)(2,1)S(1)} %collective-permute-done.1.refs_3_, ...), custom_call_target="tpu_custom_call" | custom-call | flops 2415919104 | bytes 6144 | tf_op jit(solution)/shard_map/forward_2/pallas_call | solution.py:199
  146.1 7.0 %collective-permute-done.2.refs_3_ = bf16[128,1536]{1,0:T(8,128)(2,1)S(1)} collective-permute-done((bf16[128,1536]{1,0:T(8,128)(2,1)S(1)}, bf16[128,1536]{1,0:T(8,128)(2,1)S(1)}, u32[]{:S(2)}, u32[]{:S(2)}) %collective-permute-start.2) | collective-permute-done | bytes 393248 | tf_op jit(solution)/shard_map/ppermute | solution.py:536
  153.1 8.3 %forward_3.1 = (bf16[128,1536]{1,0:T(8,128)(2,1)S(1)}, bf16[128,1536]{1,0:T(8,128)(2,1)S(1)}, f32[48,128,128]{2,1,0:T(8,128)S(1)}, bf16[48,128,128]{2,1,0:T(8,128)(2,1)S(1)}) custom-call(s32[288]{0:T(512)S(1)} %reshape_squeeze.5.refs_0_, s32[288]{0:T(512)S(1)} %reshape_squeeze.4.refs_1_, s32[1]{0:T(128)} %bitcast.refs_2_, ...), custom_call_target="tpu_custom_call" | custom-call | flops 2415919104 | bytes 6144 | tf_op jit(solution)/shard_map/forward_3/pallas_call | solution.py:199
  161.5 2.7 collective-permute-start.3
  164.1 8.3 %backward_3.1 = bf16[128,1536]{1,0:T(8,128)(2,1)S(1)} custom-call(s32[288]{0:T(512)S(1)} %reshape_squeeze.5.refs_0_, s32[288]{0:T(512)S(1)} %reshape_squeeze.4.refs_1_, bf16[128,1536]{1,0:T(8,128)(2,1)S(1)} %get-tuple-element.43.refs_2_.refs_4_, bf16[128,1536]{1,0:T(8,128)(2,1)S(1)} %get-tuple-element.44.refs_3_.refs_5_, ...), custom_call_target="tpu_custom_call" | custom-call | flops 1000000 | bytes 100000 | tf_op jit(solution)/shard_map/backward_3/pallas_call | solution.py:290
  172.4 1.5 collective-permute-start.7
  173.9 8.4 %collective-permute-done.7.refs_3_ = bf16[128,1536]{1,0:T(8,128)(2,1)S(1)} collective-permute-done((bf16[128,1536]{1,0:T(8,128)(2,1)S(1)}, bf16[128,1536]{1,0:T(8,128)(2,1)S(1)}, u32[]{:S(2)}, u32[]{:S(2)}) %collective-permute-start.7) | collective-permute-done | bytes 393248 | tf_op jit(solution)/shard_map/ppermute | solution.py:552
  182.3 8.3 %backward_2.1 = (bf16[128,1536]{1,0:T(8,128)(2,1)S(1)}, bf16[128,1536]{1,0:T(8,128)(2,1)S(1)}) custom-call(s32[288]{0:T(512)S(1)} %reshape_squeeze.5.refs_0_, s32[288]{0:T(512)S(1)} %reshape_squeeze.4.refs_1_, s32[1]{0:T(128)} %bitcast.refs_2_, bf16[128,1536]{1,0:T(8,128)(2,1)S(1)} %collective-permute-done.7.refs_3_, ...), custom_call_target="tpu_custom_call" | custom-call | flops 1000000 | bytes 100000 | tf_op jit(solution)/shard_map/backward_2/pallas_call | solution.py:290
  191.9 4.3 %collective-permute-done.4.before_ref = bf16[48,128,128]{2,1,0:T(8,128)(2,1)S(1)} collective-permute-done((bf16[48,128,128]{2,1,0:T(8,128)(2,1)S(1)}, bf16[48,128,128]{2,1,0:T(8,128)(2,1)S(1)}, u32[]{:S(2)}, u32[]{:S(2)}) %collective-permute-start.4) | collective-permute-done | bytes 1572896 | tf_op jit(solution)/shard_map/ppermute | solution.py:426
  198.2 2.7 collective-permute-start.5
  200.9 9.0 %backward_1.1 = (bf16[128,1536]{1,0:T(8,128)(2,1)}, bf16[128,1536]{1,0:T(8,128)(2,1)S(1)}) custom-call(s32[288]{0:T(512)S(1)} %reshape_squeeze.5.refs_0_, s32[288]{0:T(512)S(1)} %reshape_squeeze.4.refs_1_, s32[1]{0:T(128)} %bitcast.refs_2_, bf16[128,1536]{1,0:T(8,128)(2,1)S(1)} %collective-permute-done.8.refs_3_, ...), custom_call_target="tpu_custom_call" | custom-call | flops 30000001024 | bytes 100000 | tf_op jit(solution)/shard_map/backward_1/pallas_call | solution.py:290
  210.7 3.8 %collective-permute-done.6.high_ref = bf16[24,128,128]{2,1,0:T(8,128)(2,1)S(1)} collective-permute-done((bf16[24,128,128]{2,1,0:T(8,128)(2,1)}, bf16[24,128,128]{2,1,0:T(8,128)(2,1)S(1)}, u32[]{:S(2)}, u32[]{:S(2)}) %collective-permute-start.6) | collective-permute-done | bytes 786464 | tf_op jit(solution)/shard_map/ppermute | solution.py:428
  214.5 1.4 copy-done.1
  215.9 1.4 copy-done.3
  217.4 2.4 join_pieces.1.refs_2_
  220.0 2.3 collective-permute-start.12
  222.3 1.8 collective-permute-start.11
  225.1 1.9 collective-permute-done.11
  227.6 4.9 %weight_gradient.1 = (f32[4616,128]{1,0:T(8,128)S(1)}, f32[4616,128]{1,0:T(8,128)S(1)}) custom-call(s32[11]{0:T(128)S(1)} %stack.15.refs_0_, s32[288]{0:T(512)S(1)} %reshape_squeeze.4.refs_1_, bf16[48,128,512]{2,1,0:T(8,128)(2,1)S(1)} %join_pieces.1.refs_2_, bf16[512,384]{1,0:T(8,128)(2,1)S(1)} %pad_maximum_fusion.2.refs_3_), custom_call_target="tpu_custom_call" | custom-call | flops 1207959552 | bytes 6291456 | tf_op jit(solution)/shard_map/weight_gradient/pallas_call | solution.py:381
  232.5 6.2 %collective-permute-start.13 = (f32[4616,128]{1,0:T(8,128)S(1)}, f32[4616,128]{1,0:T(8,128)S(1)}, u32[]{:S(2)}, u32[]{:S(2)}) collective-permute-start(f32[4616,128]{1,0:T(8,128)S(1)} %get-tuple-element.58), channel_id=1, source_target_pairs={{0,1},{1,0},{2,3},{3,2},{4,5},{5,4},{6,7},{7,6},{8,9},{9,8},{10,11... | collective-permute-start | bytes 7090184 | tf_op jit(solution)/shard_map/ppermute | solution.py:455
  238.8 4.2 %collective-permute-done.13 = f32[4616,128]{1,0:T(8,128)S(1)} collective-permute-done((f32[4616,128]{1,0:T(8,128)S(1)}, f32[4616,128]{1,0:T(8,128)S(1)}, u32[]{:S(2)}, u32[]{:S(2)}) %collective-permute-start.13) | collective-permute-done | bytes 2363424 | tf_op jit(solution)/shard_map/ppermute | solution.py:455
  244.5 1.7 collective-permute-start.15
  246.4 3.6 %collective-permute-start.18 = (f16[304,128]{1,0:T(8,128)(2,1)S(1)}, f16[304,128]{1,0:T(8,128)(2,1)S(1)}, u32[]{:S(2)}, u32[]{:S(2)}) collective-permute-start(f16[304,128]{1,0:T(8,128)(2,1)S(1)} %get-tuple-element.90), channel_id=1, source_target_pairs={{0,12},{1,13},{2,14},{3,15},{4,0},{5,1},{6,2},{7,3},{8,4},{9,5},{1... | collective-permute-start | bytes 233480 | tf_op jit(solution)/shard_map/ppermute | solution.py:464
  250.0 6.1 %collective-permute-done.16 = f16[304,128]{1,0:T(8,128)(2,1)S(1)} collective-permute-done((f16[304,128]{1,0:T(8,128)(2,1)S(1)}, f16[304,128]{1,0:T(8,128)(2,1)S(1)}, u32[]{:S(2)}, u32[]{:S(2)}) %collective-permute-start.16) | collective-permute-done | bytes 77856 | tf_op jit(solution)/shard_map/ppermute | solution.py:464
  256.6 2.8 %collective-permute-start.19 = (f16[592,128]{1,0:T(8,128)(2,1)S(1)}, f16[592,128]{1,0:T(8,128)(2,1)S(1)}, u32[]{:S(2)}, u32[]{:S(2)}) collective-permute-start(f16[592,128]{1,0:T(8,128)(2,1)S(1)} %pad_maximum_fusion.4), channel_id=1, source_target_pairs={{0,12},{1,13},{2,14},{3,15},{4,0},{5,1},{6,2},{7,3},{8,4},{9,5},{1... | collective-permute-start | bytes 454664 | tf_op jit(solution)/shard_map/ppermute | solution.py:464
  259.6 5.8 %collective-permute-done.19 = f16[592,128]{1,0:T(8,128)(2,1)S(1)} collective-permute-done((f16[592,128]{1,0:T(8,128)(2,1)S(1)}, f16[592,128]{1,0:T(8,128)(2,1)S(1)}, u32[]{:S(2)}, u32[]{:S(2)}) %collective-permute-start.19) | collective-permute-done | bytes 151584 | tf_op jit(solution)/shard_map/ppermute | solution.py:464
  265.4 2.2 collective-permute-done.17
  (75 shorter events, 17.6 us)
Async XLA Ops:
  6.5 92.0 %all-gather.2.cloned.1.call-start = ((), (), s32[]{:S(2)}) async-start(), calls=%async_computation | async-start | bytes 9584640 | tf_op jit(solution)/shard_map/all_gather | solution.py:510
  107.3 0.7 collective-permute-start
  115.6 21.6 %collective-permute-start.1 = (bf16[128,1536]{1,0:T(8,128)(2,1)S(1)}, bf16[128,1536]{1,0:T(8,128)(2,1)S(1)}, u32[]{:S(2)}, u32[]{:S(2)}) collective-permute-start(bf16[128,1536]{1,0:T(8,128)(2,1)S(1)} %get-tuple-element.38), channel_id=1, source_target_pairs={{64,128},{65,129},{66,130},{67,131},{68,132},{69,133},{70,134},{71... | collective-permute-start | bytes 1179656 | tf_op jit(solution)/shard_map/ppermute | solution.py:536
  137.2 15.9 %copy-start.4 = (bf16[128,1536]{1,0:T(8,128)(2,1)S(1)}, bf16[128,1536]{1,0:T(8,128)(2,1)}, u32[]{:S(2)}) copy-start(bf16[128,1536]{1,0:T(8,128)(2,1)} %refs_8_.1) | copy-start | bytes 1179652
  144.8 8.3 %collective-permute-start.2 = (bf16[128,1536]{1,0:T(8,128)(2,1)S(1)}, bf16[128,1536]{1,0:T(8,128)(2,1)S(1)}, u32[]{:S(2)}, u32[]{:S(2)}) collective-permute-start(bf16[128,1536]{1,0:T(8,128)(2,1)S(1)} %get-tuple-element.40), channel_id=1, source_target_pairs={{128,192},{129,193},{130,194},{131,195},{132,196},{133,197},{134,1... | collective-permute-start | bytes 1179656 | tf_op jit(solution)/shard_map/ppermute | solution.py:536
  161.4 11.0 %copy-start.2 = (bf16[48,128,128]{2,1,0:T(8,128)(2,1)}, bf16[48,128,128]{2,1,0:T(8,128)(2,1)S(1)}, u32[]{:S(2)}) copy-start(bf16[48,128,128]{2,1,0:T(8,128)(2,1)S(1)} %get-tuple-element.42.own_ref) | copy-start | bytes 4718596
  161.4 34.9 %collective-permute-start.4 = (bf16[48,128,128]{2,1,0:T(8,128)(2,1)S(1)}, bf16[48,128,128]{2,1,0:T(8,128)(2,1)S(1)}, u32[]{:S(2)}, u32[]{:S(2)}) collective-permute-start(bf16[48,128,128]{2,1,0:T(8,128)(2,1)S(1)} %get-tuple-element.42.own_ref), channel_id=1, source_target_pairs={{0,16},{1,17},{2,18},{3,19},{4,20},{5,21},{6,22},{7,23},{8,24},{9,... | collective-permute-start | bytes 4718600 | tf_op jit(solution)/shard_map/ppermute | solution.py:426
  161.5 35.7 %collective-permute-start.3 = (bf16[48,128,128]{2,1,0:T(8,128)(2,1)S(1)}, bf16[48,128,128]{2,1,0:T(8,128)(2,1)S(1)}, u32[]{:S(2)}, u32[]{:S(2)}) collective-permute-start(bf16[48,128,128]{2,1,0:T(8,128)(2,1)S(1)} %get-tuple-element.42.own_ref), channel_id=1, source_target_pairs={{0,48},{1,49},{2,50},{3,51},{4,52},{5,53},{6,54},{7,55},{8,56},{9,... | collective-permute-start | bytes 4718600 | tf_op jit(solution)/shard_map/ppermute | solution.py:425
  172.4 9.9 %collective-permute-start.7 = (bf16[128,1536]{1,0:T(8,128)(2,1)S(1)}, bf16[128,1536]{1,0:T(8,128)(2,1)S(1)}, u32[]{:S(2)}, u32[]{:S(2)}) collective-permute-start(bf16[128,1536]{1,0:T(8,128)(2,1)S(1)} %backward_3.1), channel_id=1, source_target_pairs={{192,128},{193,129},{194,130},{195,131},{196,132},{197,133},{198,1... | collective-permute-start | bytes 1179656 | tf_op jit(solution)/shard_map/ppermute | solution.py:552
  190.6 10.3 %collective-permute-start.8 = (bf16[128,1536]{1,0:T(8,128)(2,1)S(1)}, bf16[128,1536]{1,0:T(8,128)(2,1)S(1)}, u32[]{:S(2)}, u32[]{:S(2)}) collective-permute-start(bf16[128,1536]{1,0:T(8,128)(2,1)S(1)} %get-tuple-element.46), channel_id=1, source_target_pairs={{128,64},{129,65},{130,66},{131,67},{132,68},{133,69},{134,70},{13... | collective-permute-start | bytes 1179656 | tf_op jit(solution)/shard_map/ppermute | solution.py:552
  197.2 17.2 %collective-permute-start.6 = (bf16[24,128,128]{2,1,0:T(8,128)(2,1)}, bf16[24,128,128]{2,1,0:T(8,128)(2,1)S(1)}, u32[]{:S(2)}, u32[]{:S(2)}) collective-permute-start(bf16[24,128,128]{2,1,0:T(8,128)(2,1)} %slice.141), channel_id=1, source_target_pairs={{0,16},{1,17},{2,18},{3,19},{4,20},{5,21},{6,22},{7,23},{8,24},{9,... | collective-permute-start | bytes 2359304 | tf_op jit(solution)/shard_map/ppermute | solution.py:428
  197.2 12.7 %copy-start = (bf16[48,128,128]{2,1,0:T(8,128)(2,1)}, bf16[48,128,128]{2,1,0:T(8,128)(2,1)S(1)}, u32[]{:S(2)}) copy-start(bf16[48,128,128]{2,1,0:T(8,128)(2,1)S(1)} %collective-permute-done.3.after_ref) | copy-start | bytes 4718596
  198.2 16.3 %collective-permute-start.5 = (bf16[24,128,128]{2,1,0:T(8,128)(2,1)}, bf16[24,128,128]{2,1,0:T(8,128)(2,1)}, u32[]{:S(2)}, u32[]{:S(2)}) collective-permute-start(bf16[24,128,128]{2,1,0:T(8,128)(2,1)} %slice.140), channel_id=1, source_target_pairs={{0,48},{1,49},{2,50},{3,51},{4,52},{5,53},{6,54},{7,55},{8,56},{9,... | collective-permute-start | bytes 2359304 | tf_op jit(solution)/shard_map/ppermute | solution.py:427
  210.0 9.8 %collective-permute-start.9 = (bf16[128,1536]{1,0:T(8,128)(2,1)}, bf16[128,1536]{1,0:T(8,128)(2,1)S(1)}, u32[]{:S(2)}, u32[]{:S(2)}) collective-permute-start(bf16[128,1536]{1,0:T(8,128)(2,1)} %get-tuple-element.48), channel_id=1, source_target_pairs={{64,0},{65,1},{66,2},{67,3},{68,4},{69,5},{70,6},{71,7},{72,8},{73... | collective-permute-start | bytes 1179656 | tf_op jit(solution)/shard_map/ppermute | solution.py:552
  214.5 1.4 copy-start.1
  215.9 1.4 copy-start.3
  220.0 5.1 %collective-permute-start.12 = (bf16[128,384]{1,0:T(8,128)(2,1)S(1)}, bf16[128,384]{1,0:T(8,128)(2,1)S(1)}, u32[]{:S(2)}, u32[]{:S(2)}) collective-permute-start(bf16[128,384]{1,0:T(8,128)(2,1)S(1)} %get-tuple-element.78), channel_id=1, source_target_pairs={{0,32},{1,33},{2,34},{3,35},{4,36},{5,37},{6,38},{7,39},{8,40},{9,... | collective-permute-start | bytes 294920 | tf_op jit(solution)/shard_map/ppermute | solution.py:449
  222.3 4.7 %collective-permute-start.11 = (bf16[128,384]{1,0:T(8,128)(2,1)S(1)}, bf16[128,384]{1,0:T(8,128)(2,1)S(1)}, u32[]{:S(2)}, u32[]{:S(2)}) collective-permute-start(bf16[128,384]{1,0:T(8,128)(2,1)S(1)} %get-tuple-element.79), channel_id=1, source_target_pairs={{0,16},{1,17},{2,18},{3,19},{4,20},{5,21},{6,22},{7,23},{8,24},{9,... | collective-permute-start | bytes 294920 | tf_op jit(solution)/shard_map/ppermute | solution.py:449
  224.1 3.5 %collective-permute-start.10 = (bf16[128,384]{1,0:T(8,128)(2,1)S(1)}, bf16[128,384]{1,0:T(8,128)(2,1)S(1)}, u32[]{:S(2)}, u32[]{:S(2)}) collective-permute-start(bf16[128,384]{1,0:T(8,128)(2,1)S(1)} %get-tuple-element.80), channel_id=1, source_target_pairs={{0,48},{1,49},{2,50},{3,51},{4,52},{5,53},{6,54},{7,55},{8,56},{9,... | collective-permute-start | bytes 294920 | tf_op jit(solution)/shard_map/ppermute | solution.py:449
  232.5 10.4 %collective-permute-start.13 = (f32[4616,128]{1,0:T(8,128)S(1)}, f32[4616,128]{1,0:T(8,128)S(1)}, u32[]{:S(2)}, u32[]{:S(2)}) collective-permute-start(f32[4616,128]{1,0:T(8,128)S(1)} %get-tuple-element.58), channel_id=1, source_target_pairs={{0,1},{1,0},{2,3},{3,2},{4,5},{5,4},{6,7},{7,6},{8,9},{9,8},{10,11... | collective-permute-start | bytes 7090184 | tf_op jit(solution)/shard_map/ppermute | solution.py:455
  243.5 12.6 %collective-permute-start.14 = (f16[1168,128]{1,0:T(8,128)(2,1)S(1)}, f16[1168,128]{1,0:T(8,128)(2,1)S(1)}, u32[]{:S(2)}, u32[]{:S(2)}) collective-permute-start(f16[1168,128]{1,0:T(8,128)(2,1)S(1)} %get-tuple-element.87), channel_id=1, source_target_pairs={{0,2},{1,3},{2,4},{3,5},{4,6},{5,7},{6,8},{7,9},{8,10},{9,11},{10,... | collective-permute-start | bytes 897032 | tf_op jit(solution)/shard_map/ppermute | solution.py:464
  244.5 11.6 %collective-permute-start.15 = (f16[1168,128]{1,0:T(8,128)(2,1)S(1)}, f16[1168,128]{1,0:T(8,128)(2,1)S(1)}, u32[]{:S(2)}, u32[]{:S(2)}) collective-permute-start(f16[1168,128]{1,0:T(8,128)(2,1)S(1)} %get-tuple-element.88), channel_id=1, source_target_pairs={{0,14},{1,15},{2,0},{3,1},{4,2},{5,3},{6,4},{7,5},{8,6},{9,7},{10,... | collective-permute-start | bytes 897032 | tf_op jit(solution)/shard_map/ppermute | solution.py:464
  246.3 9.7 %collective-permute-start.16 = (f16[304,128]{1,0:T(8,128)(2,1)S(1)}, f16[304,128]{1,0:T(8,128)(2,1)S(1)}, u32[]{:S(2)}, u32[]{:S(2)}) collective-permute-start(f16[304,128]{1,0:T(8,128)(2,1)S(1)} %get-tuple-element.89), channel_id=1, source_target_pairs={{0,4},{1,5},{2,6},{3,7},{4,8},{5,9},{6,10},{7,11},{8,12},{9,13},{1... | collective-permute-start | bytes 233480 | tf_op jit(solution)/shard_map/ppermute | solution.py:464
  246.4 9.6 %collective-permute-start.18 = (f16[304,128]{1,0:T(8,128)(2,1)S(1)}, f16[304,128]{1,0:T(8,128)(2,1)S(1)}, u32[]{:S(2)}, u32[]{:S(2)}) collective-permute-start(f16[304,128]{1,0:T(8,128)(2,1)S(1)} %get-tuple-element.90), channel_id=1, source_target_pairs={{0,12},{1,13},{2,14},{3,15},{4,0},{5,1},{6,2},{7,3},{8,4},{9,5},{1... | collective-permute-start | bytes 233480 | tf_op jit(solution)/shard_map/ppermute | solution.py:464
  256.6 8.8 %collective-permute-start.19 = (f16[592,128]{1,0:T(8,128)(2,1)S(1)}, f16[592,128]{1,0:T(8,128)(2,1)S(1)}, u32[]{:S(2)}, u32[]{:S(2)}) collective-permute-start(f16[592,128]{1,0:T(8,128)(2,1)S(1)} %pad_maximum_fusion.4), channel_id=1, source_target_pairs={{0,12},{1,13},{2,14},{3,15},{4,0},{5,1},{6,2},{7,3},{8,4},{9,5},{1... | collective-permute-start | bytes 454664 | tf_op jit(solution)/shard_map/ppermute | solution.py:464
  259.5 8.2 %collective-permute-start.17 = (f16[592,128]{1,0:T(8,128)(2,1)S(1)}, f16[592,128]{1,0:T(8,128)(2,1)S(1)}, u32[]{:S(2)}, u32[]{:S(2)}) collective-permute-start(f16[592,128]{1,0:T(8,128)(2,1)S(1)} %pad_maximum_fusion.3), channel_id=1, source_target_pairs={{0,4},{1,5},{2,6},{3,7},{4,8},{5,9},{6,10},{7,11},{8,12},{9,13},{1... | collective-permute-start | bytes 454664 | tf_op jit(solution)/shard_map/ppermute | solution.py:464
Sparse Core Ops, SparseCore 0:
  10.1 88.3 all-gather.1
